TPU v7x, 32 devices: a whole 2x2x4 slice. The times are simulated.
32 devices in a mesh: seq: 8 (over z, core), head: 4 (over y, x).
Axes of the slice: x: 2, y: 2, z: 4, core: 2. Of those that a mesh axis runs over, the one named last changes fastest.
Arguments:
- mixer_input: bfloat16 [2048, 4096], P('seq', 'head'), may hold values from -600 to 600
- gate_input: bfloat16 [2048, 4096], P('seq', 'head'), may hold values from -5 to 5
- b_proj: bfloat16 [2048, 128], P('seq'), may hold values from -0.5 to 0.5
- c_proj: bfloat16 [2048, 128], P('seq'), may hold values from -0.5 to 0.5
- decay_codes: int32 [64, 2048], P('head', 'seq'), may hold values from 1 to 4096
- decay_rates: float32 [64], P('head'), may hold values from 0 to 1
- skip_gain: float32 [64], P('head'), may hold values from 0.5 to 1.5
- norm_gain: float32 [4096], P('head'), may hold values from 0.5 to 1.5
- queries: bfloat16 [2048, 4096], P('seq', 'head'), may hold values from -5 to 5
- keys: bfloat16 [2048, 4096], P('seq', 'head'), may hold values from -5 to 5
Outputs:
- mamba_out: bfloat16 [2048, 4096], P('seq', 'head')
- attn_out: bfloat16 [2048, 4096], P('seq', 'head')
All inputs are finite; a program needn't handle non-finite values.
Results may differ from a plain program's by a relative error of at most 0.013.
Values may be sent and summed in bfloat16 or wider, within the bound.
No kernel may reach another device: no remote copies, remote signals or barrier semaphores. Data moves between devices by JAX's collectives and lax.ppermute only.
A program may use at most 64 MiB of HBM per device.

v0:
```python
import functools
import math

import jax
import jax.numpy as jnp
from jax import lax
from jax.sharding import PartitionSpec as P

HD = 128
CHANNELS_PER_HD = 64
BLOCK = 256


HIGH = lax.Precision.HIGHEST
NEG = -1e30


def carried_in(array, axis, combine, identity):
    devices, mine = (lax.axis_size(axis), lax.axis_index(axis))
    everything = jax.tree.map(
        lambda part, kind: lax.all_gather(part.astype(kind), axis),
        array,
        (jnp.bfloat16, jnp.bfloat16),
    )
    start = jax.tree.map(
        lambda part, zero: jnp.broadcast_to(jnp.asarray(zero, part.dtype), part.shape),
        array,
        identity,
    )

    def hop(k, before):
        reached = k < mine
        new = combine(
            before, jax.tree.map(lambda part, own: part[k].astype(own.dtype), everything, array)
        )
        return jax.tree.map(lambda a, b: jnp.where(reached, a, b), new, before)

    return lax.fori_loop(0, devices, hop, start)


def block_step(state_carry, inputs):
    x_block, b_block, c_block, decay_block = inputs
    running = jnp.cumsum(decay_block, axis=1)
    span = decay_block.shape[1]
    causal = (
        jnp.arange(span, dtype=jnp.int32)[:, None] >= jnp.arange(span, dtype=jnp.int32)[None, :]
    )
    log_gaps = jnp.where(causal[None, :, :], running[:, :, None] - running[:, None, :], NEG)
    decays = jnp.exp(log_gaps)
    match_strength = jnp.dot(c_block, b_block.T, preferred_element_type=jnp.float32)
    x_float = x_block.astype(jnp.float32)
    within = jnp.einsum(
        "hts,shp->thp", decays * match_strength[None, :, :], x_float, precision=HIGH
    )
    c_float = c_block.astype(jnp.float32)
    carried = jnp.exp(running).T[:, :, None] * jnp.einsum(
        "tn,hnp->thp", c_float, state_carry, precision=HIGH
    )
    to_end = jnp.exp(running[:, -1:] - running)
    updated_state = jnp.exp(running[:, -1])[:, None, None] * state_carry + jnp.einsum(
        "hs,sn,shp->hnp", to_end, b_block.astype(jnp.float32), x_float, precision=HIGH
    )
    return (updated_state, within + carried)


def local_scan(x_local, b_local, c_local, log_decay):
    tok_rows = x_local.shape[0]
    heads_local = log_decay.shape[0]
    block_count = tok_rows // BLOCK
    x_blocks = x_local.reshape(block_count, BLOCK, heads_local, CHANNELS_PER_HD)
    b_blocks = b_local.reshape(block_count, BLOCK, b_local.shape[1])
    c_blocks = c_local.reshape(block_count, BLOCK, c_local.shape[1])
    decay_blocks = log_decay.reshape(heads_local, block_count, BLOCK).transpose(1, 0, 2)
    initial = jnp.zeros((heads_local, b_local.shape[1], CHANNELS_PER_HD), jnp.float32)
    final_state, y_blocks = lax.scan(
        block_step, initial, (x_blocks, b_blocks, c_blocks, decay_blocks)
    )
    return (final_state, y_blocks.reshape(tok_rows, heads_local, CHANNELS_PER_HD))


def masked_scores(q_rows, q_pos, k_rows, k_pos):
    score_scale = 1.0 / math.sqrt(k_rows.shape[-1])
    scores = (
        jnp.einsum("qhd,khd->hqk", q_rows, k_rows, preferred_element_type=jnp.float32) * score_scale
    )
    visible = k_pos[None, None, :] <= q_pos[None, :, None]
    return (jnp.where(visible, scores, NEG), visible)


def online_update(group_state, q_rows, q_pos, k_rows, v_rows, k_pos):
    row_top, row_total, weighted_sum = group_state
    scores, visible = masked_scores(q_rows, q_pos, k_rows, k_pos)
    new_top = jnp.maximum(row_top, jnp.max(scores, axis=2))
    rescale = jnp.exp(row_top - new_top)
    weights = jnp.where(visible, jnp.exp(scores - new_top[:, :, None]), 0.0)
    row_total = row_total * rescale + jnp.sum(weights, axis=2)
    weighted_sum = weighted_sum * rescale[:, :, None] + jnp.einsum(
        "hqk,khd->hqd", weights.astype(jnp.bfloat16), v_rows, preferred_element_type=jnp.float32
    )
    return (new_top, row_total, weighted_sum)


def when_visible(state_update, group_state, q_pos, key_offset):
    return lax.cond(key_offset > q_pos[-1], lambda held: held, state_update, group_state)


def on_device(
    mixer_input,
    gate_input,
    b_proj,
    c_proj,
    decay_codes,
    decay_rates,
    skip_gain,
    norm_gain,
    queries,
    keys,
):
    tok_rows = mixer_input.shape[0]
    heads_local = decay_rates.shape[0]
    heads_att = queries.shape[1] // HD
    seq_rank = lax.axis_index("seq")
    own_positions = seq_rank * tok_rows + jnp.arange(tok_rows, dtype=jnp.int32)
    groups = [(queries, own_positions)]
    groups = [(q_rows.reshape(q_rows.shape[0], heads_att, HD), q_pos) for q_rows, q_pos in groups]
    log_decay = -decay_rates[:, None] * decay_codes.astype(jnp.float32)
    local_state, y_local = local_scan(mixer_input, b_proj, c_proj, log_decay)
    total_log = jnp.sum(log_decay, axis=1)

    def combine(earlier, later):
        return (earlier[0] + later[0], jnp.exp(later[0])[:, None, None] * earlier[1] + later[1])

    identity = (jnp.zeros_like(total_log), jnp.zeros_like(local_state))
    _, incoming = carried_in((total_log, local_state), "seq", combine, identity)
    running = jnp.cumsum(log_decay, axis=1)
    carried = jnp.einsum("tn,hnp->thp", c_proj.astype(jnp.float32), incoming, precision=HIGH)
    carried = carried * jnp.exp(running).T[:, :, None]
    x_float = mixer_input.reshape(tok_rows, heads_local, CHANNELS_PER_HD).astype(jnp.float32)
    ssm_out = (y_local + carried + skip_gain[None, :, None] * x_float).reshape(
        tok_rows, heads_local * CHANNELS_PER_HD
    )
    gated = ssm_out * jax.nn.silu(gate_input.astype(jnp.float32))
    squares = lax.psum(jnp.sum(gated * gated, axis=1), "head")
    channels = gated.shape[1] * lax.axis_size("head")
    mamba_out = (
        gated * lax.rsqrt(squares / channels + 1e-05)[:, None] * norm_gain[None, :]
    ).astype(jnp.bfloat16)
    initial = tuple(
        (
            (
                jnp.full((heads_att, q_pos.shape[0]), NEG, jnp.float32),
                jnp.zeros((heads_att, q_pos.shape[0]), jnp.float32),
                jnp.zeros((heads_att, q_pos.shape[0], HD), jnp.float32),
            )
            for _, q_pos in groups
        )
    )
    states = initial
    k_piece = lax.all_gather(keys, "seq", axis=0, tiled=True)
    v_piece = lax.all_gather(mamba_out, "seq", axis=0, tiled=True)
    row_count = k_piece.shape[0]
    block_rows = math.gcd(row_count, 512)

    def one_block(block_id, states):
        key_offset = block_id * block_rows
        k_rows = lax.dynamic_slice_in_dim(k_piece, block_id * block_rows, block_rows, 0).reshape(
            block_rows, heads_att, HD
        )
        v_rows = lax.dynamic_slice_in_dim(v_piece, block_id * block_rows, block_rows, 0).reshape(
            block_rows, heads_att, HD
        )
        k_pos = key_offset + jnp.arange(block_rows, dtype=jnp.int32)
        return tuple(
            (
                when_visible(
                    functools.partial(
                        online_update,
                        q_rows=group[0],
                        q_pos=group[1],
                        k_rows=k_rows,
                        v_rows=v_rows,
                        k_pos=k_pos,
                    ),
                    group_state,
                    group[1],
                    key_offset,
                )
                for group, group_state in zip(groups, states)
            )
        )

    finals = lax.fori_loop(0, row_count // block_rows, one_block, states)
    results = [(group_state[2], group_state[1]) for group_state in finals]
    rows_out = [
        (weighted / totals[:, :, None])
        .transpose(1, 0, 2)
        .reshape(weighted.shape[1], heads_att * HD)
        .astype(jnp.bfloat16)
        for weighted, totals in results
    ]
    attn_out = rows_out[0]
    return (mamba_out, attn_out)


def solution(mesh):
    in_specs = (
        P("seq", "head"),
        P("seq", "head"),
        P("seq", None),
        P("seq", None),
        P("head", "seq"),
        P("head"),
        P("head"),
        P("head"),
        P("seq", "head"),
        P("seq", "head"),
    )
    out_specs = (P("seq", "head"), P("seq", "head"))
    return jax.shard_map(
        on_device, mesh=mesh, in_specs=in_specs, out_specs=out_specs, check_vma=False
    )
```

profile of v0, /device:TPU:25, one launch (start us, length us, event | category | flops | bytes accessed | tf_op | source)
XLA Modules:
  0.0 200.4 jit_solution(12899004294406485471)
XLA Ops:
  7.2 0.7 neg.8
  7.9 0.9 fusion.43
  8.8 0.6 reduce-window.12
  9.9 1.2 copy.56
  11.2 2.2 %fusion.32 = bf16[16,128,64]{1,2,0:T(8,128)(2,1)} fusion(bf16[256,16,64]{0,2,1:T(8,128)(2,1)S(1)} %bitcast.92, f32[256,16]{0,1:T(8,128)S(1)} %get-tuple-element.482, f32[16]{0:T(128)S(1)} %exponential_multiply_fusion, bf16[256,128]{1,0:T(8,128)(2,1)} %param.18), kind=kOutput, calls=%fused_computation.45 | convolution fusion | flops 403439616 | bytes 868416 | tf_op jit(solution)/shard_map/while/body/eval_jaxpr/hs,sn,shp->hnp/dot_general | solution.py:60
  13.5 1.3 dynamic-slice.3
  15.6 13.3 %all-reduce = bf16[128]{0:T(256)(128)(2,1)S(1)} all-reduce(bf16[128]{0:T(256)(128)(2,1)S(1)} %dynamic-update-slice), channel_id=2, replica_groups=mesh['seq'=8,'head'=4] {'seq'}, use_global_device_ids=true, to_apply=%add | all-reduce | flops 128 | bytes 512
  29.1 1.0 fusion.47
  30.1 3.0 %fusion.23 = f32[256,16,64]{0,2,1:T(8,128)S(1)} fusion(bf16[256,16,64]{0,2,1:T(8,128)(2,1)S(1)} %bitcast.93, f32[256,256]{1,0:T(8,128)S(1)} %fusion.47, f32[16,256]{1,0:T(8,128)S(1)} %copy_bitcast_fusion.1, pred[256,256]{1,0:T(8,128)(4,1)S(1)} %iota_compare_fusion), kind=kOutput, calls=%fused_computation.32 | convolution fusion | flops 808452096 | bytes 1916928 | tf_op jit(solution)/shard_map/while/body/eval_jaxpr/hts,shp->thp/dot_general | solution.py:52
  33.1 0.6 fusion.30
  33.7 9.1 %all-gather.10.cloned.1.call-done = bf16[128,128,64]{1,2,0:T(8,128)(2,1)} async-done(((bf16[16,128,64]{1,2,0:T(8,128)(2,1)}), bf16[128,128,64]{1,2,0:T(8,128)(2,1)}) %all-gather.10.cloned.1.call-update) | async-done | bytes 2097168 | tf_op jit(solution)/shard_map/all_gather | solution.py:21
  42.8 13.6 %while.37 = (s32[]{:T(128)}, f32[16,128,64]{2,1,0:T(8,128)S(1)}, s32[]{:T(128)}, bf16[8,16]{1,0:T(8,128)(2,1)S(1)}, bf16[8,16,128,64]{2,3,1,0:T(8,128)(2,1)}, /*index=5*/s32[]{:T(128)}, s32[]{:T(128)}) while((s32[]{:T(128)}, f32[16,128,64]{2,1,0:T(8,128)S(1)}, s32[]{:T(128)}, bf16[8,16]{1,0:T(8,128)(2,1)S(1)}, ...), condition=%wide.region_4.5_spmd.clone, body=%wide.region_3.4_spmd.clone.sunk | while | flops 655380 | bytes 2359569 | solution.py:38
  42.8 1.0 constant_dynamic-slice_fusion.4
  43.8 0.3 copy.82
  44.1 0.4 fusion.57
  44.5 1.0 constant_dynamic-slice_fusion.4
  45.8 0.4 fusion.57
  46.2 1.0 constant_dynamic-slice_fusion.4
  47.5 0.4 fusion.57
  47.9 1.0 constant_dynamic-slice_fusion.4
  49.2 0.4 fusion.57
  49.6 1.0 constant_dynamic-slice_fusion.4
  50.9 0.4 fusion.57
  51.3 1.0 constant_dynamic-slice_fusion.4
  52.6 0.4 fusion.57
  53.0 1.0 constant_dynamic-slice_fusion.4
  54.3 0.4 fusion.57
  54.7 1.0 constant_dynamic-slice_fusion.4
  56.0 0.4 fusion.57
  56.4 2.1 %fusion.28 = f32[256,16,64]{0,2,1:T(8,128)} fusion(f32[256,16,64]{0,2,1:T(8,128)S(1)} %fusion.30, f32[16,128,64]{2,1,0:T(8,128)S(1)} %get-tuple-element.383, bf16[256,16,64]{0,2,1:T(8,128)(2,1)S(1)} %bitcast.94, f32[16]{0:T(128)S(1)} %copy-done.5, f32[256,16]{0,1:T(8,128)S(1)} %get-tuple-element.483, bf16[256,128]{1,0:T(8,128)(2,1)S(1)} %copy-done), kind=kOutput, calls=%fused_computation.36 | convolution fusion | flops 403963904 | bytes 3227712 | tf_op jit(solution)/shard_map/tn,hnp->thp/dot_general | solution.py:136
  58.5 1.6 copy.59
  60.2 0.4 multiply_reduce_fusion
  60.6 7.8 %psum.7 = f32[256]{0:T(256)S(1)} all-reduce(f32[256]{0:T(256)S(1)} %multiply_reduce_fusion), channel_id=1, replica_groups=mesh['seq'=8,'head'=4] {'head'}, use_global_device_ids=true, to_apply=%region_6.7 | all-reduce | flops 256 | bytes 2048 | tf_op jit(solution)/shard_map/psum | solution.py:143
  68.3 1.2 multiply_convert_fusion
  69.8 1.0 copy.60
  71.3 44.5 %all-gather.8.cloned.1.call-done = bf16[2048,1024]{1,0:T(8,128)(2,1)} async-done(((bf16[256,1024]{1,0:T(8,128)(2,1)}), bf16[2048,1024]{1,0:T(8,128)(2,1)}) %all-gather.8.cloned.1.call-update) | async-done | bytes 4194320 | tf_op jit(solution)/shard_map/all_gather | solution.py:160
  115.8 6.5 %copy.63 = bf16[2048,1024]{0,1:T(8,128)(2,1)} copy(bf16[2048,1024]{1,0:T(8,128)(2,1)} %all-gather.8.cloned.1.call-done) | data formatting | bytes 8388608 | tf_op jit(solution)/shard_map/while | solution.py:192
  122.3 41.8 %all-gather.6.cloned.1.call-done = bf16[2048,1024]{0,1:T(8,128)(2,1)} async-done(((bf16[256,1024]{0,1:T(8,128)(2,1)}), bf16[2048,1024]{0,1:T(8,128)(2,1)}) %all-gather.6.cloned.1.call-update) | async-done | bytes 4194320 | tf_op jit(solution)/shard_map/all_gather | solution.py:159
  164.2 28.6 %while.36 = (s32[]{:T(128)}, f32[8,256]{1,0:T(8,128)S(1)}, f32[8,256]{1,0:T(8,128)S(1)}, f32[8,256,128]{2,1,0:T(8,128)S(1)}, s32[256]{0:T(256)S(1)}, /*index=5*/...) while((s32[]{:T(128)}, f32[8,256]{1,0:T(8,128)S(1)}, ...), condition=%wide.region_12.13_spmd, body=%wide.region_7.12_spmd.sunk | while | flops 551162368 | bytes 22160680 | solution.py:192
  164.2 0.6 slice.28
  165.3 6.0 %conditional.2 = (f32[8,256]{1,0:T(8,128)S(1)}, f32[8,256]{1,0:T(8,128)S(1)}, f32[8,256,128]{2,1,0:T(8,128)S(1)}) conditional(s32[]{:T(128)} %convert_element_type.129, (s32[]{:T(128)}, s32[512]{0:T(512)S(1)}, s32[256]{0:T(256)S(1)}, bf16[2048,1024]{0,1:T(8,128)(2,1)}, bf16[256,8,128]{2,0,1:T(8,128)(2,1)S(1)}, /*index=5*/f32[8,256]{1,0:T(8,128)S(1)}, ...), branch_computations={%region_8.10_spmd, %region_11.11_spmd} | conditional | flops 551162368 | bytes 22142018 | solution.py:104
  165.5 1.7 constant_dynamic-slice_fusion
  167.2 0.9 fusion
  168.2 1.0 fusion.2
  169.2 2.1 %fusion.6 = f32[8,256,128]{2,1,0:T(8,128)S(1)} fusion(bf16[512,8,128]{0,2,1:T(8,128)(2,1)S(1)} %bitcast.91, f32[8,512,256]{2,1,0:T(8,128)S(1)} %get-tuple-element.477, f32[8,256]{1,0:T(8,128)S(1)} %max.5, pred[256,512]{0,1:T(8,128)(4,1)S(1)} %broadcast_compare_fusion, f32[8,256,128]{2,1,0:T(8,128)S(1)} %get-tuple-element.364, ...), kind=kOutput, calls=%fused_computation.7 | convolution fusion | flops 274202624 | bytes 7487488 | tf_op jit(solution)/shard_map/while/body/eval_jaxpr/cond/branch_0_fun/hqk,khd->hqd/dot_general | solution.py:97
  171.3 0.6 slice.28
  172.5 6.0 %conditional.2 = (f32[8,256]{1,0:T(8,128)S(1)}, f32[8,256]{1,0:T(8,128)S(1)}, f32[8,256,128]{2,1,0:T(8,128)S(1)}) conditional(s32[]{:T(128)} %convert_element_type.129, (s32[]{:T(128)}, s32[512]{0:T(512)S(1)}, s32[256]{0:T(256)S(1)}, bf16[2048,1024]{0,1:T(8,128)(2,1)}, bf16[256,8,128]{2,0,1:T(8,128)(2,1)S(1)}, /*index=5*/f32[8,256]{1,0:T(8,128)S(1)}, ...), branch_computations={%region_8.10_spmd, %region_11.11_spmd} | conditional | flops 551162368 | bytes 22142018 | solution.py:104
  172.7 1.7 constant_dynamic-slice_fusion
  174.4 0.9 fusion
  175.3 1.0 fusion.2
  176.3 2.1 %fusion.6 = f32[8,256,128]{2,1,0:T(8,128)S(1)} fusion(bf16[512,8,128]{0,2,1:T(8,128)(2,1)S(1)} %bitcast.91, f32[8,512,256]{2,1,0:T(8,128)S(1)} %get-tuple-element.477, f32[8,256]{1,0:T(8,128)S(1)} %max.5, pred[256,512]{0,1:T(8,128)(4,1)S(1)} %broadcast_compare_fusion, f32[8,256,128]{2,1,0:T(8,128)S(1)} %get-tuple-element.364, ...), kind=kOutput, calls=%fused_computation.7 | convolution fusion | flops 274202624 | bytes 7487488 | tf_op jit(solution)/shard_map/while/body/eval_jaxpr/cond/branch_0_fun/hqk,khd->hqd/dot_general | solution.py:97
  178.5 0.6 slice.28
  179.6 6.0 %conditional.2 = (f32[8,256]{1,0:T(8,128)S(1)}, f32[8,256]{1,0:T(8,128)S(1)}, f32[8,256,128]{2,1,0:T(8,128)S(1)}) conditional(s32[]{:T(128)} %convert_element_type.129, (s32[]{:T(128)}, s32[512]{0:T(512)S(1)}, s32[256]{0:T(256)S(1)}, bf16[2048,1024]{0,1:T(8,128)(2,1)}, bf16[256,8,128]{2,0,1:T(8,128)(2,1)S(1)}, /*index=5*/f32[8,256]{1,0:T(8,128)S(1)}, ...), branch_computations={%region_8.10_spmd, %region_11.11_spmd} | conditional | flops 551162368 | bytes 22142018 | solution.py:104
  179.8 1.7 constant_dynamic-slice_fusion
  181.5 0.9 fusion
  182.5 1.0 fusion.2
  183.5 2.1 %fusion.6 = f32[8,256,128]{2,1,0:T(8,128)S(1)} fusion(bf16[512,8,128]{0,2,1:T(8,128)(2,1)S(1)} %bitcast.91, f32[8,512,256]{2,1,0:T(8,128)S(1)} %get-tuple-element.477, f32[8,256]{1,0:T(8,128)S(1)} %max.5, pred[256,512]{0,1:T(8,128)(4,1)S(1)} %broadcast_compare_fusion, f32[8,256,128]{2,1,0:T(8,128)S(1)} %get-tuple-element.364, ...), kind=kOutput, calls=%fused_computation.7 | convolution fusion | flops 274202624 | bytes 7487488 | tf_op jit(solution)/shard_map/while/body/eval_jaxpr/cond/branch_0_fun/hqk,khd->hqd/dot_general | solution.py:97
  185.6 0.6 slice.28
  186.8 6.0 %conditional.2 = (f32[8,256]{1,0:T(8,128)S(1)}, f32[8,256]{1,0:T(8,128)S(1)}, f32[8,256,128]{2,1,0:T(8,128)S(1)}) conditional(s32[]{:T(128)} %convert_element_type.129, (s32[]{:T(128)}, s32[512]{0:T(512)S(1)}, s32[256]{0:T(256)S(1)}, bf16[2048,1024]{0,1:T(8,128)(2,1)}, bf16[256,8,128]{2,0,1:T(8,128)(2,1)S(1)}, /*index=5*/f32[8,256]{1,0:T(8,128)S(1)}, ...), branch_computations={%region_8.10_spmd, %region_11.11_spmd} | conditional | flops 551162368 | bytes 22142018 | solution.py:104
  187.0 1.7 constant_dynamic-slice_fusion
  188.7 0.9 fusion
  189.6 1.0 fusion.2
  190.6 2.1 %fusion.6 = f32[8,256,128]{2,1,0:T(8,128)S(1)} fusion(bf16[512,8,128]{0,2,1:T(8,128)(2,1)S(1)} %bitcast.91, f32[8,512,256]{2,1,0:T(8,128)S(1)} %get-tuple-element.477, f32[8,256]{1,0:T(8,128)S(1)} %max.5, pred[256,512]{0,1:T(8,128)(4,1)S(1)} %broadcast_compare_fusion, f32[8,256,128]{2,1,0:T(8,128)S(1)} %get-tuple-element.364, ...), kind=kOutput, calls=%fused_computation.7 | convolution fusion | flops 274202624 | bytes 7487488 | tf_op jit(solution)/shard_map/while/body/eval_jaxpr/cond/branch_0_fun/hqk,khd->hqd/dot_general | solution.py:97
  192.8 1.1 copy_bitcast_fusion
  (77 shorter events, 4.6 us)
Async XLA Ops:
  7.2 21.9 %copy-start = (bf16[256,128]{1,0:T(8,128)(2,1)S(1)}, bf16[256,128]{1,0:T(8,128)(2,1)}, u32[]{:S(2)}) copy-start(bf16[256,128]{1,0:T(8,128)(2,1)} %param.19) | copy-start | bytes 196612
  7.2 35.6 %all-gather.10.cloned.1.call-start = ((), (), s32[]{:S(2)}) async-start(), calls=%async_computation.2 | async-start | bytes 2359296 | tf_op jit(solution)/shard_map/all_gather | solution.py:21
  13.4 102.4 %all-gather.8.cloned.1.call-start = ((), (), s32[]{:S(2)}) async-start(), calls=%async_computation.1 | async-start | bytes 4718592 | tf_op jit(solution)/shard_map/all_gather | solution.py:160
  42.8 13.6 %copy-start.5 = (f32[16]{0:T(128)S(1)}, f32[16]{0:T(128)}, u32[]{:S(2)}) copy-start(f32[16]{0:T(128)} %param.22) | copy-start | bytes 196
  56.4 3.8 %copy-start.1 = (bf16[256,1024]{1,0:T(8,128)(2,1)S(1)}, bf16[256,1024]{1,0:T(8,128)(2,1)}, u32[]{:S(2)}) copy-start(bf16[256,1024]{1,0:T(8,128)(2,1)} %param.17) | copy-start | bytes 1572868
  56.4 12.0 %copy-start.4 = (f32[1024]{0:T(1024)S(1)}, f32[1024]{0:T(1024)}, u32[]{:S(2)}) copy-start(f32[1024]{0:T(1024)} %param.23) | copy-start | bytes 12292
  58.5 11.3 %copy-start.2 = (bf16[256,1024]{1,0:T(8,128)(2,1)S(1)}, bf16[256,1024]{1,0:T(8,128)(2,1)}, u32[]{:S(2)}) copy-start(bf16[256,1024]{1,0:T(8,128)(2,1)} %param.25) | copy-start | bytes 1572868
  58.5 12.3 %copy-start.3 = (bf16[256,1024]{1,0:T(8,128)(2,1)S(1)}, bf16[256,1024]{1,0:T(8,128)(2,1)}, u32[]{:S(2)}) copy-start(bf16[256,1024]{1,0:T(8,128)(2,1)} %param.24) | copy-start | bytes 1572868
  69.5 94.6 %all-gather.6.cloned.1.call-start = ((), (), s32[]{:S(2)}) async-start(), calls=%async_computation | async-start | bytes 4718592 | tf_op jit(solution)/shard_map/all_gather | solution.py:159
Sparse Core Ops, SparseCore 0:
  13.5 29.2 all-gather.9
  69.7 46.0 all-gather.7
  118.0 46.0 all-gather.5
where the time goes:
time: 201 us; the launch traced here: 200 us
  waiting for transfers between devices  95.4 us (47%)
  local copies, waits for them, and re-layouts  32 us (16%)
  blocking collectives  21.1 us (10%)
  matrix products  21 us (10%)
  between operations  14.6 us (7%)
  other arithmetic  12.9 us (6%)
  loops' own time  3.13 us (2%)
    all_gather x1, waiting for transfers between devices, on_device(): v_piece = lax.all_gather(mamba_out, 'seq', axis=0, tiled=True)  44.5 us
    all_gather x1, waiting for transfers between devices, on_device(): k_piece = lax.all_gather(keys, 'seq', axis=0, tiled=True)  41.8 us
    unnamed x1, blocking collectives  13.3 us
    dynamic_slice x16, local copies, waits for them, and re-layouts, hop(): part[k].astype(own.dtype)  10.1 us
    all_gather x1, waiting for transfers between devices, carried_in(): lax.all_gather(part.astype(kind), axis)  9.1 us
    dot_general x4, matrix products, online_update(): jnp.einsum('hqk,khd->hqd', weights.astype(jnp.bfloat16), v_rows, preferre...  8.4 us
    psum x1, blocking collectives, on_device(): squares = lax.psum(jnp.sum(gated * gated, axis=1), 'head')  7.76 us
    while x2, local copies, waits for them, and re-layouts, on_device(): finals = lax.fori_loop(0, row_count // block_rows, one_block, states)  6.79 us
  transfers between devices with their start and end apart: 3, of which 3 were waited for; matrix products, arithmetic and copies ran while one was open for 7% of the time, Pallas kernels for 0%

commit v1 on v0

--- a/solution.py
+++ b/solution.py
@@ -4,6 +4,8 @@
 import jax
 import jax.numpy as jnp
 from jax import lax
+from jax.experimental import pallas as pl
+from jax.experimental.pallas import tpu as pltpu
 from jax.sharding import PartitionSpec as P
 
 HD = 128
@@ -13,6 +15,357 @@
 
 HIGH = lax.Precision.HIGHEST
 NEG = -1e30
+LOG2E = 1.4426950408889634
+MIB = 1 << 20
+
+
+VMEM = pl.BlockSpec(memory_space=pltpu.VMEM)
+SMEM = pl.BlockSpec(memory_space=pltpu.SMEM)
+
+
+def call(body, outs, args, scalars, scratch=(), flops=0, moved=0, exps=0, limit=16 * MIB):
+    return pl.pallas_call(
+        body,
+        out_shape=outs,
+        in_specs=[SMEM] * scalars + [VMEM] * (len(args) - scalars),
+        out_specs=jax.tree.map(lambda _: VMEM, outs),
+        scratch_shapes=list(scratch),
+        compiler_params=pltpu.CompilerParams(vmem_limit_bytes=limit),
+        cost_estimate=pl.CostEstimate(flops=flops, bytes_accessed=moved, transcendentals=exps),
+    )(*args)
+
+
+def nt(a, b):
+    return lax.dot_general(a, b, (((1,), (1,)), ((), ())), preferred_element_type=jnp.float32)
+
+
+def nn(a, b):
+    return jnp.dot(a, b, preferred_element_type=jnp.float32)
+
+
+def step_counts(codes):
+    heads, rows = codes.shape
+    r = lax.broadcasted_iota(jnp.int32, (rows, rows), 0)
+    s = lax.broadcasted_iota(jnp.int32, (rows, rows), 1)
+    upper = (r <= s).astype(jnp.float32).astype(jnp.bfloat16)
+    lower = (s <= r).astype(jnp.float32).astype(jnp.bfloat16)
+    high = lax.shift_right_logical(codes, 7).astype(jnp.float32).astype(jnp.bfloat16)
+    low = (codes & 127).astype(jnp.float32).astype(jnp.bfloat16)
+    return (
+        128.0 * nn(high, upper) + nn(low, upper),
+        128.0 * nt(lower, high) + nt(lower, low),
+    )
+
+
+def left_lanes(rows):
+    return lax.broadcasted_iota(jnp.int32, (rows, HD), 1) < CHANNELS_PER_HD
+
+
+def lanes_of(block):
+    return pl.ds(pl.multiple_of(block * HD, HD), HD)
+
+
+def rotated(me, k, n):
+    return lax.rem(me + k, n)
+
+
+def qk_kernel(n, me_ref, q_ref, k_ref, *outs):
+    rows = q_ref.shape[0]
+    me = me_ref[0]
+    for k in range(n):
+        cols = lanes_of(rotated(me, k, n))
+        outs[k][pl.ds(0, rows), :] = q_ref[:, cols]
+        outs[k][pl.ds(rows, rows), :] = k_ref[:, cols]
+
+
+def state_kernel(n, me_ref, rates_ref, x_ref, b_ref, codes_ref, *rest):
+    outs, held = rest[:n], rest[n]
+    rows = x_ref.shape[0]
+    me = me_ref[0]
+    _, counts = step_counts(codes_ref[...])
+    b_turned = b_ref[...].astype(jnp.float32).T.astype(jnp.bfloat16)
+    left = left_lanes(rows)
+    part = lax.broadcasted_iota(jnp.int32, (16, HD), 0)
+    for pair in range(n):
+        ends = []
+        totals = []
+        for h in (2 * pair, 2 * pair + 1):
+            column = counts[:, h : h + 1]
+            total = counts[rows - 1 : rows, h : h + 1]
+            totals.append(total)
+            ends.append(jnp.exp2((total - column) * (-rates_ref[h] * LOG2E)))
+        weight = jnp.where(left, ends[0], ends[1])
+        x = x_ref[:, pair * HD : (pair + 1) * HD].astype(jnp.float32)
+        held[pair, pl.ds(0, HD), :] = nn(b_turned, (x * weight).astype(jnp.bfloat16)).astype(
+            jnp.bfloat16
+        )
+        total = jnp.where(left_lanes(16), totals[0], totals[1]).astype(jnp.int32)
+        parts = jnp.where(
+            part == 0,
+            lax.shift_right_logical(total, 16),
+            jnp.where(
+                part == 1,
+                lax.shift_right_logical(total, 8) & 255,
+                jnp.where(part == 2, total & 255, 0),
+            ),
+        )
+        held[pair, pl.ds(HD, 16), :] = parts.astype(jnp.float32).astype(jnp.bfloat16)
+    for k in range(n):
+        outs[k][...] = held[rotated(me, k, n)]
+
+
+def carry_kernel(n, me_ref, rates_ref, *rest):
+    ins, outs, held, ahead = rest[:n], rest[n : 2 * n], rest[2 * n], rest[2 * n + 1]
+    me = me_ref[0]
+    for k in range(n):
+        held[rotated(me, n - k, n)] = ins[k][...]
+    rate = jnp.where(left_lanes(1), rates_ref[2 * me], rates_ref[2 * me + 1])
+    state = jnp.zeros((HD, HD), jnp.float32)
+    for r in range(n):
+        ahead[r] = state.astype(jnp.bfloat16)
+        parts = held[r, pl.ds(HD, 16), :].astype(jnp.float32)
+        total = 65536.0 * parts[0:1] + 256.0 * parts[1:2] + parts[2:3]
+        decay = jnp.exp2(total * (-rate * LOG2E))
+        state = decay * state + held[r, pl.ds(0, HD), :].astype(jnp.float32)
+    for k in range(n):
+        outs[k][...] = ahead[rotated(me, k, n)]
+
+
+def within_kernel(
+    n, rates_ref, skip_ref, x_ref, gate_ref, b_ref, c_ref, codes_ref, own_ref, lead_ref
+):
+    rows = x_ref.shape[0]
+    across, down = step_counts(codes_ref[...])
+    t = lax.broadcasted_iota(jnp.int32, (rows, rows), 0)
+    s = lax.broadcasted_iota(jnp.int32, (rows, rows), 1)
+    match = jnp.where(s <= t, nt(c_ref[...], b_ref[...]), 0.0)
+    left = left_lanes(rows)
+    for pair in range(n):
+        cols = slice(pair * HD, (pair + 1) * HD)
+        x = x_ref[:, cols]
+        ys = []
+        leads = []
+        for h in (2 * pair, 2 * pair + 1):
+            slope = -rates_ref[h] * LOG2E
+            gap = jnp.maximum(down[:, h : h + 1] - across[h : h + 1, :], 0.0)
+            ys.append(nn((jnp.exp2(gap * slope) * match).astype(jnp.bfloat16), x))
+            leads.append(jnp.exp2(down[:, h : h + 1] * slope))
+        skip = jnp.where(left_lanes(1), skip_ref[2 * pair], skip_ref[2 * pair + 1])
+        gate = gate_ref[:, cols].astype(jnp.float32)
+        gate = gate / (1.0 + jnp.exp(-gate))
+        own_ref[:, cols] = (jnp.where(left, ys[0], ys[1]) + skip * x.astype(jnp.float32)) * gate
+        lead_ref[:, cols] = jnp.where(left, leads[0], leads[1]) * gate
+
+
+def gated_kernel(n, me_ref, own_ref, lead_ref, c_ref, *rest):
+    states, gated_ref, squares_ref, outs = rest[:n], rest[n], rest[n + 1], rest[n + 2 :]
+    me = me_ref[0]
+    ones = jnp.ones((8, HD), jnp.bfloat16)
+    total = jnp.zeros(squares_ref.shape, jnp.float32)
+    for k in range(n):
+        cols = lanes_of(rotated(me, n - k, n))
+        gated = own_ref[:, cols] + lead_ref[:, cols] * nn(c_ref[...], states[k][...])
+        gated_ref[:, cols] = gated
+        outs[(n - k) % n][...] = gated.astype(jnp.bfloat16)
+        square = gated * gated
+        high = square.astype(jnp.bfloat16)
+        low = (square - high.astype(jnp.float32)).astype(jnp.bfloat16)
+        total = total + nt(ones, high) + nt(ones, low)
+    squares_ref[...] = total
+
+
+def turned(row):
+    size = row.shape[1]
+    r = lax.broadcasted_iota(jnp.int32, (size, size), 0)
+    s = lax.broadcasted_iota(jnp.int32, (size, size), 1)
+    return jnp.sum(jnp.where(r == s, jnp.broadcast_to(row, (size, size)), 0.0), axis=1, keepdims=True)
+
+
+def norm_kernel(m, channels, gated_ref, gain_ref, *rest):
+    squares, out_ref, factor_ref = rest[:m], rest[m], rest[m + 1]
+    total = squares[0][...]
+    for part in squares[1:]:
+        total = total + part[...]
+    factor = lax.rsqrt(total / channels + 1e-05)
+    factor_ref[...] = factor
+    column = turned(factor[0:1])
+    for at in range(0, gated_ref.shape[1], HD):
+        cols = slice(at, at + HD)
+        out_ref[:, cols] = (gated_ref[:, cols] * column * gain_ref[:, cols]).astype(jnp.bfloat16)
+
+
+def weights_kernel(n, me_ref, *rest):
+    ins, out_ref, q_ref, k_ref = rest[:n], rest[n], rest[n + 1], rest[n + 2]
+    rows = ins[0].shape[0] // 2
+    me = me_ref[0]
+    for k in range(n):
+        at = pl.ds(pl.multiple_of(rotated(me, n - k, n) * rows, rows), rows)
+        q_ref[at, :] = ins[k][pl.ds(0, rows), :]
+        k_ref[at, :] = ins[k][pl.ds(rows, rows), :]
+    scale = LOG2E / math.sqrt(HD)
+    half = rows // 2
+    for i in range(2 * n):
+        seen = (i // 2) * rows
+        q = q_ref[pl.ds(i * half, half), :]
+        t = lax.broadcasted_iota(jnp.int32, (half, rows), 0) + (i % 2) * half
+        s = lax.broadcasted_iota(jnp.int32, (half, rows), 1)
+        blocks = [nt(q, k_ref[pl.ds(at, rows), :]) for at in range(0, seen, rows)]
+        blocks.append(jnp.where(s <= t, nt(q, k_ref[pl.ds(seen, rows), :]), NEG))
+        top = functools.reduce(jnp.maximum, blocks)
+        top = jnp.max(top, axis=1, keepdims=True) * scale
+        blocks = [jnp.exp2(block * scale - top) for block in blocks]
+        total = jnp.sum(functools.reduce(jnp.add, blocks), axis=1, keepdims=True)
+        inverse = 1.0 / total
+        for j, block in enumerate(blocks):
+            out_ref[pl.ds(i * half, half), pl.ds(j * rows, rows)] = (block * inverse).astype(
+                jnp.bfloat16
+            )
+
+
+def values_kernel(n, me_ref, weights_ref, gain_ref, *rest):
+    ins, factors, outs = rest[:n], rest[n : 2 * n], rest[2 * n : 3 * n]
+    v_ref, o_ref = rest[3 * n :]
+    rows = ins[0].shape[0]
+    me = me_ref[0]
+    gain = gain_ref[:, lanes_of(me)]
+    for k in range(n):
+        at = pl.ds(pl.multiple_of(rotated(me, n - k, n) * rows, rows), rows)
+        column = turned(factors[k][0:1, :])
+        v_ref[at, :] = (ins[k][...].astype(jnp.float32) * column * gain).astype(jnp.bfloat16)
+    for i in range(n):
+        seen = (i + 1) * rows
+        o_ref[i] = nn(
+            weights_ref[pl.ds(i * rows, rows), pl.ds(0, seen)], v_ref[pl.ds(0, seen), :]
+        ).astype(jnp.bfloat16)
+    for k in range(n):
+        outs[k][...] = o_ref[rotated(me, k, n)]
+
+
+def join_kernel(n, me_ref, *rest):
+    me = me_ref[0]
+    for k in range(n):
+        rest[n][:, lanes_of(rotated(me, n - k, n))] = rest[k][...]
+
+
+def exchange(parts, axis):
+    n = len(parts)
+    return [parts[0]] + [
+        lax.ppermute(parts[k], axis, [(i, (i + k) % n) for i in range(n)]) for k in range(1, n)
+    ]
+
+
+def one_head_each(
+    mixer_input,
+    gate_input,
+    b_proj,
+    c_proj,
+    decay_codes,
+    decay_rates,
+    skip_gain,
+    norm_gain,
+    queries,
+    keys,
+):
+    n, m = lax.axis_size("seq"), lax.axis_size("head")
+    rows, width = mixer_input.shape
+    me = lax.axis_index("seq").astype(jnp.int32).reshape(1)
+    gain = norm_gain.reshape(1, width)
+    shape = jax.ShapeDtypeStruct
+    bf16, f32 = jnp.bfloat16, jnp.float32
+    chunk = shape((rows, HD), bf16)
+
+    states = call(
+        functools.partial(state_kernel, n),
+        [shape((HD + 16, HD), bf16)] * n,
+        (me, decay_rates, mixer_input, b_proj, decay_codes),
+        2,
+        [pltpu.VMEM((n, HD + 16, HD), bf16)],
+        flops=2 * rows * HD * width,
+        moved=3 * rows * width,
+    )
+    states = exchange(states, "seq")
+    qk = call(
+        functools.partial(qk_kernel, n),
+        [shape((2 * rows, HD), bf16)] * n,
+        (me, queries, keys),
+        1,
+        moved=8 * rows * width,
+    )
+    qk = exchange(qk, "seq")
+    own, lead = call(
+        functools.partial(within_kernel, n),
+        [shape((rows, width), f32)] * 2,
+        (decay_rates, skip_gain, mixer_input, gate_input, b_proj, c_proj, decay_codes),
+        2,
+        flops=4 * rows * rows * width,
+        moved=12 * rows * width,
+        exps=2 * n * rows * rows,
+    )
+    ahead = call(
+        functools.partial(carry_kernel, n),
+        [shape((HD, HD), bf16)] * n,
+        (me, decay_rates, *states),
+        2,
+        [pltpu.VMEM((n, HD + 16, HD), bf16), pltpu.VMEM((n, HD, HD), bf16)],
+        flops=4 * n * HD * HD,
+        moved=4 * n * HD * HD,
+    )
+    ahead = exchange(ahead, "seq")
+    gated, squares, *values = call(
+        functools.partial(gated_kernel, n),
+        [shape((rows, width), f32), shape((8, rows), f32)] + [chunk] * n,
+        (me, own, lead, c_proj, *ahead),
+        1,
+        flops=4 * rows * HD * width,
+        moved=14 * rows * width,
+    )
+    values = exchange(values, "seq")
+    squares = exchange([squares] * m, "head")
+    mamba_out, factor = call(
+        functools.partial(norm_kernel, m, width * m),
+        [shape((rows, width), bf16), shape((8, rows), f32)],
+        (gated, gain, *squares),
+        0,
+        flops=4 * rows * width,
+        moved=6 * rows * width,
+    )
+    factors = exchange([factor] * n, "seq")
+    weights = call(
+        functools.partial(weights_kernel, n),
+        shape((n * rows, n * rows), bf16),
+        (me, *qk),
+        1,
+        [pltpu.VMEM((n * rows, HD), bf16), pltpu.VMEM((n * rows, HD), bf16)],
+        flops=n * n * rows * rows * HD,
+        moved=2 * n * n * rows * rows,
+        exps=n * n * rows * rows // 2,
+        limit=24 * MIB,
+    )
+    results = call(
+        functools.partial(values_kernel, n),
+        [chunk] * n,
+        (me, weights, gain, *values, *factors),
+        1,
+        [pltpu.VMEM((n * rows, HD), bf16), pltpu.VMEM((n, rows, HD), bf16)],
+        flops=n * n * rows * rows * HD,
+        moved=2 * n * n * rows * rows,
+    )
+    results = exchange(results, "seq")
+    attn_out = call(
+        functools.partial(join_kernel, n),
+        shape((rows, width), bf16),
+        (me, *results),
+        1,
+        moved=4 * rows * width,
+    )
+    return (mamba_out, attn_out)
+
+
+def running_sum(log_decay):
+    span = log_decay.shape[1]
+    at = jnp.arange(span, dtype=jnp.int32)
+    earlier = (at[:, None] <= at[None, :]).astype(jnp.float32)
+    return jnp.dot(log_decay, earlier, precision=HIGH)
 
 
 def carried_in(array, axis, combine, identity):
@@ -40,7 +393,7 @@
 
 def block_step(state_carry, inputs):
     x_block, b_block, c_block, decay_block = inputs
-    running = jnp.cumsum(decay_block, axis=1)
+    running = running_sum(decay_block)
     span = decay_block.shape[1]
     causal = (
         jnp.arange(span, dtype=jnp.int32)[:, None] >= jnp.arange(span, dtype=jnp.int32)[None, :]
@@ -104,7 +457,7 @@
     return lax.cond(key_offset > q_pos[-1], lambda held: held, state_update, group_state)
 
 
-def on_device(
+def gathered(
     mixer_input,
     gate_input,
     b_proj,
@@ -132,7 +485,7 @@
 
     identity = (jnp.zeros_like(total_log), jnp.zeros_like(local_state))
     _, incoming = carried_in((total_log, local_state), "seq", combine, identity)
-    running = jnp.cumsum(log_decay, axis=1)
+    running = running_sum(log_decay)
     carried = jnp.einsum("tn,hnp->thp", c_proj.astype(jnp.float32), incoming, precision=HIGH)
     carried = carried * jnp.exp(running).T[:, :, None]
     x_float = mixer_input.reshape(tok_rows, heads_local, CHANNELS_PER_HD).astype(jnp.float32)
@@ -202,6 +555,21 @@
     return (mamba_out, attn_out)
 
 
+def on_device(mixer_input, gate_input, b_proj, c_proj, decay_codes, *others):
+    n = lax.axis_size("seq")
+    rows, width = mixer_input.shape
+    fits = (
+        width == n * HD
+        and decay_codes.shape[0] == 2 * n
+        and b_proj.shape[1] == HD
+        and rows == BLOCK
+        and n <= 8
+    )
+    return (one_head_each if fits else gathered)(
+        mixer_input, gate_input, b_proj, c_proj, decay_codes, *others
+    )
+
+
 def solution(mesh):
     in_specs = (
         P("seq", "head"),

time: 201 us -> 120 us (0.60)
  the two profiles are of different devices: /device:TPU:25 before, /device:TPU:0 now
where the time goes in v1:
time: 120 us; the launch traced here: 119 us
  starting transfers between devices  57.8 us (48%)
  waiting for transfers between devices  35.7 us (30%)
  Pallas kernels  13.2 us (11%)
  local copies, waits for them, and re-layouts  11.8 us (10%)
    ppermute x45, starting transfers between devices, exchange(): lax.ppermute(parts[k], axis, [(i, (i + k) % n) for i in range(n)])  57.8 us
    ppermute x45, waiting for transfers between devices, exchange(): lax.ppermute(parts[k], axis, [(i, (i + k) % n) for i in range(n)])  35.7 us
    pallas_call x9, Pallas kernels, call(): pl.pallas_call(body, out_shape=outs, in_specs=[SMEM] * scalars + [VMEM] *...  13.2 us
    unnamed x30, local copies, waits for them, and re-layouts  11.8 us
  transfers between devices with their start and end apart: 45, of which 20 were waited for; matrix products, arithmetic and copies ran while one was open for 0% of the time, Pallas kernels for 7%

profile of v1, /device:TPU:0, one launch (start us, length us, event | category | flops | bytes accessed | tf_op | source)
XLA Modules:
  0.0 119.2 jit_solution(17958180924005143683)
XLA Ops:
  0.6 1.0 copy-done
  1.7 0.8 copy-done.4
  2.5 0.7 copy-done.9
  3.2 0.7 copy-done.11
  3.9 1.7 %shard_map.114 = (bf16[144,128]{1,0:T(8,128)(2,1)S(1)}, bf16[144,128]{1,0:T(8,128)(2,1)S(1)}, bf16[144,128]{1,0:T(8,128)(2,1)S(1)}, bf16[144,128]{1,0:T(8,128)(2...) custom-call(s32[1]{0:T(128)} %bitcast.me_ref, ...), custom_call_target="tpu_custom_call" | custom-call | flops 67108864 | bytes 786432 | tf_op jit(solution)/shard_map/pallas_call | solution.py:27
  6.1 2.6 %collective-permute-start.1 = (bf16[144,128]{1,0:T(8,128)(2,1)S(1)}, bf16[144,128]{1,0:T(8,128)(2,1)S(1)}, u32[]{:S(2)}, u32[]{:S(2)}) collective-permute-start(bf16[144,128]{1,0:T(8,128)(2,1)S(1)} %get-tuple-element.52), channel_id=1, source_target_pairs={{0,8},{4,12},{8,16},{12,20},{16,24},{20,28},{24,0},{28,4},{1,9},{5... | collective-permute-start | bytes 110600 | tf_op jit(solution)/shard_map/ppermute | solution.py:253
  8.8 2.5 %collective-permute-start.2 = (bf16[144,128]{1,0:T(8,128)(2,1)S(1)}, bf16[144,128]{1,0:T(8,128)(2,1)S(1)}, u32[]{:S(2)}, u32[]{:S(2)}) collective-permute-start(bf16[144,128]{1,0:T(8,128)(2,1)S(1)} %get-tuple-element.53), channel_id=1, source_target_pairs={{0,12},{4,16},{8,20},{12,24},{16,28},{20,0},{24,4},{28,8},{1,13},{... | collective-permute-start | bytes 110600 | tf_op jit(solution)/shard_map/ppermute | solution.py:253
  11.3 1.2 %collective-permute-start.3 = (bf16[144,128]{1,0:T(8,128)(2,1)S(1)}, bf16[144,128]{1,0:T(8,128)(2,1)S(1)}, u32[]{:S(2)}, u32[]{:S(2)}) collective-permute-start(bf16[144,128]{1,0:T(8,128)(2,1)S(1)} %get-tuple-element.54), channel_id=1, source_target_pairs={{0,16},{4,20},{8,24},{12,28},{16,0},{20,4},{24,8},{28,12},{1,17},{... | collective-permute-start | bytes 110600 | tf_op jit(solution)/shard_map/ppermute | solution.py:253
  12.5 1.2 collective-permute-start.4
  13.7 1.4 %collective-permute-start.5 = (bf16[144,128]{1,0:T(8,128)(2,1)S(1)}, bf16[144,128]{1,0:T(8,128)(2,1)S(1)}, u32[]{:S(2)}, u32[]{:S(2)}) collective-permute-start(bf16[144,128]{1,0:T(8,128)(2,1)S(1)} %get-tuple-element.56), channel_id=1, source_target_pairs={{0,24},{4,28},{8,0},{12,4},{16,8},{20,12},{24,16},{28,20},{1,25},{... | collective-permute-start | bytes 110600 | tf_op jit(solution)/shard_map/ppermute | solution.py:253
  15.1 1.4 %collective-permute-start.6 = (bf16[144,128]{1,0:T(8,128)(2,1)S(1)}, bf16[144,128]{1,0:T(8,128)(2,1)S(1)}, u32[]{:S(2)}, u32[]{:S(2)}) collective-permute-start(bf16[144,128]{1,0:T(8,128)(2,1)S(1)} %get-tuple-element.57), channel_id=1, source_target_pairs={{0,28},{4,0},{8,4},{12,8},{16,12},{20,16},{24,20},{28,24},{1,29},{... | collective-permute-start | bytes 110600 | tf_op jit(solution)/shard_map/ppermute | solution.py:253
  16.7 1.3 %collective-permute-done.5.rest_6_ = bf16[144,128]{1,0:T(8,128)(2,1)S(1)} collective-permute-done((bf16[144,128]{1,0:T(8,128)(2,1)S(1)}, bf16[144,128]{1,0:T(8,128)(2,1)S(1)}, u32[]{:S(2)}, u32[]{:S(2)}) %collective-permute-start.5) | collective-permute-done | bytes 36896 | tf_op jit(solution)/shard_map/ppermute | solution.py:253
  18.1 0.7 shard_map.115
  18.8 0.8 collective-permute-start.7
  20.1 2.2 %collective-permute-start.9 = (bf16[128,128]{1,0:T(8,128)(2,1)S(1)}, bf16[128,128]{1,0:T(8,128)(2,1)S(1)}, u32[]{:S(2)}, u32[]{:S(2)}) collective-permute-start(bf16[128,128]{1,0:T(8,128)(2,1)S(1)} %get-tuple-element.61), channel_id=1, source_target_pairs={{0,12},{4,16},{8,20},{12,24},{16,28},{20,0},{24,4},{28,8},{1,13},{... | collective-permute-start | bytes 98312 | tf_op jit(solution)/shard_map/ppermute | solution.py:253
  22.3 1.4 %collective-permute-start.10 = (bf16[128,128]{1,0:T(8,128)(2,1)S(1)}, bf16[128,128]{1,0:T(8,128)(2,1)S(1)}, u32[]{:S(2)}, u32[]{:S(2)}) collective-permute-start(bf16[128,128]{1,0:T(8,128)(2,1)S(1)} %get-tuple-element.62), channel_id=1, source_target_pairs={{0,16},{4,20},{8,24},{12,28},{16,0},{20,4},{24,8},{28,12},{1,17},{... | collective-permute-start | bytes 98312 | tf_op jit(solution)/shard_map/ppermute | solution.py:253
  23.7 1.0 copy-done.2
  24.7 1.0 copy-done.3
  26.6 3.4 %collective-permute-start.11 = (bf16[128,128]{1,0:T(8,128)(2,1)S(1)}, bf16[128,128]{1,0:T(8,128)(2,1)S(1)}, u32[]{:S(2)}, u32[]{:S(2)}) collective-permute-start(bf16[128,128]{1,0:T(8,128)(2,1)S(1)} %get-tuple-element.63), channel_id=1, source_target_pairs={{0,20},{4,24},{8,28},{12,0},{16,4},{20,8},{24,12},{28,16},{1,21},{... | collective-permute-start | bytes 98312 | tf_op jit(solution)/shard_map/ppermute | solution.py:253
  29.9 1.1 collective-permute-start.12
  31.5 1.0 copy-done.1
  32.5 0.8 copy-done.5
  33.4 0.8 copy-done.6
  34.2 0.7 copy-done.10
  34.9 0.7 copy-done.12
  35.6 1.0 copy-done.13
  36.6 0.7 copy-done.14
  37.3 2.5 %shard_map.113 = (f32[256,1024]{1,0:T(8,128)S(1)}, f32[256,1024]{1,0:T(8,128)S(1)}) custom-call(f32[16]{0:T(128)S(1)} %copy-done.12, f32[16]{0:T(128)S(1)} %copy-done.14, bf16[256,1024]{1,0:T(8,128)(2,1)S(1)} %copy-done.1, bf16[256,1024]{1,0:T(8,128)(2,1)S(1)} %copy-done.13, bf16[256,128]{1,0:T(8,128)(2,1)S(1)} %copy-done.5, bf16[256,128]{1,0:T(8,128)(2,1)S(1)} %copy-done.6, ...), custom_call_target="tpu_custom_call" | custom-call | flops 268435456 | bytes 3145728 | tf_op jit(solution)/shard_map/pallas_call | solution.py:27
  39.8 1.1 shard_map.116
  40.9 1.5 %collective-permute-start.14 = (f32[8,256]{1,0:T(8,128)S(1)}, f32[8,256]{1,0:T(8,128)S(1)}, u32[]{:S(2)}, u32[]{:S(2)}) collective-permute-start(f32[8,256]{1,0:T(8,128)S(1)} %get-tuple-element.67.rest_0_), channel_id=1, source_target_pairs={{0,1},{1,2},{2,3},{3,0},{4,5},{5,6},{6,7},{7,4},{8,9},{9,10},{10,1... | collective-permute-start | bytes 24584 | tf_op jit(solution)/shard_map/ppermute | solution.py:253
  42.4 1.5 %collective-permute-start.15 = (f32[8,256]{1,0:T(8,128)S(1)}, f32[8,256]{1,0:T(8,128)S(1)}, u32[]{:S(2)}, u32[]{:S(2)}) collective-permute-start(f32[8,256]{1,0:T(8,128)S(1)} %get-tuple-element.67.rest_0_), channel_id=1, source_target_pairs={{0,2},{1,3},{2,0},{3,1},{4,6},{5,7},{6,4},{7,5},{8,10},{9,11},{10,... | collective-permute-start | bytes 24584 | tf_op jit(solution)/shard_map/ppermute | solution.py:253
  43.9 1.4 %collective-permute-start.16 = (f32[8,256]{1,0:T(8,128)S(1)}, f32[8,256]{1,0:T(8,128)S(1)}, u32[]{:S(2)}, u32[]{:S(2)}) collective-permute-start(f32[8,256]{1,0:T(8,128)S(1)} %get-tuple-element.67.rest_0_), channel_id=1, source_target_pairs={{0,3},{1,0},{2,1},{3,2},{4,7},{5,4},{6,5},{7,6},{8,11},{9,8},{10,9... | collective-permute-start | bytes 24584 | tf_op jit(solution)/shard_map/ppermute | solution.py:253
  45.5 0.6 collective-permute-done.15.rest_2_
  46.1 1.5 %collective-permute-start.20 = (bf16[512,128]{1,0:T(8,128)(2,1)S(1)}, bf16[512,128]{1,0:T(8,128)(2,1)S(1)}, u32[]{:S(2)}, u32[]{:S(2)}) collective-permute-start(bf16[512,128]{1,0:T(8,128)(2,1)S(1)} %get-tuple-element.73), channel_id=1, source_target_pairs={{0,16},{4,20},{8,24},{12,28},{16,0},{20,4},{24,8},{28,12},{1,17},{... | collective-permute-start | bytes 393224 | tf_op jit(solution)/shard_map/ppermute | solution.py:253
  47.6 0.7 copy-done.7
  48.3 1.0 shard_map.117
  49.3 0.7 collective-permute-start.31
  49.9 5.4 %collective-permute-done.31.rest_9_ = f32[8,256]{1,0:T(8,128)S(1)} collective-permute-done((f32[8,256]{1,0:T(8,128)S(1)}, f32[8,256]{1,0:T(8,128)S(1)}, u32[]{:S(2)}, u32[]{:S(2)}) %collective-permute-start.31) | collective-permute-done | bytes 8224 | tf_op jit(solution)/shard_map/ppermute | solution.py:253
  55.3 5.4 %collective-permute-done.32.rest_10_ = f32[8,256]{1,0:T(8,128)S(1)} collective-permute-done((f32[8,256]{1,0:T(8,128)S(1)}, f32[8,256]{1,0:T(8,128)S(1)}, u32[]{:S(2)}, u32[]{:S(2)}) %collective-permute-start.32) | collective-permute-done | bytes 8224 | tf_op jit(solution)/shard_map/ppermute | solution.py:253
  60.8 4.0 %collective-permute-done.33.rest_11_ = f32[8,256]{1,0:T(8,128)S(1)} collective-permute-done((f32[8,256]{1,0:T(8,128)S(1)}, f32[8,256]{1,0:T(8,128)S(1)}, u32[]{:S(2)}, u32[]{:S(2)}) %collective-permute-start.33) | collective-permute-done | bytes 8224 | tf_op jit(solution)/shard_map/ppermute | solution.py:253
  64.7 1.8 %collective-permute-start.34 = (f32[8,256]{1,0:T(8,128)S(1)}, f32[8,256]{1,0:T(8,128)S(1)}, u32[]{:S(2)}, u32[]{:S(2)}) collective-permute-start(f32[8,256]{1,0:T(8,128)S(1)} %get-tuple-element.85.rest_8_), channel_id=1, source_target_pairs={{0,16},{4,20},{8,24},{12,28},{16,0},{20,4},{24,8},{28,12},{1,17},{... | collective-permute-start | bytes 24584 | tf_op jit(solution)/shard_map/ppermute | solution.py:253
  66.6 2.7 %collective-permute-done.34.rest_12_ = f32[8,256]{1,0:T(8,128)S(1)} collective-permute-done((f32[8,256]{1,0:T(8,128)S(1)}, f32[8,256]{1,0:T(8,128)S(1)}, u32[]{:S(2)}, u32[]{:S(2)}) %collective-permute-start.34) | collective-permute-done | bytes 8224 | tf_op jit(solution)/shard_map/ppermute | solution.py:253
  69.3 3.1 %collective-permute-done.35.rest_13_ = f32[8,256]{1,0:T(8,128)S(1)} collective-permute-done((f32[8,256]{1,0:T(8,128)S(1)}, f32[8,256]{1,0:T(8,128)S(1)}, u32[]{:S(2)}, u32[]{:S(2)}) %collective-permute-start.35) | collective-permute-done | bytes 8224 | tf_op jit(solution)/shard_map/ppermute | solution.py:253
  72.4 3.1 %collective-permute-start.36 = (f32[8,256]{1,0:T(8,128)S(1)}, f32[8,256]{1,0:T(8,128)S(1)}, u32[]{:S(2)}, u32[]{:S(2)}) collective-permute-start(f32[8,256]{1,0:T(8,128)S(1)} %get-tuple-element.85.rest_8_), channel_id=1, source_target_pairs={{0,24},{4,28},{8,0},{12,4},{16,8},{20,12},{24,16},{28,20},{1,25},{... | collective-permute-start | bytes 24584 | tf_op jit(solution)/shard_map/ppermute | solution.py:253
  75.4 1.4 %collective-permute-done.36.rest_14_ = f32[8,256]{1,0:T(8,128)S(1)} collective-permute-done((f32[8,256]{1,0:T(8,128)S(1)}, f32[8,256]{1,0:T(8,128)S(1)}, u32[]{:S(2)}, u32[]{:S(2)}) %collective-permute-start.36) | collective-permute-done | bytes 8224 | tf_op jit(solution)/shard_map/ppermute | solution.py:253
  76.8 0.6 collective-permute-start.37
  77.4 1.4 %collective-permute-done.37.rest_15_ = f32[8,256]{1,0:T(8,128)S(1)} collective-permute-done((f32[8,256]{1,0:T(8,128)S(1)}, f32[8,256]{1,0:T(8,128)S(1)}, u32[]{:S(2)}, u32[]{:S(2)}) %collective-permute-start.37) | collective-permute-done | bytes 8224 | tf_op jit(solution)/shard_map/ppermute | solution.py:253
  78.8 3.7 %collective-permute-start.21 = (bf16[512,128]{1,0:T(8,128)(2,1)S(1)}, bf16[512,128]{1,0:T(8,128)(2,1)S(1)}, u32[]{:S(2)}, u32[]{:S(2)}) collective-permute-start(bf16[512,128]{1,0:T(8,128)(2,1)S(1)} %get-tuple-element.74), channel_id=1, source_target_pairs={{0,20},{4,24},{8,28},{12,0},{16,4},{20,8},{24,12},{28,16},{1,21},{... | collective-permute-start | bytes 393224 | tf_op jit(solution)/shard_map/ppermute | solution.py:253
  82.5 1.2 collective-permute-start.23
  83.7 1.3 %collective-permute-start.25 = (bf16[256,128]{1,0:T(8,128)(2,1)S(1)}, bf16[256,128]{1,0:T(8,128)(2,1)S(1)}, u32[]{:S(2)}, u32[]{:S(2)}) collective-permute-start(bf16[256,128]{1,0:T(8,128)(2,1)S(1)} %get-tuple-element.79), channel_id=1, source_target_pairs={{0,8},{4,12},{8,16},{12,20},{16,24},{20,28},{24,0},{28,4},{1,9},{5... | collective-permute-start | bytes 196616 | tf_op jit(solution)/shard_map/ppermute | solution.py:253
  85.0 1.4 %collective-permute-done.21.rest_5_ = bf16[512,128]{1,0:T(8,128)(2,1)S(1)} collective-permute-done((bf16[512,128]{1,0:T(8,128)(2,1)S(1)}, bf16[512,128]{1,0:T(8,128)(2,1)S(1)}, u32[]{:S(2)}, u32[]{:S(2)}) %collective-permute-start.21) | collective-permute-done | bytes 131104 | tf_op jit(solution)/shard_map/ppermute | solution.py:253
  86.6 2.6 %collective-permute-done.22.rest_6_ = bf16[512,128]{1,0:T(8,128)(2,1)S(1)} collective-permute-done((bf16[512,128]{1,0:T(8,128)(2,1)S(1)}, bf16[512,128]{1,0:T(8,128)(2,1)S(1)}, u32[]{:S(2)}, u32[]{:S(2)}) %collective-permute-start.22) | collective-permute-done | bytes 131104 | tf_op jit(solution)/shard_map/ppermute | solution.py:253
  89.2 8.2 %collective-permute-start.27 = (bf16[256,128]{1,0:T(8,128)(2,1)S(1)}, bf16[256,128]{1,0:T(8,128)(2,1)S(1)}, u32[]{:S(2)}, u32[]{:S(2)}) collective-permute-start(bf16[256,128]{1,0:T(8,128)(2,1)S(1)} %get-tuple-element.81), channel_id=1, source_target_pairs={{0,16},{4,20},{8,24},{12,28},{16,0},{20,4},{24,8},{28,12},{1,17},{... | collective-permute-start | bytes 196616 | tf_op jit(solution)/shard_map/ppermute | solution.py:253
  97.4 2.1 %collective-permute-start.29 = (bf16[256,128]{1,0:T(8,128)(2,1)S(1)}, bf16[256,128]{1,0:T(8,128)(2,1)S(1)}, u32[]{:S(2)}, u32[]{:S(2)}) collective-permute-start(bf16[256,128]{1,0:T(8,128)(2,1)S(1)} %get-tuple-element.83), channel_id=1, source_target_pairs={{0,24},{4,28},{8,0},{12,4},{16,8},{20,12},{24,16},{28,20},{1,25},{... | collective-permute-start | bytes 196616 | tf_op jit(solution)/shard_map/ppermute | solution.py:253
  99.5 3.2 %shard_map.119.weights_ref = bf16[2048,2048]{1,0:T(8,128)(2,1)S(1)} custom-call(s32[1]{0:T(128)} %bitcast.me_ref, bf16[512,128]{1,0:T(8,128)(2,1)S(1)} %get-tuple-element.69.rest_0_, bf16[512,128]{1,0:T(8,128)(2,1)S(1)} %collective-permute-done.17.rest_1_, bf16[512,128]{1,0:T(8,128)(2,1)S(1)} %collective-permute-done.18.rest_2_, ...), custom_call_target="tpu_custom_call" | custom-call | flops 536870912 | bytes 8388608 | tf_op jit(solution)/shard_map/pallas_call | solution.py:27
  103.0 1.8 %shard_map.120 = (bf16[256,128]{1,0:T(8,128)(2,1)S(1)}, bf16[256,128]{1,0:T(8,128)(2,1)S(1)}, bf16[256,128]{1,0:T(8,128)(2,1)S(1)}, bf16[256,128]{1,0:T(8,128)(2...) custom-call(s32[1]{0:T(128)} %bitcast.me_ref, ...), custom_call_target="tpu_custom_call" | custom-call | flops 536870912 | bytes 8388608 | tf_op jit(solution)/shard_map/pallas_call | solution.py:27
  104.8 1.2 %collective-permute-start.38 = (bf16[256,128]{1,0:T(8,128)(2,1)S(1)}, bf16[256,128]{1,0:T(8,128)(2,1)S(1)}, u32[]{:S(2)}, u32[]{:S(2)}) collective-permute-start(bf16[256,128]{1,0:T(8,128)(2,1)S(1)} %get-tuple-element.87), channel_id=1, source_target_pairs={{0,4},{4,8},{8,12},{12,16},{16,20},{20,24},{24,28},{28,0},{1,5},{5... | collective-permute-start | bytes 196616 | tf_op jit(solution)/shard_map/ppermute | solution.py:253
  106.6 1.5 %collective-permute-start.40 = (bf16[256,128]{1,0:T(8,128)(2,1)S(1)}, bf16[256,128]{1,0:T(8,128)(2,1)S(1)}, u32[]{:S(2)}, u32[]{:S(2)}) collective-permute-start(bf16[256,128]{1,0:T(8,128)(2,1)S(1)} %get-tuple-element.89), channel_id=1, source_target_pairs={{0,12},{4,16},{8,20},{12,24},{16,28},{20,0},{24,4},{28,8},{1,13},{... | collective-permute-start | bytes 196616 | tf_op jit(solution)/shard_map/ppermute | solution.py:253
  108.1 1.8 %collective-permute-start.41 = (bf16[256,128]{1,0:T(8,128)(2,1)S(1)}, bf16[256,128]{1,0:T(8,128)(2,1)S(1)}, u32[]{:S(2)}, u32[]{:S(2)}) collective-permute-start(bf16[256,128]{1,0:T(8,128)(2,1)S(1)} %get-tuple-element.90), channel_id=1, source_target_pairs={{0,16},{4,20},{8,24},{12,28},{16,0},{20,4},{24,8},{28,12},{1,17},{... | collective-permute-start | bytes 196616 | tf_op jit(solution)/shard_map/ppermute | solution.py:253
  109.9 1.1 collective-permute-start.42
  111.0 1.5 %collective-permute-start.43 = (bf16[256,128]{1,0:T(8,128)(2,1)S(1)}, bf16[256,128]{1,0:T(8,128)(2,1)S(1)}, u32[]{:S(2)}, u32[]{:S(2)}) collective-permute-start(bf16[256,128]{1,0:T(8,128)(2,1)S(1)} %get-tuple-element.92), channel_id=1, source_target_pairs={{0,24},{4,28},{8,0},{12,4},{16,8},{20,12},{24,16},{28,20},{1,25},{... | collective-permute-start | bytes 196616 | tf_op jit(solution)/shard_map/ppermute | solution.py:253
  112.8 3.9 %collective-permute-done.40.rest_3_ = bf16[256,128]{1,0:T(8,128)(2,1)S(1)} collective-permute-done((bf16[256,128]{1,0:T(8,128)(2,1)S(1)}, bf16[256,128]{1,0:T(8,128)(2,1)S(1)}, u32[]{:S(2)}, u32[]{:S(2)}) %collective-permute-start.40) | collective-permute-done | bytes 65568 | tf_op jit(solution)/shard_map/ppermute | solution.py:253
  117.1 1.1 collective-permute-done.43.rest_6_
  118.3 0.9 shard_map.121
  (65 shorter events, 4.5 us)
Async XLA Ops:
  0.6 1.0 copy-start
  1.7 0.8 copy-start.4
  2.5 0.7 copy-start.9
  3.2 0.7 copy-start.11
  3.9 99.1 %copy-start.8 = (f32[1024]{0:T(1024)S(1)}, f32[1024]{0:T(1024)}, u32[]{:S(2)}) copy-start(f32[1024]{0:T(1024)} %param.17) | copy-start | bytes 12292
  5.6 8.1 %collective-permute-start = (bf16[144,128]{1,0:T(8,128)(2,1)S(1)}, bf16[144,128]{1,0:T(8,128)(2,1)S(1)}, u32[]{:S(2)}, u32[]{:S(2)}) collective-permute-start(bf16[144,128]{1,0:T(8,128)(2,1)S(1)} %get-tuple-element.51), channel_id=1, source_target_pairs={{0,4},{4,8},{8,12},{12,16},{16,20},{20,24},{24,28},{28,0},{1,5},{5... | collective-permute-start | bytes 110600 | tf_op jit(solution)/shard_map/ppermute | solution.py:253
  6.1 9.0 %collective-permute-start.1 = (bf16[144,128]{1,0:T(8,128)(2,1)S(1)}, bf16[144,128]{1,0:T(8,128)(2,1)S(1)}, u32[]{:S(2)}, u32[]{:S(2)}) collective-permute-start(bf16[144,128]{1,0:T(8,128)(2,1)S(1)} %get-tuple-element.52), channel_id=1, source_target_pairs={{0,8},{4,12},{8,16},{12,20},{16,24},{20,28},{24,0},{28,4},{1,9},{5... | collective-permute-start | bytes 110600 | tf_op jit(solution)/shard_map/ppermute | solution.py:253
  8.8 7.7 %collective-permute-start.2 = (bf16[144,128]{1,0:T(8,128)(2,1)S(1)}, bf16[144,128]{1,0:T(8,128)(2,1)S(1)}, u32[]{:S(2)}, u32[]{:S(2)}) collective-permute-start(bf16[144,128]{1,0:T(8,128)(2,1)S(1)} %get-tuple-element.53), channel_id=1, source_target_pairs={{0,12},{4,16},{8,20},{12,24},{16,28},{20,0},{24,4},{28,8},{1,13},{... | collective-permute-start | bytes 110600 | tf_op jit(solution)/shard_map/ppermute | solution.py:253
  11.3 5.4 %collective-permute-start.3 = (bf16[144,128]{1,0:T(8,128)(2,1)S(1)}, bf16[144,128]{1,0:T(8,128)(2,1)S(1)}, u32[]{:S(2)}, u32[]{:S(2)}) collective-permute-start(bf16[144,128]{1,0:T(8,128)(2,1)S(1)} %get-tuple-element.54), channel_id=1, source_target_pairs={{0,16},{4,20},{8,24},{12,28},{16,0},{20,4},{24,8},{28,12},{1,17},{... | collective-permute-start | bytes 110600 | tf_op jit(solution)/shard_map/ppermute | solution.py:253
  12.5 4.1 %collective-permute-start.4 = (bf16[144,128]{1,0:T(8,128)(2,1)S(1)}, bf16[144,128]{1,0:T(8,128)(2,1)S(1)}, u32[]{:S(2)}, u32[]{:S(2)}) collective-permute-start(bf16[144,128]{1,0:T(8,128)(2,1)S(1)} %get-tuple-element.55), channel_id=1, source_target_pairs={{0,20},{4,24},{8,28},{12,0},{16,4},{20,8},{24,12},{28,16},{1,21},{... | collective-permute-start | bytes 110600 | tf_op jit(solution)/shard_map/ppermute | solution.py:253
  13.7 4.2 %collective-permute-start.5 = (bf16[144,128]{1,0:T(8,128)(2,1)S(1)}, bf16[144,128]{1,0:T(8,128)(2,1)S(1)}, u32[]{:S(2)}, u32[]{:S(2)}) collective-permute-start(bf16[144,128]{1,0:T(8,128)(2,1)S(1)} %get-tuple-element.56), channel_id=1, source_target_pairs={{0,24},{4,28},{8,0},{12,4},{16,8},{20,12},{24,16},{28,20},{1,25},{... | collective-permute-start | bytes 110600 | tf_op jit(solution)/shard_map/ppermute | solution.py:253
  15.1 3.0 %collective-permute-start.6 = (bf16[144,128]{1,0:T(8,128)(2,1)S(1)}, bf16[144,128]{1,0:T(8,128)(2,1)S(1)}, u32[]{:S(2)}, u32[]{:S(2)}) collective-permute-start(bf16[144,128]{1,0:T(8,128)(2,1)S(1)} %get-tuple-element.57), channel_id=1, source_target_pairs={{0,28},{4,0},{8,4},{12,8},{16,12},{20,16},{24,20},{28,24},{1,29},{... | collective-permute-start | bytes 110600 | tf_op jit(solution)/shard_map/ppermute | solution.py:253
  18.8 7.3 %collective-permute-start.7 = (bf16[128,128]{1,0:T(8,128)(2,1)S(1)}, bf16[128,128]{1,0:T(8,128)(2,1)S(1)}, u32[]{:S(2)}, u32[]{:S(2)}) collective-permute-start(bf16[128,128]{1,0:T(8,128)(2,1)S(1)} %get-tuple-element.59), channel_id=1, source_target_pairs={{0,4},{4,8},{8,12},{12,16},{16,20},{20,24},{24,28},{28,0},{1,5},{5... | collective-permute-start | bytes 98312 | tf_op jit(solution)/shard_map/ppermute | solution.py:253
  19.6 6.9 %collective-permute-start.8 = (bf16[128,128]{1,0:T(8,128)(2,1)S(1)}, bf16[128,128]{1,0:T(8,128)(2,1)S(1)}, u32[]{:S(2)}, u32[]{:S(2)}) collective-permute-start(bf16[128,128]{1,0:T(8,128)(2,1)S(1)} %get-tuple-element.60), channel_id=1, source_target_pairs={{0,8},{4,12},{8,16},{12,20},{16,24},{20,28},{24,0},{28,4},{1,9},{5... | collective-permute-start | bytes 98312 | tf_op jit(solution)/shard_map/ppermute | solution.py:253
  20.1 9.9 %collective-permute-start.9 = (bf16[128,128]{1,0:T(8,128)(2,1)S(1)}, bf16[128,128]{1,0:T(8,128)(2,1)S(1)}, u32[]{:S(2)}, u32[]{:S(2)}) collective-permute-start(bf16[128,128]{1,0:T(8,128)(2,1)S(1)} %get-tuple-element.61), channel_id=1, source_target_pairs={{0,12},{4,16},{8,20},{12,24},{16,28},{20,0},{24,4},{28,8},{1,13},{... | collective-permute-start | bytes 98312 | tf_op jit(solution)/shard_map/ppermute | solution.py:253
  22.3 8.7 %collective-permute-start.10 = (bf16[128,128]{1,0:T(8,128)(2,1)S(1)}, bf16[128,128]{1,0:T(8,128)(2,1)S(1)}, u32[]{:S(2)}, u32[]{:S(2)}) collective-permute-start(bf16[128,128]{1,0:T(8,128)(2,1)S(1)} %get-tuple-element.62), channel_id=1, source_target_pairs={{0,16},{4,20},{8,24},{12,28},{16,0},{20,4},{24,8},{28,12},{1,17},{... | collective-permute-start | bytes 98312 | tf_op jit(solution)/shard_map/ppermute | solution.py:253
  23.7 1.0 copy-start.2
  24.7 1.0 copy-start.3
  26.1 56.4 %collective-permute-start.17 = (bf16[512,128]{1,0:T(8,128)(2,1)S(1)}, bf16[512,128]{1,0:T(8,128)(2,1)S(1)}, u32[]{:S(2)}, u32[]{:S(2)}) collective-permute-start(bf16[512,128]{1,0:T(8,128)(2,1)S(1)} %get-tuple-element.70), channel_id=1, source_target_pairs={{0,4},{4,8},{8,12},{12,16},{16,20},{20,24},{24,28},{28,0},{1,5},{5... | collective-permute-start | bytes 393224 | tf_op jit(solution)/shard_map/ppermute | solution.py:253
  26.1 56.4 %collective-permute-start.18 = (bf16[512,128]{1,0:T(8,128)(2,1)S(1)}, bf16[512,128]{1,0:T(8,128)(2,1)S(1)}, u32[]{:S(2)}, u32[]{:S(2)}) collective-permute-start(bf16[512,128]{1,0:T(8,128)(2,1)S(1)} %get-tuple-element.71), channel_id=1, source_target_pairs={{0,8},{4,12},{8,16},{12,20},{16,24},{20,28},{24,0},{28,4},{1,9},{5... | collective-permute-start | bytes 393224 | tf_op jit(solution)/shard_map/ppermute | solution.py:253
  26.6 13.2 %collective-permute-start.11 = (bf16[128,128]{1,0:T(8,128)(2,1)S(1)}, bf16[128,128]{1,0:T(8,128)(2,1)S(1)}, u32[]{:S(2)}, u32[]{:S(2)}) collective-permute-start(bf16[128,128]{1,0:T(8,128)(2,1)S(1)} %get-tuple-element.63), channel_id=1, source_target_pairs={{0,20},{4,24},{8,28},{12,0},{16,4},{20,8},{24,12},{28,16},{1,21},{... | collective-permute-start | bytes 98312 | tf_op jit(solution)/shard_map/ppermute | solution.py:253
  29.9 9.8 %collective-permute-start.12 = (bf16[128,128]{1,0:T(8,128)(2,1)S(1)}, bf16[128,128]{1,0:T(8,128)(2,1)S(1)}, u32[]{:S(2)}, u32[]{:S(2)}) collective-permute-start(bf16[128,128]{1,0:T(8,128)(2,1)S(1)} %get-tuple-element.64), channel_id=1, source_target_pairs={{0,24},{4,28},{8,0},{12,4},{16,8},{20,12},{24,16},{28,20},{1,25},{... | collective-permute-start | bytes 98312 | tf_op jit(solution)/shard_map/ppermute | solution.py:253
  31.0 8.8 %collective-permute-start.13 = (bf16[128,128]{1,0:T(8,128)(2,1)S(1)}, bf16[128,128]{1,0:T(8,128)(2,1)S(1)}, u32[]{:S(2)}, u32[]{:S(2)}) collective-permute-start(bf16[128,128]{1,0:T(8,128)(2,1)S(1)} %get-tuple-element.65), channel_id=1, source_target_pairs={{0,28},{4,0},{8,4},{12,8},{16,12},{20,16},{24,20},{28,24},{1,29},{... | collective-permute-start | bytes 98312 | tf_op jit(solution)/shard_map/ppermute | solution.py:253
  31.5 1.0 copy-start.1
  32.5 0.8 copy-start.5
  33.4 0.8 copy-start.6
  34.2 0.7 copy-start.10
  34.9 0.7 copy-start.12
  35.6 1.0 copy-start.13
  36.6 0.7 copy-start.14
  40.9 4.6 %collective-permute-start.14 = (f32[8,256]{1,0:T(8,128)S(1)}, f32[8,256]{1,0:T(8,128)S(1)}, u32[]{:S(2)}, u32[]{:S(2)}) collective-permute-start(f32[8,256]{1,0:T(8,128)S(1)} %get-tuple-element.67.rest_0_), channel_id=1, source_target_pairs={{0,1},{1,2},{2,3},{3,0},{4,5},{5,6},{6,7},{7,4},{8,9},{9,10},{10,1... | collective-permute-start | bytes 24584 | tf_op jit(solution)/shard_map/ppermute | solution.py:253
  42.4 3.7 %collective-permute-start.15 = (f32[8,256]{1,0:T(8,128)S(1)}, f32[8,256]{1,0:T(8,128)S(1)}, u32[]{:S(2)}, u32[]{:S(2)}) collective-permute-start(f32[8,256]{1,0:T(8,128)S(1)} %get-tuple-element.67.rest_0_), channel_id=1, source_target_pairs={{0,2},{1,3},{2,0},{3,1},{4,6},{5,7},{6,4},{7,5},{8,10},{9,11},{10,... | collective-permute-start | bytes 24584 | tf_op jit(solution)/shard_map/ppermute | solution.py:253
  43.9 3.7 %collective-permute-start.16 = (f32[8,256]{1,0:T(8,128)S(1)}, f32[8,256]{1,0:T(8,128)S(1)}, u32[]{:S(2)}, u32[]{:S(2)}) collective-permute-start(f32[8,256]{1,0:T(8,128)S(1)} %get-tuple-element.67.rest_0_), channel_id=1, source_target_pairs={{0,3},{1,0},{2,1},{3,2},{4,7},{5,4},{6,5},{7,6},{8,11},{9,8},{10,9... | collective-permute-start | bytes 24584 | tf_op jit(solution)/shard_map/ppermute | solution.py:253
  45.5 38.2 %collective-permute-start.19 = (bf16[512,128]{1,0:T(8,128)(2,1)S(1)}, bf16[512,128]{1,0:T(8,128)(2,1)S(1)}, u32[]{:S(2)}, u32[]{:S(2)}) collective-permute-start(bf16[512,128]{1,0:T(8,128)(2,1)S(1)} %get-tuple-element.72), channel_id=1, source_target_pairs={{0,12},{4,16},{8,20},{12,24},{16,28},{20,0},{24,4},{28,8},{1,13},{... | collective-permute-start | bytes 393224 | tf_op jit(solution)/shard_map/ppermute | solution.py:253
  46.1 37.6 %collective-permute-start.20 = (bf16[512,128]{1,0:T(8,128)(2,1)S(1)}, bf16[512,128]{1,0:T(8,128)(2,1)S(1)}, u32[]{:S(2)}, u32[]{:S(2)}) collective-permute-start(bf16[512,128]{1,0:T(8,128)(2,1)S(1)} %get-tuple-element.73), channel_id=1, source_target_pairs={{0,16},{4,20},{8,24},{12,28},{16,0},{20,4},{24,8},{28,12},{1,17},{... | collective-permute-start | bytes 393224 | tf_op jit(solution)/shard_map/ppermute | solution.py:253
  47.6 0.7 copy-start.7
  49.3 6.0 %collective-permute-start.31 = (f32[8,256]{1,0:T(8,128)S(1)}, f32[8,256]{1,0:T(8,128)S(1)}, u32[]{:S(2)}, u32[]{:S(2)}) collective-permute-start(f32[8,256]{1,0:T(8,128)S(1)} %get-tuple-element.85.rest_8_), channel_id=1, source_target_pairs={{0,4},{4,8},{8,12},{12,16},{16,20},{20,24},{24,28},{28,0},{1,5},{5... | collective-permute-start | bytes 24584 | tf_op jit(solution)/shard_map/ppermute | solution.py:253
  55.3 5.4 %collective-permute-start.32 = (f32[8,256]{1,0:T(8,128)S(1)}, f32[8,256]{1,0:T(8,128)S(1)}, u32[]{:S(2)}, u32[]{:S(2)}) collective-permute-start(f32[8,256]{1,0:T(8,128)S(1)} %get-tuple-element.85.rest_8_), channel_id=1, source_target_pairs={{0,8},{4,12},{8,16},{12,20},{16,24},{20,28},{24,0},{28,4},{1,9},{5... | collective-permute-start | bytes 24584 | tf_op jit(solution)/shard_map/ppermute | solution.py:253
  60.8 4.0 %collective-permute-start.33 = (f32[8,256]{1,0:T(8,128)S(1)}, f32[8,256]{1,0:T(8,128)S(1)}, u32[]{:S(2)}, u32[]{:S(2)}) collective-permute-start(f32[8,256]{1,0:T(8,128)S(1)} %get-tuple-element.85.rest_8_), channel_id=1, source_target_pairs={{0,12},{4,16},{8,20},{12,24},{16,28},{20,0},{24,4},{28,8},{1,13},{... | collective-permute-start | bytes 24584 | tf_op jit(solution)/shard_map/ppermute | solution.py:253
  64.7 4.5 %collective-permute-start.34 = (f32[8,256]{1,0:T(8,128)S(1)}, f32[8,256]{1,0:T(8,128)S(1)}, u32[]{:S(2)}, u32[]{:S(2)}) collective-permute-start(f32[8,256]{1,0:T(8,128)S(1)} %get-tuple-element.85.rest_8_), channel_id=1, source_target_pairs={{0,16},{4,20},{8,24},{12,28},{16,0},{20,4},{24,8},{28,12},{1,17},{... | collective-permute-start | bytes 24584 | tf_op jit(solution)/shard_map/ppermute | solution.py:253
  69.3 3.1 %collective-permute-start.35 = (f32[8,256]{1,0:T(8,128)S(1)}, f32[8,256]{1,0:T(8,128)S(1)}, u32[]{:S(2)}, u32[]{:S(2)}) collective-permute-start(f32[8,256]{1,0:T(8,128)S(1)} %get-tuple-element.85.rest_8_), channel_id=1, source_target_pairs={{0,20},{4,24},{8,28},{12,0},{16,4},{20,8},{24,12},{28,16},{1,21},{... | collective-permute-start | bytes 24584 | tf_op jit(solution)/shard_map/ppermute | solution.py:253
  72.4 4.4 %collective-permute-start.36 = (f32[8,256]{1,0:T(8,128)S(1)}, f32[8,256]{1,0:T(8,128)S(1)}, u32[]{:S(2)}, u32[]{:S(2)}) collective-permute-start(f32[8,256]{1,0:T(8,128)S(1)} %get-tuple-element.85.rest_8_), channel_id=1, source_target_pairs={{0,24},{4,28},{8,0},{12,4},{16,8},{20,12},{24,16},{28,20},{1,25},{... | collective-permute-start | bytes 24584 | tf_op jit(solution)/shard_map/ppermute | solution.py:253
  76.8 2.0 %collective-permute-start.37 = (f32[8,256]{1,0:T(8,128)S(1)}, f32[8,256]{1,0:T(8,128)S(1)}, u32[]{:S(2)}, u32[]{:S(2)}) collective-permute-start(f32[8,256]{1,0:T(8,128)S(1)} %get-tuple-element.85.rest_8_), channel_id=1, source_target_pairs={{0,28},{4,0},{8,4},{12,8},{16,12},{20,16},{24,20},{28,24},{1,29},{... | collective-permute-start | bytes 24584 | tf_op jit(solution)/shard_map/ppermute | solution.py:253
  78.8 7.6 %collective-permute-start.21 = (bf16[512,128]{1,0:T(8,128)(2,1)S(1)}, bf16[512,128]{1,0:T(8,128)(2,1)S(1)}, u32[]{:S(2)}, u32[]{:S(2)}) collective-permute-start(bf16[512,128]{1,0:T(8,128)(2,1)S(1)} %get-tuple-element.74), channel_id=1, source_target_pairs={{0,20},{4,24},{8,28},{12,0},{16,4},{20,8},{24,12},{28,16},{1,21},{... | collective-permute-start | bytes 393224 | tf_op jit(solution)/shard_map/ppermute | solution.py:253
  82.5 6.7 %collective-permute-start.22 = (bf16[512,128]{1,0:T(8,128)(2,1)S(1)}, bf16[512,128]{1,0:T(8,128)(2,1)S(1)}, u32[]{:S(2)}, u32[]{:S(2)}) collective-permute-start(bf16[512,128]{1,0:T(8,128)(2,1)S(1)} %get-tuple-element.75), channel_id=1, source_target_pairs={{0,24},{4,28},{8,0},{12,4},{16,8},{20,12},{24,16},{28,20},{1,25},{... | collective-permute-start | bytes 393224 | tf_op jit(solution)/shard_map/ppermute | solution.py:253
  82.5 14.9 %collective-permute-start.23 = (bf16[512,128]{1,0:T(8,128)(2,1)S(1)}, bf16[512,128]{1,0:T(8,128)(2,1)S(1)}, u32[]{:S(2)}, u32[]{:S(2)}) collective-permute-start(bf16[512,128]{1,0:T(8,128)(2,1)S(1)} %get-tuple-element.76), channel_id=1, source_target_pairs={{0,28},{4,0},{8,4},{12,8},{16,12},{20,16},{24,20},{28,24},{1,29},{... | collective-permute-start | bytes 393224 | tf_op jit(solution)/shard_map/ppermute | solution.py:253
  83.7 13.8 %collective-permute-start.24 = (bf16[256,128]{1,0:T(8,128)(2,1)S(1)}, bf16[256,128]{1,0:T(8,128)(2,1)S(1)}, u32[]{:S(2)}, u32[]{:S(2)}) collective-permute-start(bf16[256,128]{1,0:T(8,128)(2,1)S(1)} %get-tuple-element.78), channel_id=1, source_target_pairs={{0,4},{4,8},{8,12},{12,16},{16,20},{20,24},{24,28},{28,0},{1,5},{5... | collective-permute-start | bytes 196616 | tf_op jit(solution)/shard_map/ppermute | solution.py:253
  83.7 15.8 %collective-permute-start.25 = (bf16[256,128]{1,0:T(8,128)(2,1)S(1)}, bf16[256,128]{1,0:T(8,128)(2,1)S(1)}, u32[]{:S(2)}, u32[]{:S(2)}) collective-permute-start(bf16[256,128]{1,0:T(8,128)(2,1)S(1)} %get-tuple-element.79), channel_id=1, source_target_pairs={{0,8},{4,12},{8,16},{12,20},{16,24},{20,28},{24,0},{28,4},{1,9},{5... | collective-permute-start | bytes 196616 | tf_op jit(solution)/shard_map/ppermute | solution.py:253
  86.4 16.3 %collective-permute-start.26 = (bf16[256,128]{1,0:T(8,128)(2,1)S(1)}, bf16[256,128]{1,0:T(8,128)(2,1)S(1)}, u32[]{:S(2)}, u32[]{:S(2)}) collective-permute-start(bf16[256,128]{1,0:T(8,128)(2,1)S(1)} %get-tuple-element.80), channel_id=1, source_target_pairs={{0,12},{4,16},{8,20},{12,24},{16,28},{20,0},{24,4},{28,8},{1,13},{... | collective-permute-start | bytes 196616 | tf_op jit(solution)/shard_map/ppermute | solution.py:253
  89.2 13.5 %collective-permute-start.27 = (bf16[256,128]{1,0:T(8,128)(2,1)S(1)}, bf16[256,128]{1,0:T(8,128)(2,1)S(1)}, u32[]{:S(2)}, u32[]{:S(2)}) collective-permute-start(bf16[256,128]{1,0:T(8,128)(2,1)S(1)} %get-tuple-element.81), channel_id=1, source_target_pairs={{0,16},{4,20},{8,24},{12,28},{16,0},{20,4},{24,8},{28,12},{1,17},{... | collective-permute-start | bytes 196616 | tf_op jit(solution)/shard_map/ppermute | solution.py:253
  97.4 5.5 %collective-permute-start.28 = (bf16[256,128]{1,0:T(8,128)(2,1)S(1)}, bf16[256,128]{1,0:T(8,128)(2,1)S(1)}, u32[]{:S(2)}, u32[]{:S(2)}) collective-permute-start(bf16[256,128]{1,0:T(8,128)(2,1)S(1)} %get-tuple-element.82), channel_id=1, source_target_pairs={{0,20},{4,24},{8,28},{12,0},{16,4},{20,8},{24,12},{28,16},{1,21},{... | collective-permute-start | bytes 196616 | tf_op jit(solution)/shard_map/ppermute | solution.py:253
  97.4 5.6 %collective-permute-start.29 = (bf16[256,128]{1,0:T(8,128)(2,1)S(1)}, bf16[256,128]{1,0:T(8,128)(2,1)S(1)}, u32[]{:S(2)}, u32[]{:S(2)}) collective-permute-start(bf16[256,128]{1,0:T(8,128)(2,1)S(1)} %get-tuple-element.83), channel_id=1, source_target_pairs={{0,24},{4,28},{8,0},{12,4},{16,8},{20,12},{24,16},{28,20},{1,25},{... | collective-permute-start | bytes 196616 | tf_op jit(solution)/shard_map/ppermute | solution.py:253
  99.5 3.5 %collective-permute-start.30 = (bf16[256,128]{1,0:T(8,128)(2,1)S(1)}, bf16[256,128]{1,0:T(8,128)(2,1)S(1)}, u32[]{:S(2)}, u32[]{:S(2)}) collective-permute-start(bf16[256,128]{1,0:T(8,128)(2,1)S(1)} %get-tuple-element.84), channel_id=1, source_target_pairs={{0,28},{4,0},{8,4},{12,8},{16,12},{20,16},{24,20},{28,24},{1,29},{... | collective-permute-start | bytes 196616 | tf_op jit(solution)/shard_map/ppermute | solution.py:253
  104.8 6.2 %collective-permute-start.38 = (bf16[256,128]{1,0:T(8,128)(2,1)S(1)}, bf16[256,128]{1,0:T(8,128)(2,1)S(1)}, u32[]{:S(2)}, u32[]{:S(2)}) collective-permute-start(bf16[256,128]{1,0:T(8,128)(2,1)S(1)} %get-tuple-element.87), channel_id=1, source_target_pairs={{0,4},{4,8},{8,12},{12,16},{16,20},{20,24},{24,28},{28,0},{1,5},{5... | collective-permute-start | bytes 196616 | tf_op jit(solution)/shard_map/ppermute | solution.py:253
  106.0 6.8 %collective-permute-start.39 = (bf16[256,128]{1,0:T(8,128)(2,1)S(1)}, bf16[256,128]{1,0:T(8,128)(2,1)S(1)}, u32[]{:S(2)}, u32[]{:S(2)}) collective-permute-start(bf16[256,128]{1,0:T(8,128)(2,1)S(1)} %get-tuple-element.88), channel_id=1, source_target_pairs={{0,8},{4,12},{8,16},{12,20},{16,24},{20,28},{24,0},{28,4},{1,9},{5... | collective-permute-start | bytes 196616 | tf_op jit(solution)/shard_map/ppermute | solution.py:253
  106.6 10.1 %collective-permute-start.40 = (bf16[256,128]{1,0:T(8,128)(2,1)S(1)}, bf16[256,128]{1,0:T(8,128)(2,1)S(1)}, u32[]{:S(2)}, u32[]{:S(2)}) collective-permute-start(bf16[256,128]{1,0:T(8,128)(2,1)S(1)} %get-tuple-element.89), channel_id=1, source_target_pairs={{0,12},{4,16},{8,20},{12,24},{16,28},{20,0},{24,4},{28,8},{1,13},{... | collective-permute-start | bytes 196616 | tf_op jit(solution)/shard_map/ppermute | solution.py:253
  108.1 9.0 %collective-permute-start.41 = (bf16[256,128]{1,0:T(8,128)(2,1)S(1)}, bf16[256,128]{1,0:T(8,128)(2,1)S(1)}, u32[]{:S(2)}, u32[]{:S(2)}) collective-permute-start(bf16[256,128]{1,0:T(8,128)(2,1)S(1)} %get-tuple-element.90), channel_id=1, source_target_pairs={{0,16},{4,20},{8,24},{12,28},{16,0},{20,4},{24,8},{28,12},{1,17},{... | collective-permute-start | bytes 196616 | tf_op jit(solution)/shard_map/ppermute | solution.py:253
  109.9 7.2 %collective-permute-start.42 = (bf16[256,128]{1,0:T(8,128)(2,1)S(1)}, bf16[256,128]{1,0:T(8,128)(2,1)S(1)}, u32[]{:S(2)}, u32[]{:S(2)}) collective-permute-start(bf16[256,128]{1,0:T(8,128)(2,1)S(1)} %get-tuple-element.91), channel_id=1, source_target_pairs={{0,20},{4,24},{8,28},{12,0},{16,4},{20,8},{24,12},{28,16},{1,21},{... | collective-permute-start | bytes 196616 | tf_op jit(solution)/shard_map/ppermute | solution.py:253
  111.0 7.2 %collective-permute-start.43 = (bf16[256,128]{1,0:T(8,128)(2,1)S(1)}, bf16[256,128]{1,0:T(8,128)(2,1)S(1)}, u32[]{:S(2)}, u32[]{:S(2)}) collective-permute-start(bf16[256,128]{1,0:T(8,128)(2,1)S(1)} %get-tuple-element.92), channel_id=1, source_target_pairs={{0,24},{4,28},{8,0},{12,4},{16,8},{20,12},{24,16},{28,20},{1,25},{... | collective-permute-start | bytes 196616 | tf_op jit(solution)/shard_map/ppermute | solution.py:253
  112.8 5.4 %collective-permute-start.44 = (bf16[256,128]{1,0:T(8,128)(2,1)S(1)}, bf16[256,128]{1,0:T(8,128)(2,1)S(1)}, u32[]{:S(2)}, u32[]{:S(2)}) collective-permute-start(bf16[256,128]{1,0:T(8,128)(2,1)S(1)} %get-tuple-element.93), channel_id=1, source_target_pairs={{0,28},{4,0},{8,4},{12,8},{16,12},{20,16},{24,20},{28,24},{1,29},{... | collective-permute-start | bytes 196616 | tf_op jit(solution)/shard_map/ppermute | solution.py:253

commit v2 on v0

--- a/solution.py
+++ b/solution.py
@@ -4,6 +4,8 @@
 import jax
 import jax.numpy as jnp
 from jax import lax
+from jax.experimental import pallas as pl
+from jax.experimental.pallas import tpu as pltpu
 from jax.sharding import PartitionSpec as P
 
 HD = 128
@@ -13,6 +15,447 @@
 
 HIGH = lax.Precision.HIGHEST
 NEG = -1e30
+LOG2E = 1.4426950408889634
+MIB = 1 << 20
+
+
+VMEM = pl.BlockSpec(memory_space=pltpu.VMEM)
+SMEM = pl.BlockSpec(memory_space=pltpu.SMEM)
+HBM = pl.BlockSpec(memory_space=pltpu.HBM)
+ANY = pl.BlockSpec(memory_space=pl.ANY)
+CHIPS = 4
+WIDE = 2 * HD
+PARTS = 16
+
+
+def call(body, outs, args, spaces, scratch=(), flops=0, moved=0, exps=0, limit=16 * MIB):
+    kinds = {"s": SMEM, "h": HBM, "a": ANY, "v": VMEM}
+    spaces = spaces + "v" * (len(args) - len(spaces))
+    return pl.pallas_call(
+        body,
+        out_shape=outs,
+        in_specs=[kinds[space] for space in spaces],
+        out_specs=jax.tree.map(lambda _: VMEM, outs),
+        scratch_shapes=list(scratch),
+        compiler_params=pltpu.CompilerParams(vmem_limit_bytes=limit),
+        cost_estimate=pl.CostEstimate(flops=0, bytes_accessed=0, transcendentals=0),
+    )(
+        *(
+            pltpu.with_memory_space_constraint(arg, pltpu.HBM) if space == "h" else arg
+            for arg, space in zip(args, spaces)
+        )
+    )
+
+
+def nt(a, b):
+    return lax.dot_general(a, b, (((1,), (1,)), ((), ())), preferred_element_type=jnp.float32)
+
+
+def nn(a, b):
+    return jnp.dot(a, b, preferred_element_type=jnp.float32)
+
+
+def step_counts(codes):
+    rows = codes.shape[1]
+    r = lax.broadcasted_iota(jnp.int32, (rows, rows), 0)
+    s = lax.broadcasted_iota(jnp.int32, (rows, rows), 1)
+    upper = (r <= s).astype(jnp.float32).astype(jnp.bfloat16)
+    lower = (s <= r).astype(jnp.float32).astype(jnp.bfloat16)
+    high = lax.shift_right_logical(codes, 7).astype(jnp.float32).astype(jnp.bfloat16)
+    low = (codes & 127).astype(jnp.float32).astype(jnp.bfloat16)
+    return (
+        128.0 * nn(high, upper) + nn(low, upper),
+        128.0 * nt(lower, high) + nt(lower, low),
+    )
+
+
+def left_lanes(rows):
+    return lax.broadcasted_iota(jnp.int32, (rows, HD), 1) < CHANNELS_PER_HD
+
+
+def chip_of(me):
+    return lax.shift_right_logical(me, 1)
+
+
+def around(chip, by):
+    return (chip + by) & (CHIPS - 1)
+
+
+def block_of(index, size):
+    return pl.ds(pl.multiple_of(index * size, size), size)
+
+
+def as_parts(total):
+    total = jnp.broadcast_to(total, (PARTS, total.shape[1])).astype(jnp.int32)
+    part = lax.broadcasted_iota(jnp.int32, total.shape, 0)
+    high = lax.shift_right_logical(total, 16)
+    middle = lax.shift_right_logical(total, 8) & 255
+    chosen = jnp.where(
+        part == 0, high, jnp.where(part == 1, middle, jnp.where(part == 2, total & 255, 0))
+    )
+    return chosen.astype(jnp.float32).astype(jnp.bfloat16)
+
+
+def opened(rows):
+    rows = rows.astype(jnp.float32)
+    total = 65536.0 * rows[HD : HD + 1] + 256.0 * rows[HD + 1 : HD + 2] + rows[HD + 2 : HD + 3]
+    return rows[:HD], total
+
+
+def followed(first, second, slope):
+    return jnp.exp2(second[1] * slope) * first[0] + second[0], first[1] + second[1]
+
+
+def first_kernel(
+    me_ref, rates_ref, skip_ref, q_hbm, k_hbm, codes_hbm, b_hbm, x_hbm, c_hbm, gate_hbm, gain_hbm, *rest
+):
+    qk, state_ref, slope_ref, skips_ref = rest[:CHIPS], *rest[CHIPS : CHIPS + 3]
+    codes_ref, b_ref, x_ref, c_ref, gate_ref, gain_ref, sems = rest[CHIPS + 3 :]
+    rows = x_ref.shape[0]
+    chip = chip_of(me_ref[0])
+    pairs = [(codes_hbm, codes_ref), (b_hbm, b_ref), (x_hbm, x_ref)]
+    for d in range(CHIPS):
+        cols = block_of(around(chip, d), WIDE)
+        pairs.append((q_hbm.at[:, cols], qk[d].at[pl.ds(0, rows), :]))
+        pairs.append((k_hbm.at[:, cols], qk[d].at[pl.ds(rows, rows), :]))
+    pairs += [(c_hbm, c_ref), (gate_hbm, gate_ref), (gain_hbm, gain_ref)]
+    copies = [pltpu.make_async_copy(a, b, sems.at[i]) for i, (a, b) in enumerate(pairs)]
+    for copy in copies:
+        copy.start()
+    for pair in range(x_ref.shape[1] // HD):
+        cols = slice(pair * HD, (pair + 1) * HD)
+        left = left_lanes(8)
+        one, two = 2 * pair, 2 * pair + 1
+        slope_ref[:, cols] = jnp.where(left, rates_ref[one], rates_ref[two]) * -LOG2E
+        skips_ref[:, cols] = jnp.where(left, skip_ref[one], skip_ref[two])
+    copies[0].wait()
+    _, counts = step_counts(codes_ref[...])
+    copies[1].wait()
+    b_turned = b_ref[...].astype(jnp.float32).T.astype(jnp.bfloat16)
+    left = left_lanes(rows)
+    copies[2].wait()
+    for pair in range(x_ref.shape[1] // HD):
+        cols = slice(pair * HD, (pair + 1) * HD)
+        column = jnp.where(left, counts[:, 2 * pair : 2 * pair + 1], counts[:, 2 * pair + 1 : 2 * pair + 2])
+        total = column[rows - 1 : rows, :]
+        weight = jnp.exp2((total - column) * slope_ref[0:1, cols])
+        x = (x_ref[:, cols].astype(jnp.float32) * weight).astype(jnp.bfloat16)
+        state_ref[pl.ds(0, HD), cols] = nn(b_turned, x).astype(jnp.bfloat16)
+        state_ref[pl.ds(HD, PARTS), cols] = as_parts(total)
+    for copy in copies[3:]:
+        copy.wait()
+
+
+def chip_kernel(me_ref, slope_ref, own_ref, other_ref, out_ref):
+    core = me_ref[0] & 1
+    half = own_ref.shape[1] // 2
+    cols = block_of(core, half)
+    own, other = own_ref[:, cols], other_ref[:, cols]
+    first = opened(jnp.where(core == 0, own, other))
+    second = opened(jnp.where(core == 0, other, own))
+    state, total = followed(first, second, slope_ref[0:1, cols])
+    out_ref[pl.ds(0, HD), :] = state.astype(jnp.bfloat16)
+    out_ref[pl.ds(HD, PARTS), :] = as_parts(total)
+
+
+def two_chips_kernel(me_ref, after_ref, slope_ref, own_ref, other_ref, out_ref):
+    me = me_ref[0]
+    odd = chip_of(me) & 1
+    own, other = own_ref[...], other_ref[...]
+    first = opened(jnp.where(odd == 0, own, other))
+    second = opened(jnp.where(odd == 0, other, own))
+    state, total = followed(first, second, slope_ref[0:1, block_of(me & 1, own.shape[1])])
+    out_ref[pl.ds(0, HD), :] = state.astype(jnp.bfloat16)
+    out_ref[pl.ds(HD, PARTS), :] = as_parts(total)
+
+
+def ahead_kernel(me_ref, slope_ref, other_ref, far_ref, out_ref):
+    me = me_ref[0]
+    odd = chip_of(me) & 1
+    near, total = opened(other_ref[...])
+    near = jnp.where(odd == 1, near, 0.0)
+    total = jnp.where(odd == 1, total, 0.0)
+    far, _ = opened(far_ref[...])
+    slope = slope_ref[0:1, block_of(me & 1, near.shape[1])]
+    out_ref[...] = (jnp.exp2(total * slope) * far + near).astype(jnp.bfloat16)
+
+
+def within_kernel(slope_ref, skips_ref, codes_ref, b_ref, x_ref, c_ref, gate_ref, own_ref, lead_ref):
+    rows = x_ref.shape[0]
+    across, down = step_counts(codes_ref[...])
+    t = lax.broadcasted_iota(jnp.int32, (rows, rows), 0)
+    s = lax.broadcasted_iota(jnp.int32, (rows, rows), 1)
+    match = jnp.where(s <= t, nt(c_ref[...], b_ref[...]), 0.0)
+    left = left_lanes(rows)
+    for pair in range(x_ref.shape[1] // HD):
+        cols = slice(pair * HD, (pair + 1) * HD)
+        x = x_ref[:, cols]
+        ys = []
+        leads = []
+        for h in (2 * pair, 2 * pair + 1):
+            slope = slope_ref[0:1, h * CHANNELS_PER_HD : h * CHANNELS_PER_HD + 1]
+            gap = jnp.maximum(down[:, h : h + 1] - across[h : h + 1, :], 0.0)
+            ys.append(nn((jnp.exp2(gap * slope) * match).astype(jnp.bfloat16), x))
+            leads.append(jnp.exp2(down[:, h : h + 1] * slope))
+        gate = gate_ref[:, cols].astype(jnp.float32)
+        gate = gate / (1.0 + jnp.exp(-gate))
+        given = jnp.where(left, ys[0], ys[1]) + skips_ref[0:1, cols] * x.astype(jnp.float32)
+        own_ref[:, cols] = given * gate
+        lead_ref[:, cols] = jnp.where(left, leads[0], leads[1]) * gate
+
+
+def gated_kernel(
+    me_ref, slope_ref, local_ref, ahead_ref, other_ref, own_ref, lead_ref, c_ref, gated_ref, squares_ref
+):
+    core = me_ref[0] & 1
+    c = c_ref[...]
+    ones = jnp.ones((8, HD), jnp.bfloat16)
+    squares = jnp.zeros(squares_ref.shape, jnp.float32)
+    half = ahead_ref.shape[1]
+    for at in range(0, 2 * half, HD):
+        cols, within = slice(at, at + HD), slice(at % half, at % half + HD)
+        state = jnp.where(core == at // half, ahead_ref[:, within], other_ref[:, within])
+        state = state.astype(jnp.float32)
+        later, _ = followed((state, 0.0), opened(local_ref[:, cols]), slope_ref[0:1, cols])
+        state = jnp.where(core == 1, later, state).astype(jnp.bfloat16)
+        gated = own_ref[:, cols] + lead_ref[:, cols] * nn(c, state)
+        gated_ref[:, cols] = gated
+        square = gated * gated
+        high = square.astype(jnp.bfloat16)
+        low = (square - high.astype(jnp.float32)).astype(jnp.bfloat16)
+        squares = squares + nt(ones, high) + nt(ones, low)
+    squares_ref[...] = squares
+
+
+def turned(row):
+    size = row.shape[1]
+    r = lax.broadcasted_iota(jnp.int32, (size, size), 0)
+    s = lax.broadcasted_iota(jnp.int32, (size, size), 1)
+    return jnp.sum(jnp.where(r == s, jnp.broadcast_to(row, (size, size)), 0.0), axis=1, keepdims=True)
+
+
+def norm_kernel(channels, me_ref, gain_ref, gated_ref, *rest):
+    squares, out_ref, parts = rest[: -1 - CHIPS], rest[-1 - CHIPS], rest[-CHIPS:]
+    chip = chip_of(me_ref[0])
+    total = squares[0][0:1, :]
+    for part in squares[1:]:
+        total = total + part[0:1, :]
+    column = turned(lax.rsqrt(total / channels + 1e-05))
+    for d in range(CHIPS):
+        cols = block_of(around(chip, d), WIDE)
+        out = (gated_ref[:, cols] * column * gain_ref[:, cols]).astype(jnp.bfloat16)
+        parts[d][...] = out
+        out_ref[:, cols] = out
+
+
+def keys_kernel(me_ref, after_ref, *rest):
+    chip = chip_of(me_ref[0])
+    rows = rest[0].shape[0] // 2
+    for d in range(CHIPS):
+        rest[CHIPS][block_of(around(chip, CHIPS - d), rows), :] = rest[d][pl.ds(rows, rows), :]
+
+
+def weights_kernel(me_ref, own_ref, other_ref, *rest):
+    ins, out_ref, q_ref = rest[:CHIPS], rest[CHIPS], rest[CHIPS + 1]
+    rows = ins[0].shape[0] // 2
+    me = me_ref[0]
+    chip, core = chip_of(me), me & 1
+    for d in range(CHIPS):
+        q_ref[block_of(around(chip, CHIPS - d), rows), :] = ins[d][pl.ds(0, rows), :]
+    scale = LOG2E / math.sqrt(HD)
+    half = rows // 2
+    for head in range(2):
+        lanes = slice(head * HD, (head + 1) * HD)
+        for i in range(2 * CHIPS):
+            seen = (i // 2) * rows
+            q = q_ref[pl.ds(i * half, half), lanes]
+            t = lax.broadcasted_iota(jnp.int32, (half, rows), 0) + (i % 2) * half
+            s = lax.broadcasted_iota(jnp.int32, (half, rows), 1)
+            blocks = []
+            for keys_ref, base, shown in (
+                (own_ref, 0, s <= t),
+                (other_ref, CHIPS * rows, s < core * rows),
+            ):
+                for at in range(0, seen, rows):
+                    blocks.append((base + at, nt(q, keys_ref[pl.ds(at, rows), lanes])))
+                last = nt(q, keys_ref[pl.ds(seen, rows), lanes])
+                blocks.append((base + seen, jnp.where(shown, last, NEG)))
+            top = functools.reduce(jnp.maximum, [block for _, block in blocks])
+            top = jnp.max(top, axis=1, keepdims=True) * scale
+            blocks = [(at, jnp.exp2(block * scale - top)) for at, block in blocks]
+            total = functools.reduce(jnp.add, [block for _, block in blocks])
+            inverse = 1.0 / jnp.sum(total, axis=1, keepdims=True)
+            for at, block in blocks:
+                out_ref[head, pl.ds(i * half, half), pl.ds(at, rows)] = (block * inverse).astype(
+                    jnp.bfloat16
+                )
+
+
+def values_kernel(me_ref, weights_ref, *rest):
+    own, other, outs = rest[:CHIPS], rest[CHIPS : 2 * CHIPS], rest[2 * CHIPS : 3 * CHIPS]
+    v_ref, o_ref = rest[3 * CHIPS :]
+    rows = own[0].shape[0]
+    chip = chip_of(me_ref[0])
+    for d in range(CHIPS):
+        back = around(chip, CHIPS - d)
+        v_ref[block_of(back, rows), :] = own[d][...]
+        v_ref[block_of(back + CHIPS, rows), :] = other[d][...]
+    for i in range(CHIPS):
+        at, seen = pl.ds(i * rows, rows), (i + 1) * rows
+        for head in range(2):
+            lanes = slice(head * HD, (head + 1) * HD)
+            total = 0.0
+            for base in (0, CHIPS * rows):
+                seen_at = pl.ds(base, seen)
+                total = total + nn(weights_ref[head, at, seen_at], v_ref[seen_at, lanes])
+            o_ref[at, lanes] = total.astype(jnp.bfloat16)
+    for d in range(CHIPS):
+        outs[d][...] = o_ref[block_of(around(chip, d), rows), :]
+
+
+def join_kernel(me_ref, *rest):
+    chip = chip_of(me_ref[0])
+    for d in range(CHIPS):
+        rest[CHIPS][:, block_of(around(chip, CHIPS - d), WIDE)] = rest[d][...]
+
+
+def shifted(part, d):
+    n = 2 * CHIPS
+    return lax.ppermute(part, "seq", [(i, (i + 2 * d) % n) for i in range(n)])
+
+
+def exchange(parts):
+    return [parts[0]] + [shifted(parts[d], d) for d in range(1, CHIPS)]
+
+
+def swapped(part):
+    return lax.ppermute(part, "seq", [(i, i ^ 1) for i in range(2 * CHIPS)])
+
+
+def two_heads_each(
+    mixer_input,
+    gate_input,
+    b_proj,
+    c_proj,
+    decay_codes,
+    decay_rates,
+    skip_gain,
+    norm_gain,
+    queries,
+    keys,
+):
+    n, m = lax.axis_size("seq"), lax.axis_size("head")
+    rows, width = mixer_input.shape
+    heads = decay_codes.shape[0]
+    me = lax.axis_index("seq").astype(jnp.int32).reshape(1)
+    shape = jax.ShapeDtypeStruct
+    bf16, f32 = jnp.bfloat16, jnp.float32
+    chunk = shape((rows, WIDE), bf16)
+    half_state = shape((HD + PARTS, width // 2), bf16)
+
+    *qk, state, slope, skips, codes, b, x, c, gate, gain = call(
+        first_kernel,
+        [shape((2 * rows, WIDE), bf16)] * CHIPS
+        + [shape((HD + PARTS, width), bf16), shape((8, width), f32), shape((8, width), f32)]
+        + [
+            shape(decay_codes.shape, jnp.int32),
+            shape(b_proj.shape, bf16),
+            shape((rows, width), bf16),
+            shape(c_proj.shape, bf16),
+            shape((rows, width), bf16),
+            shape((1, width), f32),
+        ],
+        (me, decay_rates, skip_gain, queries, keys, decay_codes, b_proj, mixer_input, c_proj)
+        + (gate_input, norm_gain.reshape(1, width)),
+        "ssshhhhhhhh",
+        [pltpu.SemaphoreType.DMA((6 + 2 * CHIPS,))],
+        flops=2 * rows * HD * width,
+        moved=10 * rows * width,
+    )
+    other = swapped(state)
+    qk = exchange(qk)
+    own, lead = call(
+        within_kernel,
+        [shape((rows, width), f32)] * 2,
+        (slope, skips, codes, b, x, c, gate),
+        "",
+        flops=4 * rows * rows * width,
+        moved=12 * rows * width,
+        exps=heads * rows * rows,
+    )
+    small = dict(flops=4 * HD * width, moved=4 * HD * width)
+    chip_state = call(chip_kernel, half_state, (me, slope, state, other), "s", **small)
+    chip_other = lax.ppermute(chip_state, "seq", [(i, i ^ 2) for i in range(n)])
+    two_chips = call(
+        two_chips_kernel, half_state, (me, own, slope, chip_state, chip_other), "sa", **small
+    )
+    far = lax.ppermute(two_chips, "seq", [(i, i + 4) for i in range(n // 2)])
+    ahead = call(
+        ahead_kernel, shape((HD, width // 2), bf16), (me, slope, chip_other, far), "s", **small
+    )
+    gated, squares = call(
+        gated_kernel,
+        [shape((rows, width), f32), shape((8, rows), f32)],
+        (me, slope, other, ahead, swapped(ahead), own, lead, c),
+        "s",
+        flops=4 * rows * HD * width,
+        moved=14 * rows * width,
+    )
+    squares = [squares] + [
+        lax.ppermute(squares, "head", [(i, (i + k) % m) for i in range(m)]) for k in range(1, m)
+    ]
+    mamba_out, *values = call(
+        functools.partial(norm_kernel, width * m),
+        [shape((rows, width), bf16)] + [chunk] * CHIPS,
+        (me, gain, gated, *squares),
+        "s",
+        flops=4 * rows * width,
+        moved=8 * rows * width,
+    )
+    values = exchange(values)
+    other_values = [swapped(part) for part in values]
+    own_keys = call(
+        keys_kernel,
+        shape((CHIPS * rows, WIDE), bf16),
+        (me, values[0], *qk),
+        "sa",
+        moved=4 * rows * width,
+    )
+    weights = call(
+        weights_kernel,
+        shape((2, CHIPS * rows, n * rows), bf16),
+        (me, own_keys, swapped(own_keys), *qk),
+        "s",
+        [pltpu.VMEM((CHIPS * rows, WIDE), bf16)],
+        flops=n * n * rows * rows * HD,
+        moved=2 * n * n * rows * rows,
+        exps=n * n * rows * rows // 2,
+        limit=24 * MIB,
+    )
+    results = call(
+        values_kernel,
+        [chunk] * CHIPS,
+        (me, weights, *values, *other_values),
+        "s",
+        [pltpu.VMEM((n * rows, WIDE), bf16), pltpu.VMEM((CHIPS * rows, WIDE), bf16)],
+        flops=n * n * rows * rows * HD,
+        moved=2 * n * n * rows * rows,
+    )
+    attn_out = call(
+        join_kernel,
+        shape((rows, width), bf16),
+        (me, *exchange(results)),
+        "s",
+        moved=4 * rows * width,
+    )
+    return (mamba_out, attn_out)
+
+
+def running_sum(log_decay):
+    span = log_decay.shape[1]
+    at = jnp.arange(span, dtype=jnp.int32)
+    earlier = (at[:, None] <= at[None, :]).astype(jnp.float32)
+    return jnp.dot(log_decay, earlier, precision=HIGH)
 
 
 def carried_in(array, axis, combine, identity):
@@ -40,7 +483,7 @@
 
 def block_step(state_carry, inputs):
     x_block, b_block, c_block, decay_block = inputs
-    running = jnp.cumsum(decay_block, axis=1)
+    running = running_sum(decay_block)
     span = decay_block.shape[1]
     causal = (
         jnp.arange(span, dtype=jnp.int32)[:, None] >= jnp.arange(span, dtype=jnp.int32)[None, :]
@@ -104,7 +547,7 @@
     return lax.cond(key_offset > q_pos[-1], lambda held: held, state_update, group_state)
 
 
-def on_device(
+def gathered(
     mixer_input,
     gate_input,
     b_proj,
@@ -132,7 +575,7 @@
 
     identity = (jnp.zeros_like(total_log), jnp.zeros_like(local_state))
     _, incoming = carried_in((total_log, local_state), "seq", combine, identity)
-    running = jnp.cumsum(log_decay, axis=1)
+    running = running_sum(log_decay)
     carried = jnp.einsum("tn,hnp->thp", c_proj.astype(jnp.float32), incoming, precision=HIGH)
     carried = carried * jnp.exp(running).T[:, :, None]
     x_float = mixer_input.reshape(tok_rows, heads_local, CHANNELS_PER_HD).astype(jnp.float32)
@@ -202,6 +645,21 @@
     return (mamba_out, attn_out)
 
 
+def on_device(mixer_input, gate_input, b_proj, c_proj, decay_codes, *others):
+    n = lax.axis_size("seq")
+    rows, width = mixer_input.shape
+    fits = (
+        n == 2 * CHIPS
+        and width == n * HD
+        and decay_codes.shape[0] == 2 * n
+        and b_proj.shape[1] == HD
+        and rows == BLOCK
+    )
+    return (two_heads_each if fits else gathered)(
+        mixer_input, gate_input, b_proj, c_proj, decay_codes, *others
+    )
+
+
 def solution(mesh):
     in_specs = (
         P("seq", "head"),

time: 201 us -> 81.4 us (0.40)
  the two profiles are of different devices: /device:TPU:25 before, /device:TPU:0 now
where the time goes in v2:
time: 81.4 us; the launch traced here: 80.6 us
  starting transfers between devices  35.5 us (44%)
  waiting for transfers between devices  29.4 us (36%)
  Pallas kernels  13.6 us (17%)
  local copies, waits for them, and re-layouts  1.3 us (2%)
    ppermute x9, starting transfers between devices, shifted(): return lax.ppermute(part, 'seq', [(i, (i + 2 * d) % n) for i in range(n)])  22.1 us
    ppermute x9, waiting for transfers between devices, shifted(): return lax.ppermute(part, 'seq', [(i, (i + 2 * d) % n) for i in range(n)])  21.2 us
    pallas_call x11, Pallas kernels, call(): pl.pallas_call(body, out_shape=outs, in_specs=[kinds[space] for space in...  13.6 us
    ppermute x1, starting transfers between devices, two_heads_each(): far = lax.ppermute(two_chips, 'seq', [(i, i + 4) for i in range(n // 2)])  4.66 us
    ppermute x3, starting transfers between devices, two_heads_each(): lax.ppermute(squares, 'head', [(i, (i + k) % m) for i in range(m)])  4.6 us
    ppermute x3, waiting for transfers between devices, two_heads_each(): lax.ppermute(squares, 'head', [(i, (i + k) % m) for i in range(m)])  3.64 us
    ppermute x1, starting transfers between devices, two_heads_each(): chip_other = lax.ppermute(chip_state, 'seq', [(i, i ^ 2) for i in range(n)])  3.01 us
    ppermute x7, waiting for transfers between devices, swapped(): return lax.ppermute(part, 'seq', [(i, i ^ 1) for i in range(2 * CHIPS)])  2.56 us
  transfers between devices with their start and end apart: 21, of which 11 were waited for; matrix products, arithmetic and copies ran while one was open for 0% of the time, Pallas kernels for 10%

profile of v2, /device:TPU:0, one launch (start us, length us, event | category | flops | bytes accessed | tf_op | source)
XLA Modules:
  0.0 80.6 jit_solution(14935635435098766309)
XLA Ops:
  0.6 0.0 copy-start
  0.6 0.6 copy-done
  1.3 0.0 copy-start.1
  1.3 0.7 copy-done.1
  2.0 2.7 %shard_map.113 = (bf16[512,256]{1,0:T(8,128)(2,1)S(1)}, bf16[512,256]{1,0:T(8,128)(2,1)S(1)}, bf16[512,256]{1,0:T(8,128)(2,1)S(1)}, bf16[512,256]{1,0:T(8,128)(2...) custom-call(s32[1]{0:T(128)} %bitcast.me_ref, ...), custom_call_target="tpu_custom_call" | custom-call | tf_op jit(solution)/shard_map/pallas_call | solution.py:34
  4.6 0.5 collective-permute-start
  5.1 1.2 %collective-permute-done.other_ref.local_ref = bf16[144,1024]{1,0:T(8,128)(2,1)S(1)} collective-permute-done((bf16[144,1024]{1,0:T(8,128)(2,1)S(1)}, bf16[144,1024]{1,0:T(8,128)(2,1)S(1)}, u32[]{:S(2)}, u32[]{:S(2)}) %collective-permute-start) | collective-permute-done | bytes 294944 | tf_op jit(solution)/shard_map/ppermute | solution.py:332
  6.3 0.1 shard_map.114.own_ref
  6.4 3.0 %collective-permute-start.1 = (bf16[144,512]{1,0:T(8,128)(2,1)S(1)}, bf16[144,512]{1,0:T(8,128)(2,1)S(1)}, u32[]{:S(2)}, u32[]{:S(2)}) collective-permute-start(bf16[144,512]{1,0:T(8,128)(2,1)S(1)} %shard_map.114.own_ref), channel_id=1, source_target_pairs={{0,8},{4,12},{8,0},{12,4},{16,24},{20,28},{24,16},{28,20},{1,9},{5... | collective-permute-start | bytes 442376 | tf_op jit(solution)/shard_map/ppermute | solution.py:388
  9.4 2.3 %shard_map.115 = (f32[256,1024]{1,0:T(8,128)S(1)}, f32[256,1024]{1,0:T(8,128)S(1)}) custom-call(f32[8,1024]{1,0:T(8,128)S(1)} %get-tuple-element.29.slope_ref, f32[8,1024]{1,0:T(8,128)S(1)} %get-tuple-element.31.skips_ref, s32[16,256]{1,0:T(8,128)S(1)} %get-tuple-element.32.codes_ref, bf16[256,128]{1,0:T(8,128)(2,1)S(1)} %get-tuple-element.33.b_ref, ...), custom_call_target="tpu_custom_call" | custom-call | tf_op jit(solution)/shard_map/pallas_call | solution.py:34
  11.7 1.9 %collective-permute-done.1.other_ref = bf16[144,512]{1,0:T(8,128)(2,1)S(1)} collective-permute-done((bf16[144,512]{1,0:T(8,128)(2,1)S(1)}, bf16[144,512]{1,0:T(8,128)(2,1)S(1)}, u32[]{:S(2)}, u32[]{:S(2)}) %collective-permute-start.1) | collective-permute-done | bytes 147488 | tf_op jit(solution)/shard_map/ppermute | solution.py:388
  13.6 0.1 shard_map.116
  13.7 4.7 %collective-permute-start.2 = (bf16[144,512]{1,0:T(8,128)(2,1)S(1)}, bf16[144,512]{1,0:T(8,128)(2,1)S(1)}, u32[]{:S(2)}, u32[]{:S(2)}) collective-permute-start(bf16[144,512]{1,0:T(8,128)(2,1)S(1)} %shard_map.116), channel_id=1, source_target_pairs={{0,16},{4,20},{8,24},{12,28},{1,17},{5,21},{9,25},{13,29},{2,18},{... | collective-permute-start | bytes 442376 | tf_op jit(solution)/shard_map/ppermute | solution.py:392
  18.3 1.6 %collective-permute-start.7 = (bf16[512,256]{1,0:T(8,128)(2,1)S(1)}, bf16[512,256]{1,0:T(8,128)(2,1)S(1)}, u32[]{:S(2)}, u32[]{:S(2)}) collective-permute-start(bf16[512,256]{1,0:T(8,128)(2,1)S(1)} %get-tuple-element.44), channel_id=1, source_target_pairs={{0,8},{4,12},{8,16},{12,20},{16,24},{20,28},{24,0},{28,4},{1,9},{5... | collective-permute-start | bytes 786440 | tf_op jit(solution)/shard_map/ppermute | solution.py:324
  20.0 0.0 collective-permute-start.8
  20.0 2.4 %collective-permute-start.9 = (bf16[512,256]{1,0:T(8,128)(2,1)S(1)}, bf16[512,256]{1,0:T(8,128)(2,1)S(1)}, u32[]{:S(2)}, u32[]{:S(2)}) collective-permute-start(bf16[512,256]{1,0:T(8,128)(2,1)S(1)} %get-tuple-element.46), channel_id=1, source_target_pairs={{0,24},{4,28},{8,0},{12,4},{16,8},{20,12},{24,16},{28,20},{1,25},{... | collective-permute-start | bytes 786440 | tf_op jit(solution)/shard_map/ppermute | solution.py:324
  22.4 0.2 collective-permute-done.2.far_ref
  22.6 0.1 shard_map.117.ahead_ref
  22.7 0.1 collective-permute-start.3
  22.8 1.3 %collective-permute-done.3.other_ref = bf16[128,512]{1,0:T(8,128)(2,1)S(1)} collective-permute-done((bf16[128,512]{1,0:T(8,128)(2,1)S(1)}, bf16[128,512]{1,0:T(8,128)(2,1)S(1)}, u32[]{:S(2)}, u32[]{:S(2)}) %collective-permute-start.3) | collective-permute-done | bytes 131104 | tf_op jit(solution)/shard_map/ppermute | solution.py:332
  24.1 1.1 %shard_map.118 = (f32[256,1024]{1,0:T(8,128)S(1)}, f32[8,256]{1,0:T(8,128)S(1)}) custom-call(s32[1]{0:T(128)} %bitcast.me_ref, f32[8,1024]{1,0:T(8,128)S(1)} %get-tuple-element.29.slope_ref, bf16[144,1024]{1,0:T(8,128)(2,1)S(1)} %collective-permute-done.other_ref.local_ref, bf16[128,512]{1,0:T(8,128)(2,1)S(1)} %shard_map.117.ahead_ref, ...), custom_call_target="tpu_custom_call" | custom-call | tf_op jit(solution)/shard_map/pallas_call | solution.py:34
  25.2 1.5 %collective-permute-start.4 = (f32[8,256]{1,0:T(8,128)S(1)}, f32[8,256]{1,0:T(8,128)S(1)}, u32[]{:S(2)}, u32[]{:S(2)}) collective-permute-start(f32[8,256]{1,0:T(8,128)S(1)} %get-tuple-element.40.rest_0_), channel_id=1, source_target_pairs={{0,1},{1,2},{2,3},{3,0},{4,5},{5,6},{6,7},{7,4},{8,9},{9,10},{10,1... | collective-permute-start | bytes 24584 | tf_op jit(solution)/shard_map/ppermute | solution.py:405
  26.7 1.5 %collective-permute-start.5 = (f32[8,256]{1,0:T(8,128)S(1)}, f32[8,256]{1,0:T(8,128)S(1)}, u32[]{:S(2)}, u32[]{:S(2)}) collective-permute-start(f32[8,256]{1,0:T(8,128)S(1)} %get-tuple-element.40.rest_0_), channel_id=1, source_target_pairs={{0,2},{1,3},{2,0},{3,1},{4,6},{5,7},{6,4},{7,5},{8,10},{9,11},{10,... | collective-permute-start | bytes 24584 | tf_op jit(solution)/shard_map/ppermute | solution.py:405
  28.2 1.5 %collective-permute-done.4.rest_1_ = f32[8,256]{1,0:T(8,128)S(1)} collective-permute-done((f32[8,256]{1,0:T(8,128)S(1)}, f32[8,256]{1,0:T(8,128)S(1)}, u32[]{:S(2)}, u32[]{:S(2)}) %collective-permute-start.4) | collective-permute-done | bytes 8224 | tf_op jit(solution)/shard_map/ppermute | solution.py:405
  29.8 1.5 %collective-permute-start.6 = (f32[8,256]{1,0:T(8,128)S(1)}, f32[8,256]{1,0:T(8,128)S(1)}, u32[]{:S(2)}, u32[]{:S(2)}) collective-permute-start(f32[8,256]{1,0:T(8,128)S(1)} %get-tuple-element.40.rest_0_), channel_id=1, source_target_pairs={{0,3},{1,0},{2,1},{3,2},{4,7},{5,4},{6,5},{7,6},{8,11},{9,8},{10,9... | collective-permute-start | bytes 24584 | tf_op jit(solution)/shard_map/ppermute | solution.py:405
  31.3 0.0 collective-permute-done.5.rest_2_
  31.3 2.1 %collective-permute-done.6.rest_3_ = f32[8,256]{1,0:T(8,128)S(1)} collective-permute-done((f32[8,256]{1,0:T(8,128)S(1)}, f32[8,256]{1,0:T(8,128)S(1)}, u32[]{:S(2)}, u32[]{:S(2)}) %collective-permute-start.6) | collective-permute-done | bytes 8224 | tf_op jit(solution)/shard_map/ppermute | solution.py:405
  33.4 1.0 %shard_map.119 = (bf16[256,1024]{1,0:T(8,128)(2,1)}, bf16[256,256]{1,0:T(8,128)(2,1)S(1)}, bf16[256,256]{1,0:T(8,128)(2,1)S(1)}, bf16[256,256]{1,0:T(8,128)(2,1)S(1)}, bf16[256,256]{1,0:T(8,128)(2,1)S(1)}) custom-call(s32[1]{0:T(128)} %bitcast.me_ref, f32[1,1024]{1,0:T(1,128)S(1)} %get-tuple-element.28.gain_ref, ...), custom_call_target="tpu_custom_call" | custom-call | tf_op jit(solution)/shard_map/pallas_call | solution.py:34
  34.4 0.0 collective-permute-done.7.rest_1_
  34.4 4.4 %collective-permute-done.8.rest_2_ = bf16[512,256]{1,0:T(8,128)(2,1)S(1)} collective-permute-done((bf16[512,256]{1,0:T(8,128)(2,1)S(1)}, bf16[512,256]{1,0:T(8,128)(2,1)S(1)}, u32[]{:S(2)}, u32[]{:S(2)}) %collective-permute-start.8) | collective-permute-done | bytes 262176 | tf_op jit(solution)/shard_map/ppermute | solution.py:324
  38.8 0.0 collective-permute-done.9.rest_3_
  38.8 0.1 collective-permute-start.10
  38.9 9.2 %collective-permute-start.11 = (bf16[256,256]{1,0:T(8,128)(2,1)S(1)}, bf16[256,256]{1,0:T(8,128)(2,1)S(1)}, u32[]{:S(2)}, u32[]{:S(2)}) collective-permute-start(bf16[256,256]{1,0:T(8,128)(2,1)S(1)} %get-tuple-element.47), channel_id=1, source_target_pairs={{0,8},{4,12},{8,16},{12,20},{16,24},{20,28},{24,0},{28,4},{1,9},{5... | collective-permute-start | bytes 393224 | tf_op jit(solution)/shard_map/ppermute | solution.py:324
  48.2 3.4 %collective-permute-start.12 = (bf16[256,256]{1,0:T(8,128)(2,1)S(1)}, bf16[256,256]{1,0:T(8,128)(2,1)S(1)}, u32[]{:S(2)}, u32[]{:S(2)}) collective-permute-start(bf16[256,256]{1,0:T(8,128)(2,1)S(1)} %get-tuple-element.48), channel_id=1, source_target_pairs={{0,16},{4,20},{8,24},{12,28},{16,0},{20,4},{24,8},{28,12},{1,17},{... | collective-permute-start | bytes 393224 | tf_op jit(solution)/shard_map/ppermute | solution.py:324
  51.5 0.0 collective-permute-start.13
  51.5 0.0 collective-permute-start.14
  51.5 3.9 %collective-permute-done.11.rest_1_ = bf16[256,256]{1,0:T(8,128)(2,1)S(1)} collective-permute-done((bf16[256,256]{1,0:T(8,128)(2,1)S(1)}, bf16[256,256]{1,0:T(8,128)(2,1)S(1)}, u32[]{:S(2)}, u32[]{:S(2)}) %collective-permute-start.11) | collective-permute-done | bytes 131104 | tf_op jit(solution)/shard_map/ppermute | solution.py:324
  55.4 0.0 collective-permute-start.15
  55.4 5.3 %collective-permute-done.12.rest_2_ = bf16[256,256]{1,0:T(8,128)(2,1)S(1)} collective-permute-done((bf16[256,256]{1,0:T(8,128)(2,1)S(1)}, bf16[256,256]{1,0:T(8,128)(2,1)S(1)}, u32[]{:S(2)}, u32[]{:S(2)}) %collective-permute-start.12) | collective-permute-done | bytes 131104 | tf_op jit(solution)/shard_map/ppermute | solution.py:324
  60.7 0.0 collective-permute-start.16
  60.8 0.0 collective-permute-done.13.rest_3_
  60.8 0.5 collective-permute-start.17
  61.3 0.0 collective-permute-done.10.other_ref
  61.3 3.8 %shard_map.121.weights_ref = bf16[2,1024,2048]{2,1,0:T(8,128)(2,1)S(1)} custom-call(s32[1]{0:T(128)} %bitcast.me_ref, bf16[1024,256]{1,0:T(8,128)(2,1)S(1)} %shard_map.120.own_ref, bf16[1024,256]{1,0:T(8,128)(2,1)S(1)} %collective-permute-done.10.other_ref, bf16[512,256]{1,0:T(8,128)(2,1)S(1)} %get-tuple-element.43.rest_0_, ...), custom_call_target="tpu_custom_call" | custom-call | tf_op jit(solution)/shard_map/pallas_call | solution.py:34
  65.0 0.0 collective-permute-done.14.rest_4_
  65.1 0.0 collective-permute-done.15.rest_5_
  65.1 0.0 collective-permute-done.16.rest_6_
  65.1 0.0 collective-permute-done.17.rest_7_
  65.1 1.7 %shard_map.122 = (bf16[256,256]{1,0:T(8,128)(2,1)S(1)}, bf16[256,256]{1,0:T(8,128)(2,1)S(1)}, bf16[256,256]{1,0:T(8,128)(2,1)S(1)}, bf16[256,256]{1,0:T(8,128)(2,1)S(1)}) custom-call(s32[1]{0:T(128)} %bitcast.me_ref, bf16[2,1024,2048]{2,1,0:T(8,128)(2,1)S(1)} %shard_map.121.weights_ref, bf16[256,256]{1,0:T(8,128)(2,1)S(1)} %get-tuple-element.42.after_ref.rest_0_, ...), custom_call_target="tpu_custom_call" | custom-call | tf_op jit(solution)/shard_map/pallas_call | solution.py:34
  66.8 2.9 %collective-permute-start.18 = (bf16[256,256]{1,0:T(8,128)(2,1)S(1)}, bf16[256,256]{1,0:T(8,128)(2,1)S(1)}, u32[]{:S(2)}, u32[]{:S(2)}) collective-permute-start(bf16[256,256]{1,0:T(8,128)(2,1)S(1)} %get-tuple-element.51), channel_id=1, source_target_pairs={{0,8},{4,12},{8,16},{12,20},{16,24},{20,28},{24,0},{28,4},{1,9},{5... | collective-permute-start | bytes 393224 | tf_op jit(solution)/shard_map/ppermute | solution.py:324
  69.7 0.3 collective-permute-start.19
  70.1 2.1 %collective-permute-start.20 = (bf16[256,256]{1,0:T(8,128)(2,1)S(1)}, bf16[256,256]{1,0:T(8,128)(2,1)S(1)}, u32[]{:S(2)}, u32[]{:S(2)}) collective-permute-start(bf16[256,256]{1,0:T(8,128)(2,1)S(1)} %get-tuple-element.53), channel_id=1, source_target_pairs={{0,24},{4,28},{8,0},{12,4},{16,8},{20,12},{24,16},{28,20},{1,25},{... | collective-permute-start | bytes 393224 | tf_op jit(solution)/shard_map/ppermute | solution.py:324
  72.2 2.9 %collective-permute-done.18.rest_1_ = bf16[256,256]{1,0:T(8,128)(2,1)S(1)} collective-permute-done((bf16[256,256]{1,0:T(8,128)(2,1)S(1)}, bf16[256,256]{1,0:T(8,128)(2,1)S(1)}, u32[]{:S(2)}, u32[]{:S(2)}) %collective-permute-start.18) | collective-permute-done | bytes 131104 | tf_op jit(solution)/shard_map/ppermute | solution.py:324
  75.1 4.7 %collective-permute-done.19.rest_2_ = bf16[256,256]{1,0:T(8,128)(2,1)S(1)} collective-permute-done((bf16[256,256]{1,0:T(8,128)(2,1)S(1)}, bf16[256,256]{1,0:T(8,128)(2,1)S(1)}, u32[]{:S(2)}, u32[]{:S(2)}) %collective-permute-start.19) | collective-permute-done | bytes 131104 | tf_op jit(solution)/shard_map/ppermute | solution.py:324
  79.8 0.0 collective-permute-done.20.rest_3_
  79.8 0.9 %shard_map.123 = bf16[256,1024]{1,0:T(8,128)(2,1)} custom-call(s32[1]{0:T(128)} %bitcast.me_ref, bf16[256,256]{1,0:T(8,128)(2,1)S(1)} %get-tuple-element.50.rest_0_, bf16[256,256]{1,0:T(8,128)(2,1)S(1)} %collective-permute-done.18.rest_1_, bf16[256,256]{1,0:T(8,128)(2,1)S(1)} %collective-permute-done.19.rest_2_, ...), custom_call_target="tpu_custom_call" | custom-call | tf_op jit(solution)/shard_map/pallas_call | solution.py:34
  (1 shorter events, 0.0 us)
Async XLA Ops:
  0.6 0.7 copy-start
  1.3 0.7 copy-start.1
  4.6 1.7 %collective-permute-start = (bf16[144,1024]{1,0:T(8,128)(2,1)S(1)}, bf16[144,1024]{1,0:T(8,128)(2,1)S(1)}, u32[]{:S(2)}, u32[]{:S(2)}) collective-permute-start(bf16[144,1024]{1,0:T(8,128)(2,1)S(1)} %get-tuple-element.30.own_ref), channel_id=1, source_target_pairs={{0,4},{4,0},{8,12},{12,8},{16,20},{20,16},{24,28},{28,24},{1,5},{5... | collective-permute-start | bytes 884744 | tf_op jit(solution)/shard_map/ppermute | solution.py:332
  6.4 7.2 %collective-permute-start.1 = (bf16[144,512]{1,0:T(8,128)(2,1)S(1)}, bf16[144,512]{1,0:T(8,128)(2,1)S(1)}, u32[]{:S(2)}, u32[]{:S(2)}) collective-permute-start(bf16[144,512]{1,0:T(8,128)(2,1)S(1)} %shard_map.114.own_ref), channel_id=1, source_target_pairs={{0,8},{4,12},{8,0},{12,4},{16,24},{20,28},{24,16},{28,20},{1,9},{5... | collective-permute-start | bytes 442376 | tf_op jit(solution)/shard_map/ppermute | solution.py:388
  13.7 8.9 %collective-permute-start.2 = (bf16[144,512]{1,0:T(8,128)(2,1)S(1)}, bf16[144,512]{1,0:T(8,128)(2,1)S(1)}, u32[]{:S(2)}, u32[]{:S(2)}) collective-permute-start(bf16[144,512]{1,0:T(8,128)(2,1)S(1)} %shard_map.116), channel_id=1, source_target_pairs={{0,16},{4,20},{8,24},{12,28},{1,17},{5,21},{9,25},{13,29},{2,18},{... | collective-permute-start | bytes 442376 | tf_op jit(solution)/shard_map/ppermute | solution.py:392
  18.3 16.1 %collective-permute-start.7 = (bf16[512,256]{1,0:T(8,128)(2,1)S(1)}, bf16[512,256]{1,0:T(8,128)(2,1)S(1)}, u32[]{:S(2)}, u32[]{:S(2)}) collective-permute-start(bf16[512,256]{1,0:T(8,128)(2,1)S(1)} %get-tuple-element.44), channel_id=1, source_target_pairs={{0,8},{4,12},{8,16},{12,20},{16,24},{20,28},{24,0},{28,4},{1,9},{5... | collective-permute-start | bytes 786440 | tf_op jit(solution)/shard_map/ppermute | solution.py:324
  20.0 18.8 %collective-permute-start.8 = (bf16[512,256]{1,0:T(8,128)(2,1)S(1)}, bf16[512,256]{1,0:T(8,128)(2,1)S(1)}, u32[]{:S(2)}, u32[]{:S(2)}) collective-permute-start(bf16[512,256]{1,0:T(8,128)(2,1)S(1)} %get-tuple-element.45), channel_id=1, source_target_pairs={{0,16},{4,20},{8,24},{12,28},{16,0},{20,4},{24,8},{28,12},{1,17},{... | collective-permute-start | bytes 786440 | tf_op jit(solution)/shard_map/ppermute | solution.py:324
  20.0 18.8 %collective-permute-start.9 = (bf16[512,256]{1,0:T(8,128)(2,1)S(1)}, bf16[512,256]{1,0:T(8,128)(2,1)S(1)}, u32[]{:S(2)}, u32[]{:S(2)}) collective-permute-start(bf16[512,256]{1,0:T(8,128)(2,1)S(1)} %get-tuple-element.46), channel_id=1, source_target_pairs={{0,24},{4,28},{8,0},{12,4},{16,8},{20,12},{24,16},{28,20},{1,25},{... | collective-permute-start | bytes 786440 | tf_op jit(solution)/shard_map/ppermute | solution.py:324
  22.7 1.4 %collective-permute-start.3 = (bf16[128,512]{1,0:T(8,128)(2,1)S(1)}, bf16[128,512]{1,0:T(8,128)(2,1)S(1)}, u32[]{:S(2)}, u32[]{:S(2)}) collective-permute-start(bf16[128,512]{1,0:T(8,128)(2,1)S(1)} %shard_map.117.ahead_ref), channel_id=1, source_target_pairs={{0,4},{4,0},{8,12},{12,8},{16,20},{20,16},{24,28},{28,24},{1,5},{5... | collective-permute-start | bytes 393224 | tf_op jit(solution)/shard_map/ppermute | solution.py:332
  25.2 4.6 %collective-permute-start.4 = (f32[8,256]{1,0:T(8,128)S(1)}, f32[8,256]{1,0:T(8,128)S(1)}, u32[]{:S(2)}, u32[]{:S(2)}) collective-permute-start(f32[8,256]{1,0:T(8,128)S(1)} %get-tuple-element.40.rest_0_), channel_id=1, source_target_pairs={{0,1},{1,2},{2,3},{3,0},{4,5},{5,6},{6,7},{7,4},{8,9},{9,10},{10,1... | collective-permute-start | bytes 24584 | tf_op jit(solution)/shard_map/ppermute | solution.py:405
  26.7 4.6 %collective-permute-start.5 = (f32[8,256]{1,0:T(8,128)S(1)}, f32[8,256]{1,0:T(8,128)S(1)}, u32[]{:S(2)}, u32[]{:S(2)}) collective-permute-start(f32[8,256]{1,0:T(8,128)S(1)} %get-tuple-element.40.rest_0_), channel_id=1, source_target_pairs={{0,2},{1,3},{2,0},{3,1},{4,6},{5,7},{6,4},{7,5},{8,10},{9,11},{10,... | collective-permute-start | bytes 24584 | tf_op jit(solution)/shard_map/ppermute | solution.py:405
  29.8 3.7 %collective-permute-start.6 = (f32[8,256]{1,0:T(8,128)S(1)}, f32[8,256]{1,0:T(8,128)S(1)}, u32[]{:S(2)}, u32[]{:S(2)}) collective-permute-start(f32[8,256]{1,0:T(8,128)S(1)} %get-tuple-element.40.rest_0_), channel_id=1, source_target_pairs={{0,3},{1,0},{2,1},{3,2},{4,7},{5,4},{6,5},{7,6},{8,11},{9,8},{10,9... | collective-permute-start | bytes 24584 | tf_op jit(solution)/shard_map/ppermute | solution.py:405
  38.8 22.4 %collective-permute-start.10 = (bf16[1024,256]{1,0:T(8,128)(2,1)S(1)}, bf16[1024,256]{1,0:T(8,128)(2,1)S(1)}, u32[]{:S(2)}, u32[]{:S(2)}) collective-permute-start(bf16[1024,256]{1,0:T(8,128)(2,1)S(1)} %shard_map.120.own_ref), channel_id=1, source_target_pairs={{0,4},{4,0},{8,12},{12,8},{16,20},{20,16},{24,28},{28,24},{1,5},{5... | collective-permute-start | bytes 1572872 | tf_op jit(solution)/shard_map/ppermute | solution.py:332
  38.9 16.5 %collective-permute-start.11 = (bf16[256,256]{1,0:T(8,128)(2,1)S(1)}, bf16[256,256]{1,0:T(8,128)(2,1)S(1)}, u32[]{:S(2)}, u32[]{:S(2)}) collective-permute-start(bf16[256,256]{1,0:T(8,128)(2,1)S(1)} %get-tuple-element.47), channel_id=1, source_target_pairs={{0,8},{4,12},{8,16},{12,20},{16,24},{20,28},{24,0},{28,4},{1,9},{5... | collective-permute-start | bytes 393224 | tf_op jit(solution)/shard_map/ppermute | solution.py:324
  48.2 12.6 %collective-permute-start.12 = (bf16[256,256]{1,0:T(8,128)(2,1)S(1)}, bf16[256,256]{1,0:T(8,128)(2,1)S(1)}, u32[]{:S(2)}, u32[]{:S(2)}) collective-permute-start(bf16[256,256]{1,0:T(8,128)(2,1)S(1)} %get-tuple-element.48), channel_id=1, source_target_pairs={{0,16},{4,20},{8,24},{12,28},{16,0},{20,4},{24,8},{28,12},{1,17},{... | collective-permute-start | bytes 393224 | tf_op jit(solution)/shard_map/ppermute | solution.py:324
  51.5 9.2 %collective-permute-start.13 = (bf16[256,256]{1,0:T(8,128)(2,1)S(1)}, bf16[256,256]{1,0:T(8,128)(2,1)S(1)}, u32[]{:S(2)}, u32[]{:S(2)}) collective-permute-start(bf16[256,256]{1,0:T(8,128)(2,1)S(1)} %get-tuple-element.49), channel_id=1, source_target_pairs={{0,24},{4,28},{8,0},{12,4},{16,8},{20,12},{24,16},{28,20},{1,25},{... | collective-permute-start | bytes 393224 | tf_op jit(solution)/shard_map/ppermute | solution.py:324
  51.5 13.5 %collective-permute-start.14 = (bf16[256,256]{1,0:T(8,128)(2,1)S(1)}, bf16[256,256]{1,0:T(8,128)(2,1)S(1)}, u32[]{:S(2)}, u32[]{:S(2)}) collective-permute-start(bf16[256,256]{1,0:T(8,128)(2,1)S(1)} %get-tuple-element.42.after_ref.rest_0_), channel_id=1, source_target_pairs={{0,4},{4,0},{8,12},{12,8},{16,20},{20,16},{24,28},{28,24},{1,5},{5... | collective-permute-start | bytes 393224 | tf_op jit(solution)/shard_map/ppermute | solution.py:332
  55.4 9.6 %collective-permute-start.15 = (bf16[256,256]{1,0:T(8,128)(2,1)S(1)}, bf16[256,256]{1,0:T(8,128)(2,1)S(1)}, u32[]{:S(2)}, u32[]{:S(2)}) collective-permute-start(bf16[256,256]{1,0:T(8,128)(2,1)S(1)} %collective-permute-done.11.rest_1_), channel_id=1, source_target_pairs={{0,4},{4,0},{8,12},{12,8},{16,20},{20,16},{24,28},{28,24},{1,5},{5... | collective-permute-start | bytes 393224 | tf_op jit(solution)/shard_map/ppermute | solution.py:332
  60.7 4.3 %collective-permute-start.16 = (bf16[256,256]{1,0:T(8,128)(2,1)S(1)}, bf16[256,256]{1,0:T(8,128)(2,1)S(1)}, u32[]{:S(2)}, u32[]{:S(2)}) collective-permute-start(bf16[256,256]{1,0:T(8,128)(2,1)S(1)} %collective-permute-done.12.rest_2_), channel_id=1, source_target_pairs={{0,4},{4,0},{8,12},{12,8},{16,20},{20,16},{24,28},{28,24},{1,5},{5... | collective-permute-start | bytes 393224 | tf_op jit(solution)/shard_map/ppermute | solution.py:332
  60.8 4.3 %collective-permute-start.17 = (bf16[256,256]{1,0:T(8,128)(2,1)S(1)}, bf16[256,256]{1,0:T(8,128)(2,1)S(1)}, u32[]{:S(2)}, u32[]{:S(2)}) collective-permute-start(bf16[256,256]{1,0:T(8,128)(2,1)S(1)} %collective-permute-done.13.rest_3_), channel_id=1, source_target_pairs={{0,4},{4,0},{8,12},{12,8},{16,20},{20,16},{24,28},{28,24},{1,5},{5... | collective-permute-start | bytes 393224 | tf_op jit(solution)/shard_map/ppermute | solution.py:332
  66.8 8.3 %collective-permute-start.18 = (bf16[256,256]{1,0:T(8,128)(2,1)S(1)}, bf16[256,256]{1,0:T(8,128)(2,1)S(1)}, u32[]{:S(2)}, u32[]{:S(2)}) collective-permute-start(bf16[256,256]{1,0:T(8,128)(2,1)S(1)} %get-tuple-element.51), channel_id=1, source_target_pairs={{0,8},{4,12},{8,16},{12,20},{16,24},{20,28},{24,0},{28,4},{1,9},{5... | collective-permute-start | bytes 393224 | tf_op jit(solution)/shard_map/ppermute | solution.py:324
  69.7 10.0 %collective-permute-start.19 = (bf16[256,256]{1,0:T(8,128)(2,1)S(1)}, bf16[256,256]{1,0:T(8,128)(2,1)S(1)}, u32[]{:S(2)}, u32[]{:S(2)}) collective-permute-start(bf16[256,256]{1,0:T(8,128)(2,1)S(1)} %get-tuple-element.52), channel_id=1, source_target_pairs={{0,16},{4,20},{8,24},{12,28},{16,0},{20,4},{24,8},{28,12},{1,17},{... | collective-permute-start | bytes 393224 | tf_op jit(solution)/shard_map/ppermute | solution.py:324
  70.1 9.7 %collective-permute-start.20 = (bf16[256,256]{1,0:T(8,128)(2,1)S(1)}, bf16[256,256]{1,0:T(8,128)(2,1)S(1)}, u32[]{:S(2)}, u32[]{:S(2)}) collective-permute-start(bf16[256,256]{1,0:T(8,128)(2,1)S(1)} %get-tuple-element.53), channel_id=1, source_target_pairs={{0,24},{4,28},{8,0},{12,4},{16,8},{20,12},{24,16},{28,20},{1,25},{... | collective-permute-start | bytes 393224 | tf_op jit(solution)/shard_map/ppermute | solution.py:324

commit v3 on v2

--- a/solution.py
+++ b/solution.py
@@ -28,7 +28,7 @@
 PARTS = 16
 
 
-def call(body, outs, args, spaces, scratch=(), flops=0, moved=0, exps=0, limit=16 * MIB):
+def call(body, outs, args, spaces, scratch=(), limit=16 * MIB):
     kinds = {"s": SMEM, "h": HBM, "a": ANY, "v": VMEM}
     spaces = spaces + "v" * (len(args) - len(spaces))
     return pl.pallas_call(
@@ -106,43 +106,68 @@
     return jnp.exp2(second[1] * slope) * first[0] + second[0], first[1] + second[1]
 
 
+def chunk_pairs(chip, steps, q_hbm, k_hbm, outs):
+    rows = q_hbm.shape[0]
+    pairs = []
+    for d, out in zip(steps, outs):
+        cols = block_of(around(chip, d), WIDE)
+        pairs.append((q_hbm.at[:, cols], out.at[pl.ds(0, rows), :]))
+        pairs.append((k_hbm.at[:, cols], out.at[pl.ds(rows, rows), :]))
+    return pairs
+
+
+def qk_kernel(me_ref, after_ref, q_hbm, k_hbm, *rest):
+    pairs = chunk_pairs(chip_of(me_ref[0]), (1, 3), q_hbm, k_hbm, rest[:2])
+    copies = [pltpu.make_async_copy(a, b, rest[2].at[i]) for i, (a, b) in enumerate(pairs)]
+    for copy in copies:
+        copy.start()
+    for copy in copies:
+        copy.wait()
+
+
 def first_kernel(
-    me_ref, rates_ref, skip_ref, q_hbm, k_hbm, codes_hbm, b_hbm, x_hbm, c_hbm, gate_hbm, gain_hbm, *rest
+    me_ref, rates_hbm, skip_hbm, codes_hbm, b_hbm, x_hbm, c_hbm, gate_hbm, gain_hbm, q_hbm, k_hbm,
+    state_ref, slope_ref, skips_ref, codes_ref, b_ref, x_ref, c_ref, gate_ref, gain_ref, *rest
 ):
-    qk, state_ref, slope_ref, skips_ref = rest[:CHIPS], *rest[CHIPS : CHIPS + 3]
-    codes_ref, b_ref, x_ref, c_ref, gate_ref, gain_ref, sems = rest[CHIPS + 3 :]
+    qk, (rates_ref, skip_ref, sems) = rest[:2], rest[2:]
     rows = x_ref.shape[0]
     chip = chip_of(me_ref[0])
-    pairs = [(codes_hbm, codes_ref), (b_hbm, b_ref), (x_hbm, x_ref)]
-    for d in range(CHIPS):
-        cols = block_of(around(chip, d), WIDE)
-        pairs.append((q_hbm.at[:, cols], qk[d].at[pl.ds(0, rows), :]))
-        pairs.append((k_hbm.at[:, cols], qk[d].at[pl.ds(rows, rows), :]))
-    pairs += [(c_hbm, c_ref), (gate_hbm, gate_ref), (gain_hbm, gain_ref)]
+    pairs = [
+        (codes_hbm, codes_ref),
+        (b_hbm, b_ref),
+        (rates_hbm, rates_ref),
+        (x_hbm, x_ref),
+        (skip_hbm, skip_ref),
+        (c_hbm, c_ref),
+        (gate_hbm, gate_ref),
+        (gain_hbm, gain_ref),
+    ]
+    pairs += chunk_pairs(chip, (0, 2), q_hbm, k_hbm, qk)
     copies = [pltpu.make_async_copy(a, b, sems.at[i]) for i, (a, b) in enumerate(pairs)]
     for copy in copies:
         copy.start()
-    for pair in range(x_ref.shape[1] // HD):
-        cols = slice(pair * HD, (pair + 1) * HD)
-        left = left_lanes(8)
-        one, two = 2 * pair, 2 * pair + 1
-        slope_ref[:, cols] = jnp.where(left, rates_ref[one], rates_ref[two]) * -LOG2E
-        skips_ref[:, cols] = jnp.where(left, skip_ref[one], skip_ref[two])
     copies[0].wait()
     _, counts = step_counts(codes_ref[...])
     copies[1].wait()
     b_turned = b_ref[...].astype(jnp.float32).T.astype(jnp.bfloat16)
     left = left_lanes(rows)
     copies[2].wait()
+    copies[3].wait()
     for pair in range(x_ref.shape[1] // HD):
         cols = slice(pair * HD, (pair + 1) * HD)
+        one, two = rates_ref[2 * pair], rates_ref[2 * pair + 1]
+        slope_ref[:, cols] = jnp.where(left_lanes(8), one, two) * -LOG2E
         column = jnp.where(left, counts[:, 2 * pair : 2 * pair + 1], counts[:, 2 * pair + 1 : 2 * pair + 2])
         total = column[rows - 1 : rows, :]
         weight = jnp.exp2((total - column) * slope_ref[0:1, cols])
         x = (x_ref[:, cols].astype(jnp.float32) * weight).astype(jnp.bfloat16)
         state_ref[pl.ds(0, HD), cols] = nn(b_turned, x).astype(jnp.bfloat16)
         state_ref[pl.ds(HD, PARTS), cols] = as_parts(total)
-    for copy in copies[3:]:
+    copies[4].wait()
+    for pair in range(x_ref.shape[1] // HD):
+        cols = slice(pair * HD, (pair + 1) * HD)
+        skips_ref[:, cols] = jnp.where(left_lanes(8), skip_ref[2 * pair], skip_ref[2 * pair + 1])
+    for copy in copies[5:]:
         copy.wait()
 
 
@@ -158,7 +183,7 @@
     out_ref[pl.ds(HD, PARTS), :] = as_parts(total)
 
 
-def two_chips_kernel(me_ref, after_ref, slope_ref, own_ref, other_ref, out_ref):
+def two_chips_kernel(me_ref, after_ref, also_ref, slope_ref, own_ref, other_ref, out_ref):
     me = me_ref[0]
     odd = chip_of(me) & 1
     own, other = own_ref[...], other_ref[...]
@@ -291,24 +316,43 @@
                 )
 
 
-def values_kernel(me_ref, weights_ref, *rest):
-    own, other, outs = rest[:CHIPS], rest[CHIPS : 2 * CHIPS], rest[2 * CHIPS : 3 * CHIPS]
-    v_ref, o_ref = rest[3 * CHIPS :]
+def passed_kernel(after_ref, in_ref, out_ref):
+    out_ref[...] = in_ref[...]
+
+
+def weighted(weights_ref, head, i, rows, base, v_ref):
+    seen = (i + 1) * rows
+    lanes = slice(head * HD, (head + 1) * HD)
+    held = weights_ref[head, pl.ds(i * rows, rows), pl.ds(base, seen)]
+    return nn(held, v_ref[pl.ds(0, seen), lanes])
+
+
+def in_place(me_ref, parts, v_ref):
+    chip = chip_of(me_ref[0])
+    for d, part in enumerate(parts):
+        v_ref[block_of(around(chip, CHIPS - d), part.shape[0]), :] = part[...]
+
+
+def own_values_kernel(me_ref, weights_ref, *rest):
+    own, out_ref, v_ref = rest[:CHIPS], rest[CHIPS], rest[CHIPS + 1]
     rows = own[0].shape[0]
-    chip = chip_of(me_ref[0])
-    for d in range(CHIPS):
-        back = around(chip, CHIPS - d)
-        v_ref[block_of(back, rows), :] = own[d][...]
-        v_ref[block_of(back + CHIPS, rows), :] = other[d][...]
+    in_place(me_ref, own, v_ref)
     for i in range(CHIPS):
-        at, seen = pl.ds(i * rows, rows), (i + 1) * rows
         for head in range(2):
             lanes = slice(head * HD, (head + 1) * HD)
-            total = 0.0
-            for base in (0, CHIPS * rows):
-                seen_at = pl.ds(base, seen)
-                total = total + nn(weights_ref[head, at, seen_at], v_ref[seen_at, lanes])
-            o_ref[at, lanes] = total.astype(jnp.bfloat16)
+            out_ref[pl.ds(i * rows, rows), lanes] = weighted(weights_ref, head, i, rows, 0, v_ref)
+
+
+def values_kernel(me_ref, partial_ref, weights_ref, *rest):
+    other, outs, v_ref, o_ref = rest[:CHIPS], rest[CHIPS : 2 * CHIPS], *rest[2 * CHIPS :]
+    rows = other[0].shape[0]
+    in_place(me_ref, other, v_ref)
+    for i in range(CHIPS):
+        for head in range(2):
+            at, lanes = pl.ds(i * rows, rows), slice(head * HD, (head + 1) * HD)
+            more = weighted(weights_ref, head, i, rows, CHIPS * rows, v_ref)
+            o_ref[at, lanes] = (partial_ref[at, lanes] + more).astype(jnp.bfloat16)
+    chip = chip_of(me_ref[0])
     for d in range(CHIPS):
         outs[d][...] = o_ref[block_of(around(chip, d), rows), :]
 
@@ -348,15 +392,14 @@
     rows, width = mixer_input.shape
     heads = decay_codes.shape[0]
     me = lax.axis_index("seq").astype(jnp.int32).reshape(1)
-    shape = jax.ShapeDtypeStruct
+    shape = pltpu.VMEM
     bf16, f32 = jnp.bfloat16, jnp.float32
     chunk = shape((rows, WIDE), bf16)
     half_state = shape((HD + PARTS, width // 2), bf16)
 
-    *qk, state, slope, skips, codes, b, x, c, gate, gain = call(
+    state, slope, skips, codes, b, x, c, gate, gain, qk_own, qk_two = call(
         first_kernel,
-        [shape((2 * rows, WIDE), bf16)] * CHIPS
-        + [shape((HD + PARTS, width), bf16), shape((8, width), f32), shape((8, width), f32)]
+        [shape((HD + PARTS, width), bf16), shape((8, width), f32), shape((8, width), f32)]
         + [
             shape(decay_codes.shape, jnp.int32),
             shape(b_proj.shape, bf16),
@@ -364,62 +407,63 @@
             shape(c_proj.shape, bf16),
             shape((rows, width), bf16),
             shape((1, width), f32),
+        ]
+        + [shape((2 * rows, WIDE), bf16)] * 2,
+        (me, decay_rates, skip_gain, decay_codes, b_proj, mixer_input, c_proj)
+        + (gate_input, norm_gain.reshape(1, width), queries, keys),
+        "shhhhhhhhhh",
+        [
+            pltpu.SMEM((heads,), f32),
+            pltpu.SMEM((heads,), f32),
+            pltpu.SemaphoreType.DMA((12,)),
         ],
-        (me, decay_rates, skip_gain, queries, keys, decay_codes, b_proj, mixer_input, c_proj)
-        + (gate_input, norm_gain.reshape(1, width)),
-        "ssshhhhhhhh",
-        [pltpu.SemaphoreType.DMA((6 + 2 * CHIPS,))],
-        flops=2 * rows * HD * width,
-        moved=10 * rows * width,
     )
     other = swapped(state)
-    qk = exchange(qk)
+    qk_two = shifted(qk_two, 2)
     own, lead = call(
         within_kernel,
         [shape((rows, width), f32)] * 2,
         (slope, skips, codes, b, x, c, gate),
         "",
-        flops=4 * rows * rows * width,
-        moved=12 * rows * width,
-        exps=heads * rows * rows,
-    )
-    small = dict(flops=4 * HD * width, moved=4 * HD * width)
-    chip_state = call(chip_kernel, half_state, (me, slope, state, other), "s", **small)
+    )
+    chip_state = call(chip_kernel, half_state, (me, slope, state, other), "s")
     chip_other = lax.ppermute(chip_state, "seq", [(i, i ^ 2) for i in range(n)])
     two_chips = call(
-        two_chips_kernel, half_state, (me, own, slope, chip_state, chip_other), "sa", **small
+        two_chips_kernel, half_state, (me, own, qk_two, slope, chip_state, chip_other), "saa"
     )
     far = lax.ppermute(two_chips, "seq", [(i, i + 4) for i in range(n // 2)])
+    qk_one, qk_three = call(
+        qk_kernel,
+        [shape((2 * rows, WIDE), bf16)] * 2,
+        (me, far, queries, keys),
+        "sahh",
+        [pltpu.SemaphoreType.DMA((4,))],
+    )
+    qk = [qk_own, shifted(qk_one, 1), qk_two, shifted(qk_three, 3)]
     ahead = call(
-        ahead_kernel, shape((HD, width // 2), bf16), (me, slope, chip_other, far), "s", **small
+        ahead_kernel, shape((HD, width // 2), bf16), (me, slope, chip_other, far), "s"
     )
     gated, squares = call(
         gated_kernel,
         [shape((rows, width), f32), shape((8, rows), f32)],
         (me, slope, other, ahead, swapped(ahead), own, lead, c),
         "s",
-        flops=4 * rows * HD * width,
-        moved=14 * rows * width,
     )
     squares = [squares] + [
         lax.ppermute(squares, "head", [(i, (i + k) % m) for i in range(m)]) for k in range(1, m)
     ]
     mamba_out, *values = call(
         functools.partial(norm_kernel, width * m),
-        [shape((rows, width), bf16)] + [chunk] * CHIPS,
+        [jax.ShapeDtypeStruct((rows, width), bf16)] + [chunk] * CHIPS,
         (me, gain, gated, *squares),
         "s",
-        flops=4 * rows * width,
-        moved=8 * rows * width,
     )
     values = exchange(values)
-    other_values = [swapped(part) for part in values]
     own_keys = call(
         keys_kernel,
         shape((CHIPS * rows, WIDE), bf16),
         (me, values[0], *qk),
         "sa",
-        moved=4 * rows * width,
     )
     weights = call(
         weights_kernel,
@@ -427,26 +471,29 @@
         (me, own_keys, swapped(own_keys), *qk),
         "s",
         [pltpu.VMEM((CHIPS * rows, WIDE), bf16)],
-        flops=n * n * rows * rows * HD,
-        moved=2 * n * n * rows * rows,
-        exps=n * n * rows * rows // 2,
         limit=24 * MIB,
+    )
+    passed = [call(passed_kernel, chunk, (weights, part), "a") for part in values[1:]]
+    other_values = [swapped(part) for part in (values[0], *passed)]
+    partial_sums = call(
+        own_values_kernel,
+        shape((CHIPS * rows, WIDE), f32),
+        (me, weights, *values),
+        "s",
+        [pltpu.VMEM((CHIPS * rows, WIDE), bf16)],
     )
     results = call(
         values_kernel,
         [chunk] * CHIPS,
-        (me, weights, *values, *other_values),
+        (me, partial_sums, weights, *other_values),
         "s",
-        [pltpu.VMEM((n * rows, WIDE), bf16), pltpu.VMEM((CHIPS * rows, WIDE), bf16)],
-        flops=n * n * rows * rows * HD,
-        moved=2 * n * n * rows * rows,
+        [pltpu.VMEM((CHIPS * rows, WIDE), bf16), pltpu.VMEM((CHIPS * rows, WIDE), bf16)],
     )
     attn_out = call(
         join_kernel,
-        shape((rows, width), bf16),
+        jax.ShapeDtypeStruct((rows, width), bf16),
         (me, *exchange(results)),
         "s",
-        moved=4 * rows * width,
     )
     return (mamba_out, attn_out)
 

time: 81.4 us -> 75.5 us (0.928)
  starting transfers between devices: 35.5 us -> 28.9 us
  waiting for transfers between devices: 29.4 us -> 31 us
  local copies, waits for them, and re-layouts: 1.3 us -> 0 us
  Pallas kernels: 13.6 us -> 14.5 us
    ppermute x1, starting transfers between devices: 4.66 us -> 1.46 us  [two_heads_each(): far = lax.ppermute(two_chips, 'seq', [(i, i + 4) for i in range(n // 2)])]
    ppermute x1, waiting for transfers between devices: 0.21 us -> 3.22 us  [two_heads_each(): far = lax.ppermute(two_chips, 'seq', [(i, i + 4) for i in range(n // 2)])]
    ppermute x9, waiting for transfers between devices: 21.2 us -> 24.1 us  [shifted(): return lax.ppermute(part, 'seq', [(i, (i + 2 * d) % n) for i in range(n)])]
    ppermute x9, starting transfers between devices: 22.1 us -> 19.5 us  [shifted(): return lax.ppermute(part, 'seq', [(i, (i + 2 * d) % n) for i in range(n)])]
    ppermute x1, waiting for transfers between devices: 1.86 us -> 0.01 us  [two_heads_each(): chip_other = lax.ppermute(chip_state, 'seq', [(i, i ^ 2) for i in range(n)])]
    ppermute x3, waiting for transfers between devices: 3.64 us -> 2.22 us  [two_heads_each(): lax.ppermute(squares, 'head', [(i, (i + k) % m) for i in range(m)])]
    ppermute x1, starting transfers between devices: 3.01 us -> 1.64 us  [two_heads_each(): chip_other = lax.ppermute(chip_state, 'seq', [(i, i ^ 2) for i in range(n)])]
    unnamed x4 -> x0, local copies, waits for them, and re-layouts: 1.3 us -> none
  transfers between devices with their start and end apart: 21 -> 21, of which waited for: 11 -> 10; matrix products, arithmetic and copies ran while one was open for 0% -> 0% of each run, Pallas kernels for 10% -> 12%
where the time goes in v3:
time: 75.5 us; the launch traced here: 75.2 us
  waiting for transfers between devices  31 us (41%)
  starting transfers between devices  28.9 us (38%)
  Pallas kernels  14.5 us (19%)
  between operations  0.81 us (1%)
    ppermute x9, waiting for transfers between devices, shifted(): return lax.ppermute(part, 'seq', [(i, (i + 2 * d) % n) for i in range(n)])  24.1 us
    ppermute x9, starting transfers between devices, shifted(): return lax.ppermute(part, 'seq', [(i, (i + 2 * d) % n) for i in range(n)])  19.5 us
    pallas_call x16, Pallas kernels, call(): pl.pallas_call(body, out_shape=outs, in_specs=[kinds[space] for space in...  14.5 us
    ppermute x3, starting transfers between devices, two_heads_each(): lax.ppermute(squares, 'head', [(i, (i + k) % m) for i in range(m)])  4.49 us
    ppermute x1, waiting for transfers between devices, two_heads_each(): far = lax.ppermute(two_chips, 'seq', [(i, i + 4) for i in range(n // 2)])  3.22 us
    ppermute x3, waiting for transfers between devices, two_heads_each(): lax.ppermute(squares, 'head', [(i, (i + k) % m) for i in range(m)])  2.22 us
    ppermute x7, starting transfers between devices, swapped(): return lax.ppermute(part, 'seq', [(i, i ^ 1) for i in range(2 * CHIPS)])  1.85 us
    ppermute x1, starting transfers between devices, two_heads_each(): chip_other = lax.ppermute(chip_state, 'seq', [(i, i ^ 2) for i in range(n)])  1.64 us
  transfers between devices with their start and end apart: 21, of which 10 were waited for; matrix products, arithmetic and copies ran while one was open for 0% of the time, Pallas kernels for 12%

profile of v3, /device:TPU:0, one launch (start us, length us, event | category | flops | bytes accessed | tf_op | source)
XLA Modules:
  0.0 75.2 jit_solution(1098526585356656102)
XLA Ops:
  0.6 2.1 %shard_map.113 = (bf16[144,1024]{1,0:T(8,128)(2,1)S(1)}, f32[8,1024]{1,0:T(8,128)S(1)}, f32[8,1024]{1,0:T(8,128)S(1)}, s32[16,256]{1,0:T(8,128)S(1)}, bf16[256,1...) custom-call(s32[1]{0:T(128)} %bitcast.me_ref, ...), custom_call_target="tpu_custom_call" | custom-call | tf_op jit(solution)/shard_map/pallas_call | solution.py:34
  2.8 0.5 collective-permute-start
  3.3 3.7 %collective-permute-start.2 = (bf16[512,256]{1,0:T(8,128)(2,1)S(1)}, bf16[512,256]{1,0:T(8,128)(2,1)S(1)}, u32[]{:S(2)}, u32[]{:S(2)}) collective-permute-start(bf16[512,256]{1,0:T(8,128)(2,1)S(1)} %get-tuple-element.38), channel_id=1, source_target_pairs={{0,16},{4,20},{8,24},{12,28},{16,0},{20,4},{24,8},{28,12},{1,17},{... | collective-permute-start | bytes 786440 | tf_op jit(solution)/shard_map/ppermute | solution.py:368
  7.0 0.0 collective-permute-done.other_ref.local_ref
  7.0 0.1 shard_map.114.own_ref
  7.0 1.6 %collective-permute-start.1 = (bf16[144,512]{1,0:T(8,128)(2,1)S(1)}, bf16[144,512]{1,0:T(8,128)(2,1)S(1)}, u32[]{:S(2)}, u32[]{:S(2)}) collective-permute-start(bf16[144,512]{1,0:T(8,128)(2,1)S(1)} %shard_map.114.own_ref), channel_id=1, source_target_pairs={{0,8},{4,12},{8,0},{12,4},{16,24},{20,28},{24,16},{28,20},{1,9},{5... | collective-permute-start | bytes 442376 | tf_op jit(solution)/shard_map/ppermute | solution.py:430
  8.7 2.3 %shard_map.115 = (f32[256,1024]{1,0:T(8,128)S(1)}, f32[256,1024]{1,0:T(8,128)S(1)}) custom-call(f32[8,1024]{1,0:T(8,128)S(1)} %get-tuple-element.29.slope_ref, f32[8,1024]{1,0:T(8,128)S(1)} %get-tuple-element.31.skips_ref, s32[16,256]{1,0:T(8,128)S(1)} %get-tuple-element.32.codes_ref, bf16[256,128]{1,0:T(8,128)(2,1)S(1)} %get-tuple-element.33.b_ref, ...), custom_call_target="tpu_custom_call" | custom-call | tf_op jit(solution)/shard_map/pallas_call | solution.py:34
  11.0 8.5 %collective-permute-done.2.also_ref.rest_2_ = bf16[512,256]{1,0:T(8,128)(2,1)S(1)} collective-permute-done((bf16[512,256]{1,0:T(8,128)(2,1)S(1)}, bf16[512,256]{1,0:T(8,128)(2,1)S(1)}, u32[]{:S(2)}, u32[]{:S(2)}) %collective-permute-start.2) | collective-permute-done | bytes 262176 | tf_op jit(solution)/shard_map/ppermute | solution.py:368
  19.5 0.0 collective-permute-done.1.other_ref
  19.5 0.1 shard_map.116
  19.6 1.5 %collective-permute-start.3 = (bf16[144,512]{1,0:T(8,128)(2,1)S(1)}, bf16[144,512]{1,0:T(8,128)(2,1)S(1)}, u32[]{:S(2)}, u32[]{:S(2)}) collective-permute-start(bf16[144,512]{1,0:T(8,128)(2,1)S(1)} %shard_map.116), channel_id=1, source_target_pairs={{0,16},{4,20},{8,24},{12,28},{1,17},{5,21},{9,25},{13,29},{2,18},{... | collective-permute-start | bytes 442376 | tf_op jit(solution)/shard_map/ppermute | solution.py:434
  21.0 3.2 %collective-permute-done.3.far_ref.after_ref = bf16[144,512]{1,0:T(8,128)(2,1)S(1)} collective-permute-done((bf16[144,512]{1,0:T(8,128)(2,1)S(1)}, bf16[144,512]{1,0:T(8,128)(2,1)S(1)}, u32[]{:S(2)}, u32[]{:S(2)}) %collective-permute-start.3) | collective-permute-done | bytes 147488 | tf_op jit(solution)/shard_map/ppermute | solution.py:434
  24.2 1.1 %shard_map.120 = (bf16[512,256]{1,0:T(8,128)(2,1)S(1)}, bf16[512,256]{1,0:T(8,128)(2,1)S(1)}) custom-call(s32[1]{0:T(128)} %bitcast.me_ref, bf16[144,512]{1,0:T(8,128)(2,1)S(1)} %collective-permute-done.3.far_ref.after_ref, bf16[256,1024]{1,0:T(8,128)(2,1)} %q_hbm.3, bf16[256,1024]{1,0:T(8,128)(2,1)} %k_hbm.3), custom_call_target="tpu_custom_call" | custom-call | tf_op jit(solution)/shard_map/pallas_call | solution.py:34
  25.4 4.7 %collective-permute-start.8 = (bf16[512,256]{1,0:T(8,128)(2,1)S(1)}, bf16[512,256]{1,0:T(8,128)(2,1)S(1)}, u32[]{:S(2)}, u32[]{:S(2)}) collective-permute-start(bf16[512,256]{1,0:T(8,128)(2,1)S(1)} %get-tuple-element.45), channel_id=1, source_target_pairs={{0,8},{4,12},{8,16},{12,20},{16,24},{20,28},{24,0},{28,4},{1,9},{5... | collective-permute-start | bytes 786440 | tf_op jit(solution)/shard_map/ppermute | solution.py:368
  30.1 2.9 %collective-permute-start.9 = (bf16[512,256]{1,0:T(8,128)(2,1)S(1)}, bf16[512,256]{1,0:T(8,128)(2,1)S(1)}, u32[]{:S(2)}, u32[]{:S(2)}) collective-permute-start(bf16[512,256]{1,0:T(8,128)(2,1)S(1)} %get-tuple-element.46), channel_id=1, source_target_pairs={{0,24},{4,28},{8,0},{12,4},{16,8},{20,12},{24,16},{28,20},{1,25},{... | collective-permute-start | bytes 786440 | tf_op jit(solution)/shard_map/ppermute | solution.py:368
  33.0 0.1 shard_map.117.ahead_ref
  33.0 0.1 collective-permute-start.4
  33.1 1.3 %collective-permute-done.4.other_ref = bf16[128,512]{1,0:T(8,128)(2,1)S(1)} collective-permute-done((bf16[128,512]{1,0:T(8,128)(2,1)S(1)}, bf16[128,512]{1,0:T(8,128)(2,1)S(1)}, u32[]{:S(2)}, u32[]{:S(2)}) %collective-permute-start.4) | collective-permute-done | bytes 131104 | tf_op jit(solution)/shard_map/ppermute | solution.py:376
  34.5 1.1 %shard_map.118 = (f32[256,1024]{1,0:T(8,128)S(1)}, f32[8,256]{1,0:T(8,128)S(1)}) custom-call(s32[1]{0:T(128)} %bitcast.me_ref, f32[8,1024]{1,0:T(8,128)S(1)} %get-tuple-element.29.slope_ref, bf16[144,1024]{1,0:T(8,128)(2,1)S(1)} %collective-permute-done.other_ref.local_ref, bf16[128,512]{1,0:T(8,128)(2,1)S(1)} %shard_map.117.ahead_ref, ...), custom_call_target="tpu_custom_call" | custom-call | tf_op jit(solution)/shard_map/pallas_call | solution.py:34
  35.6 1.5 %collective-permute-start.5 = (f32[8,256]{1,0:T(8,128)S(1)}, f32[8,256]{1,0:T(8,128)S(1)}, u32[]{:S(2)}, u32[]{:S(2)}) collective-permute-start(f32[8,256]{1,0:T(8,128)S(1)} %get-tuple-element.41.rest_0_), channel_id=1, source_target_pairs={{0,1},{1,2},{2,3},{3,0},{4,5},{5,6},{6,7},{7,4},{8,9},{9,10},{10,1... | collective-permute-start | bytes 24584 | tf_op jit(solution)/shard_map/ppermute | solution.py:453
  37.1 1.5 %collective-permute-start.6 = (f32[8,256]{1,0:T(8,128)S(1)}, f32[8,256]{1,0:T(8,128)S(1)}, u32[]{:S(2)}, u32[]{:S(2)}) collective-permute-start(f32[8,256]{1,0:T(8,128)S(1)} %get-tuple-element.41.rest_0_), channel_id=1, source_target_pairs={{0,2},{1,3},{2,0},{3,1},{4,6},{5,7},{6,4},{7,5},{8,10},{9,11},{10,... | collective-permute-start | bytes 24584 | tf_op jit(solution)/shard_map/ppermute | solution.py:453
  38.6 1.4 %collective-permute-start.7 = (f32[8,256]{1,0:T(8,128)S(1)}, f32[8,256]{1,0:T(8,128)S(1)}, u32[]{:S(2)}, u32[]{:S(2)}) collective-permute-start(f32[8,256]{1,0:T(8,128)S(1)} %get-tuple-element.41.rest_0_), channel_id=1, source_target_pairs={{0,3},{1,0},{2,1},{3,2},{4,7},{5,4},{6,5},{7,6},{8,11},{9,8},{10,9... | collective-permute-start | bytes 24584 | tf_op jit(solution)/shard_map/ppermute | solution.py:453
  40.1 0.1 collective-permute-done.5.rest_1_
  40.2 0.6 collective-permute-done.6.rest_2_
  40.8 1.5 %collective-permute-done.7.rest_3_ = f32[8,256]{1,0:T(8,128)S(1)} collective-permute-done((f32[8,256]{1,0:T(8,128)S(1)}, f32[8,256]{1,0:T(8,128)S(1)}, u32[]{:S(2)}, u32[]{:S(2)}) %collective-permute-start.7) | collective-permute-done | bytes 8224 | tf_op jit(solution)/shard_map/ppermute | solution.py:453
  42.3 1.0 %shard_map.119 = (bf16[256,1024]{1,0:T(8,128)(2,1)}, bf16[256,256]{1,0:T(8,128)(2,1)S(1)}, bf16[256,256]{1,0:T(8,128)(2,1)S(1)}, bf16[256,256]{1,0:T(8,128)(2,1)S(1)}, bf16[256,256]{1,0:T(8,128)(2,1)S(1)}) custom-call(s32[1]{0:T(128)} %bitcast.me_ref, f32[1,1024]{1,0:T(1,128)S(1)} %get-tuple-element.28.gain_ref, ...), custom_call_target="tpu_custom_call" | custom-call | tf_op jit(solution)/shard_map/pallas_call | solution.py:34
  43.3 0.0 collective-permute-done.8.rest_1_
  43.3 0.0 collective-permute-done.9.rest_3_
  43.3 0.1 collective-permute-start.10
  43.4 2.8 %collective-permute-start.13 = (bf16[256,256]{1,0:T(8,128)(2,1)S(1)}, bf16[256,256]{1,0:T(8,128)(2,1)S(1)}, u32[]{:S(2)}, u32[]{:S(2)}) collective-permute-start(bf16[256,256]{1,0:T(8,128)(2,1)S(1)} %get-tuple-element.49), channel_id=1, source_target_pairs={{0,24},{4,28},{8,0},{12,4},{16,8},{20,12},{24,16},{28,20},{1,25},{... | collective-permute-start | bytes 393224 | tf_op jit(solution)/shard_map/ppermute | solution.py:368
  46.1 0.3 collective-permute-start.12
  46.4 0.6 collective-permute-start.11
  47.0 0.0 collective-permute-start.14
  47.0 0.0 collective-permute-done.10.other_ref
  47.0 3.8 %shard_map.122.weights_ref.after_ref = bf16[2,1024,2048]{2,1,0:T(8,128)(2,1)S(1)} custom-call(s32[1]{0:T(128)} %bitcast.me_ref, bf16[1024,256]{1,0:T(8,128)(2,1)S(1)} %shard_map.121.own_ref, bf16[1024,256]{1,0:T(8,128)(2,1)S(1)} %collective-permute-done.10.other_ref, bf16[512,256]{1,0:T(8,128)(2,1)S(1)} %get-tuple-element.44.rest_0_, ...), custom_call_target="tpu_custom_call" | custom-call | tf_op jit(solution)/shard_map/pallas_call | solution.py:34
  50.8 0.0 collective-permute-done.13.rest_3_.in_ref
  50.9 0.6 collective-permute-start.17
  51.4 7.2 %collective-permute-done.12.rest_2_.in_ref = bf16[256,256]{1,0:T(8,128)(2,1)S(1)} collective-permute-done((bf16[256,256]{1,0:T(8,128)(2,1)S(1)}, bf16[256,256]{1,0:T(8,128)(2,1)S(1)}, u32[]{:S(2)}, u32[]{:S(2)}) %collective-permute-start.12) | collective-permute-done | bytes 131104 | tf_op jit(solution)/shard_map/ppermute | solution.py:368
  58.7 0.1 collective-permute-start.16
  58.8 0.0 collective-permute-done.11.rest_1_.in_ref
  58.8 0.5 collective-permute-start.15
  59.3 0.9 %shard_map.123.partial_ref = f32[1024,256]{1,0:T(8,128)S(1)} custom-call(s32[1]{0:T(128)} %bitcast.me_ref, bf16[2,1024,2048]{2,1,0:T(8,128)(2,1)S(1)} %shard_map.122.weights_ref.after_ref, bf16[256,256]{1,0:T(8,128)(2,1)S(1)} %get-tuple-element.43.after_ref.rest_0_, bf16[256,256]{1,0:T(8,128)(2,1)S(1)} %collective-permute-done.11.rest_1_.in_ref, ...), custom_call_target="tpu_custom_call" | custom-call | tf_op jit(solution)/shard_map/pallas_call | solution.py:34
  60.2 0.0 collective-permute-done.14.rest_0_
  60.2 0.0 collective-permute-done.17.rest_3_
  60.3 0.0 collective-permute-done.16.rest_2_
  60.3 0.1 collective-permute-done.15.rest_1_
  60.3 1.0 %shard_map.127 = (bf16[256,256]{1,0:T(8,128)(2,1)S(1)}, bf16[256,256]{1,0:T(8,128)(2,1)S(1)}, bf16[256,256]{1,0:T(8,128)(2,1)S(1)}, bf16[256,256]{1,0:T(8,128)(2,1)S(1)}) custom-call(s32[1]{0:T(128)} %bitcast.me_ref, f32[1024,256]{1,0:T(8,128)S(1)} %shard_map.123.partial_ref, bf16[2,1024,2048]{2,1,0:T(8,128)(2,1)S(1)} %shard_map.122.weights_ref.after_ref, ...), custom_call_target="tpu_custom_call" | custom-call | tf_op jit(solution)/shard_map/pallas_call | solution.py:34
  61.3 0.1 collective-permute-start.18
  61.4 1.7 %collective-permute-start.19 = (bf16[256,256]{1,0:T(8,128)(2,1)S(1)}, bf16[256,256]{1,0:T(8,128)(2,1)S(1)}, u32[]{:S(2)}, u32[]{:S(2)}) collective-permute-start(bf16[256,256]{1,0:T(8,128)(2,1)S(1)} %get-tuple-element.52), channel_id=1, source_target_pairs={{0,16},{4,20},{8,24},{12,28},{16,0},{20,4},{24,8},{28,12},{1,17},{... | collective-permute-start | bytes 393224 | tf_op jit(solution)/shard_map/ppermute | solution.py:368
  63.1 2.8 %collective-permute-start.20 = (bf16[256,256]{1,0:T(8,128)(2,1)S(1)}, bf16[256,256]{1,0:T(8,128)(2,1)S(1)}, u32[]{:S(2)}, u32[]{:S(2)}) collective-permute-start(bf16[256,256]{1,0:T(8,128)(2,1)S(1)} %get-tuple-element.53), channel_id=1, source_target_pairs={{0,24},{4,28},{8,0},{12,4},{16,8},{20,12},{24,16},{28,20},{1,25},{... | collective-permute-start | bytes 393224 | tf_op jit(solution)/shard_map/ppermute | solution.py:368
  65.9 3.7 %collective-permute-done.18.rest_1_ = bf16[256,256]{1,0:T(8,128)(2,1)S(1)} collective-permute-done((bf16[256,256]{1,0:T(8,128)(2,1)S(1)}, bf16[256,256]{1,0:T(8,128)(2,1)S(1)}, u32[]{:S(2)}, u32[]{:S(2)}) %collective-permute-start.18) | collective-permute-done | bytes 131104 | tf_op jit(solution)/shard_map/ppermute | solution.py:368
  69.6 4.7 %collective-permute-done.19.rest_2_ = bf16[256,256]{1,0:T(8,128)(2,1)S(1)} collective-permute-done((bf16[256,256]{1,0:T(8,128)(2,1)S(1)}, bf16[256,256]{1,0:T(8,128)(2,1)S(1)}, u32[]{:S(2)}, u32[]{:S(2)}) %collective-permute-start.19) | collective-permute-done | bytes 131104 | tf_op jit(solution)/shard_map/ppermute | solution.py:368
  74.3 0.0 collective-permute-done.20.rest_3_
  74.3 0.9 %shard_map.128 = bf16[256,1024]{1,0:T(8,128)(2,1)} custom-call(s32[1]{0:T(128)} %bitcast.me_ref, bf16[256,256]{1,0:T(8,128)(2,1)S(1)} %get-tuple-element.50.rest_0_, bf16[256,256]{1,0:T(8,128)(2,1)S(1)} %collective-permute-done.18.rest_1_, bf16[256,256]{1,0:T(8,128)(2,1)S(1)} %collective-permute-done.19.rest_2_, ...), custom_call_target="tpu_custom_call" | custom-call | tf_op jit(solution)/shard_map/pallas_call | solution.py:34
  (4 shorter events, 0.1 us)
Async XLA Ops:
  2.8 4.2 %collective-permute-start = (bf16[144,1024]{1,0:T(8,128)(2,1)S(1)}, bf16[144,1024]{1,0:T(8,128)(2,1)S(1)}, u32[]{:S(2)}, u32[]{:S(2)}) collective-permute-start(bf16[144,1024]{1,0:T(8,128)(2,1)S(1)} %get-tuple-element.30.own_ref), channel_id=1, source_target_pairs={{0,4},{4,0},{8,12},{12,8},{16,20},{20,16},{24,28},{28,24},{1,5},{5... | collective-permute-start | bytes 884744 | tf_op jit(solution)/shard_map/ppermute | solution.py:376
  3.3 16.2 %collective-permute-start.2 = (bf16[512,256]{1,0:T(8,128)(2,1)S(1)}, bf16[512,256]{1,0:T(8,128)(2,1)S(1)}, u32[]{:S(2)}, u32[]{:S(2)}) collective-permute-start(bf16[512,256]{1,0:T(8,128)(2,1)S(1)} %get-tuple-element.38), channel_id=1, source_target_pairs={{0,16},{4,20},{8,24},{12,28},{16,0},{20,4},{24,8},{28,12},{1,17},{... | collective-permute-start | bytes 786440 | tf_op jit(solution)/shard_map/ppermute | solution.py:368
  7.0 12.4 %collective-permute-start.1 = (bf16[144,512]{1,0:T(8,128)(2,1)S(1)}, bf16[144,512]{1,0:T(8,128)(2,1)S(1)}, u32[]{:S(2)}, u32[]{:S(2)}) collective-permute-start(bf16[144,512]{1,0:T(8,128)(2,1)S(1)} %shard_map.114.own_ref), channel_id=1, source_target_pairs={{0,8},{4,12},{8,0},{12,4},{16,24},{20,28},{24,16},{28,20},{1,9},{5... | collective-permute-start | bytes 442376 | tf_op jit(solution)/shard_map/ppermute | solution.py:430
  19.6 4.7 %collective-permute-start.3 = (bf16[144,512]{1,0:T(8,128)(2,1)S(1)}, bf16[144,512]{1,0:T(8,128)(2,1)S(1)}, u32[]{:S(2)}, u32[]{:S(2)}) collective-permute-start(bf16[144,512]{1,0:T(8,128)(2,1)S(1)} %shard_map.116), channel_id=1, source_target_pairs={{0,16},{4,20},{8,24},{12,28},{1,17},{5,21},{9,25},{13,29},{2,18},{... | collective-permute-start | bytes 442376 | tf_op jit(solution)/shard_map/ppermute | solution.py:434
  25.4 17.9 %collective-permute-start.8 = (bf16[512,256]{1,0:T(8,128)(2,1)S(1)}, bf16[512,256]{1,0:T(8,128)(2,1)S(1)}, u32[]{:S(2)}, u32[]{:S(2)}) collective-permute-start(bf16[512,256]{1,0:T(8,128)(2,1)S(1)} %get-tuple-element.45), channel_id=1, source_target_pairs={{0,8},{4,12},{8,16},{12,20},{16,24},{20,28},{24,0},{28,4},{1,9},{5... | collective-permute-start | bytes 786440 | tf_op jit(solution)/shard_map/ppermute | solution.py:368
  30.1 13.2 %collective-permute-start.9 = (bf16[512,256]{1,0:T(8,128)(2,1)S(1)}, bf16[512,256]{1,0:T(8,128)(2,1)S(1)}, u32[]{:S(2)}, u32[]{:S(2)}) collective-permute-start(bf16[512,256]{1,0:T(8,128)(2,1)S(1)} %get-tuple-element.46), channel_id=1, source_target_pairs={{0,24},{4,28},{8,0},{12,4},{16,8},{20,12},{24,16},{28,20},{1,25},{... | collective-permute-start | bytes 786440 | tf_op jit(solution)/shard_map/ppermute | solution.py:368
  33.0 1.4 %collective-permute-start.4 = (bf16[128,512]{1,0:T(8,128)(2,1)S(1)}, bf16[128,512]{1,0:T(8,128)(2,1)S(1)}, u32[]{:S(2)}, u32[]{:S(2)}) collective-permute-start(bf16[128,512]{1,0:T(8,128)(2,1)S(1)} %shard_map.117.ahead_ref), channel_id=1, source_target_pairs={{0,4},{4,0},{8,12},{12,8},{16,20},{20,16},{24,28},{28,24},{1,5},{5... | collective-permute-start | bytes 393224 | tf_op jit(solution)/shard_map/ppermute | solution.py:376
  35.6 4.6 %collective-permute-start.5 = (f32[8,256]{1,0:T(8,128)S(1)}, f32[8,256]{1,0:T(8,128)S(1)}, u32[]{:S(2)}, u32[]{:S(2)}) collective-permute-start(f32[8,256]{1,0:T(8,128)S(1)} %get-tuple-element.41.rest_0_), channel_id=1, source_target_pairs={{0,1},{1,2},{2,3},{3,0},{4,5},{5,6},{6,7},{7,4},{8,9},{9,10},{10,1... | collective-permute-start | bytes 24584 | tf_op jit(solution)/shard_map/ppermute | solution.py:453
  37.1 3.7 %collective-permute-start.6 = (f32[8,256]{1,0:T(8,128)S(1)}, f32[8,256]{1,0:T(8,128)S(1)}, u32[]{:S(2)}, u32[]{:S(2)}) collective-permute-start(f32[8,256]{1,0:T(8,128)S(1)} %get-tuple-element.41.rest_0_), channel_id=1, source_target_pairs={{0,2},{1,3},{2,0},{3,1},{4,6},{5,7},{6,4},{7,5},{8,10},{9,11},{10,... | collective-permute-start | bytes 24584 | tf_op jit(solution)/shard_map/ppermute | solution.py:453
  38.6 3.7 %collective-permute-start.7 = (f32[8,256]{1,0:T(8,128)S(1)}, f32[8,256]{1,0:T(8,128)S(1)}, u32[]{:S(2)}, u32[]{:S(2)}) collective-permute-start(f32[8,256]{1,0:T(8,128)S(1)} %get-tuple-element.41.rest_0_), channel_id=1, source_target_pairs={{0,3},{1,0},{2,1},{3,2},{4,7},{5,4},{6,5},{7,6},{8,11},{9,8},{10,9... | collective-permute-start | bytes 24584 | tf_op jit(solution)/shard_map/ppermute | solution.py:453
  43.3 3.7 %collective-permute-start.10 = (bf16[1024,256]{1,0:T(8,128)(2,1)S(1)}, bf16[1024,256]{1,0:T(8,128)(2,1)S(1)}, u32[]{:S(2)}, u32[]{:S(2)}) collective-permute-start(bf16[1024,256]{1,0:T(8,128)(2,1)S(1)} %shard_map.121.own_ref), channel_id=1, source_target_pairs={{0,4},{4,0},{8,12},{12,8},{16,20},{20,16},{24,28},{28,24},{1,5},{5... | collective-permute-start | bytes 1572872 | tf_op jit(solution)/shard_map/ppermute | solution.py:376
  43.4 7.5 %collective-permute-start.13 = (bf16[256,256]{1,0:T(8,128)(2,1)S(1)}, bf16[256,256]{1,0:T(8,128)(2,1)S(1)}, u32[]{:S(2)}, u32[]{:S(2)}) collective-permute-start(bf16[256,256]{1,0:T(8,128)(2,1)S(1)} %get-tuple-element.49), channel_id=1, source_target_pairs={{0,24},{4,28},{8,0},{12,4},{16,8},{20,12},{24,16},{28,20},{1,25},{... | collective-permute-start | bytes 393224 | tf_op jit(solution)/shard_map/ppermute | solution.py:368
  46.1 12.5 %collective-permute-start.12 = (bf16[256,256]{1,0:T(8,128)(2,1)S(1)}, bf16[256,256]{1,0:T(8,128)(2,1)S(1)}, u32[]{:S(2)}, u32[]{:S(2)}) collective-permute-start(bf16[256,256]{1,0:T(8,128)(2,1)S(1)} %get-tuple-element.48), channel_id=1, source_target_pairs={{0,16},{4,20},{8,24},{12,28},{16,0},{20,4},{24,8},{28,12},{1,17},{... | collective-permute-start | bytes 393224 | tf_op jit(solution)/shard_map/ppermute | solution.py:368
  46.4 12.3 %collective-permute-start.11 = (bf16[256,256]{1,0:T(8,128)(2,1)S(1)}, bf16[256,256]{1,0:T(8,128)(2,1)S(1)}, u32[]{:S(2)}, u32[]{:S(2)}) collective-permute-start(bf16[256,256]{1,0:T(8,128)(2,1)S(1)} %get-tuple-element.47), channel_id=1, source_target_pairs={{0,8},{4,12},{8,16},{12,20},{16,24},{20,28},{24,0},{28,4},{1,9},{5... | collective-permute-start | bytes 393224 | tf_op jit(solution)/shard_map/ppermute | solution.py:368
  47.0 13.2 %collective-permute-start.14 = (bf16[256,256]{1,0:T(8,128)(2,1)S(1)}, bf16[256,256]{1,0:T(8,128)(2,1)S(1)}, u32[]{:S(2)}, u32[]{:S(2)}) collective-permute-start(bf16[256,256]{1,0:T(8,128)(2,1)S(1)} %get-tuple-element.43.after_ref.rest_0_), channel_id=1, source_target_pairs={{0,4},{4,0},{8,12},{12,8},{16,20},{20,16},{24,28},{28,24},{1,5},{5... | collective-permute-start | bytes 393224 | tf_op jit(solution)/shard_map/ppermute | solution.py:376
  50.9 9.4 %collective-permute-start.17 = (bf16[256,256]{1,0:T(8,128)(2,1)S(1)}, bf16[256,256]{1,0:T(8,128)(2,1)S(1)}, u32[]{:S(2)}, u32[]{:S(2)}) collective-permute-start(bf16[256,256]{1,0:T(8,128)(2,1)S(1)} %shard_map.126), channel_id=1, source_target_pairs={{0,4},{4,0},{8,12},{12,8},{16,20},{20,16},{24,28},{28,24},{1,5},{5... | collective-permute-start | bytes 393224 | tf_op jit(solution)/shard_map/ppermute | solution.py:376
  58.7 1.6 %collective-permute-start.16 = (bf16[256,256]{1,0:T(8,128)(2,1)S(1)}, bf16[256,256]{1,0:T(8,128)(2,1)S(1)}, u32[]{:S(2)}, u32[]{:S(2)}) collective-permute-start(bf16[256,256]{1,0:T(8,128)(2,1)S(1)} %shard_map.125), channel_id=1, source_target_pairs={{0,4},{4,0},{8,12},{12,8},{16,20},{20,16},{24,28},{28,24},{1,5},{5... | collective-permute-start | bytes 393224 | tf_op jit(solution)/shard_map/ppermute | solution.py:376
  58.8 1.5 %collective-permute-start.15 = (bf16[256,256]{1,0:T(8,128)(2,1)S(1)}, bf16[256,256]{1,0:T(8,128)(2,1)S(1)}, u32[]{:S(2)}, u32[]{:S(2)}) collective-permute-start(bf16[256,256]{1,0:T(8,128)(2,1)S(1)} %shard_map.124), channel_id=1, source_target_pairs={{0,4},{4,0},{8,12},{12,8},{16,20},{20,16},{24,28},{28,24},{1,5},{5... | collective-permute-start | bytes 393224 | tf_op jit(solution)/shard_map/ppermute | solution.py:376
  61.3 8.3 %collective-permute-start.18 = (bf16[256,256]{1,0:T(8,128)(2,1)S(1)}, bf16[256,256]{1,0:T(8,128)(2,1)S(1)}, u32[]{:S(2)}, u32[]{:S(2)}) collective-permute-start(bf16[256,256]{1,0:T(8,128)(2,1)S(1)} %get-tuple-element.51), channel_id=1, source_target_pairs={{0,8},{4,12},{8,16},{12,20},{16,24},{20,28},{24,0},{28,4},{1,9},{5... | collective-permute-start | bytes 393224 | tf_op jit(solution)/shard_map/ppermute | solution.py:368
  61.4 13.0 %collective-permute-start.19 = (bf16[256,256]{1,0:T(8,128)(2,1)S(1)}, bf16[256,256]{1,0:T(8,128)(2,1)S(1)}, u32[]{:S(2)}, u32[]{:S(2)}) collective-permute-start(bf16[256,256]{1,0:T(8,128)(2,1)S(1)} %get-tuple-element.52), channel_id=1, source_target_pairs={{0,16},{4,20},{8,24},{12,28},{16,0},{20,4},{24,8},{28,12},{1,17},{... | collective-permute-start | bytes 393224 | tf_op jit(solution)/shard_map/ppermute | solution.py:368
  63.1 11.3 %collective-permute-start.20 = (bf16[256,256]{1,0:T(8,128)(2,1)S(1)}, bf16[256,256]{1,0:T(8,128)(2,1)S(1)}, u32[]{:S(2)}, u32[]{:S(2)}) collective-permute-start(bf16[256,256]{1,0:T(8,128)(2,1)S(1)} %get-tuple-element.53), channel_id=1, source_target_pairs={{0,24},{4,28},{8,0},{12,4},{16,8},{20,12},{24,16},{28,20},{1,25},{... | collective-permute-start | bytes 393224 | tf_op jit(solution)/shard_map/ppermute | solution.py:368

commit v4 on v3

--- a/solution.py
+++ b/solution.py
@@ -28,14 +28,17 @@
 PARTS = 16
 
 
-def call(body, outs, args, spaces, scratch=(), limit=16 * MIB):
+def call(body, outs, args, spaces, scratch=(), limit=16 * MIB, through=0):
     kinds = {"s": SMEM, "h": HBM, "a": ANY, "v": VMEM}
     spaces = spaces + "v" * (len(args) - len(spaces))
     return pl.pallas_call(
         body,
         out_shape=outs,
         in_specs=[kinds[space] for space in spaces],
-        out_specs=jax.tree.map(lambda _: VMEM, outs),
+        out_specs=[ANY if i >= len(outs) - through else VMEM for i in range(len(outs))]
+        if through
+        else jax.tree.map(lambda _: VMEM, outs),
+        input_output_aliases={len(args) - i: len(outs) - i for i in range(1, through + 1)},
         scratch_shapes=list(scratch),
         compiler_params=pltpu.CompilerParams(vmem_limit_bytes=limit),
         cost_estimate=pl.CostEstimate(flops=0, bytes_accessed=0, transcendentals=0),
@@ -77,8 +80,8 @@
     return lax.shift_right_logical(me, 1)
 
 
-def around(chip, by):
-    return (chip + by) & (CHIPS - 1)
+def across(chip, by):
+    return chip ^ by
 
 
 def block_of(index, size):
@@ -110,26 +113,17 @@
     rows = q_hbm.shape[0]
     pairs = []
     for d, out in zip(steps, outs):
-        cols = block_of(around(chip, d), WIDE)
+        cols = block_of(across(chip, d), WIDE)
         pairs.append((q_hbm.at[:, cols], out.at[pl.ds(0, rows), :]))
         pairs.append((k_hbm.at[:, cols], out.at[pl.ds(rows, rows), :]))
     return pairs
-
-
-def qk_kernel(me_ref, after_ref, q_hbm, k_hbm, *rest):
-    pairs = chunk_pairs(chip_of(me_ref[0]), (1, 3), q_hbm, k_hbm, rest[:2])
-    copies = [pltpu.make_async_copy(a, b, rest[2].at[i]) for i, (a, b) in enumerate(pairs)]
-    for copy in copies:
-        copy.start()
-    for copy in copies:
-        copy.wait()
 
 
 def first_kernel(
     me_ref, rates_hbm, skip_hbm, codes_hbm, b_hbm, x_hbm, c_hbm, gate_hbm, gain_hbm, q_hbm, k_hbm,
     state_ref, slope_ref, skips_ref, codes_ref, b_ref, x_ref, c_ref, gate_ref, gain_ref, *rest
 ):
-    qk, (rates_ref, skip_ref, sems) = rest[:2], rest[2:]
+    qk, (rates_ref, skip_ref, sems) = rest[:CHIPS], rest[CHIPS:]
     rows = x_ref.shape[0]
     chip = chip_of(me_ref[0])
     pairs = [
@@ -142,7 +136,7 @@
         (gate_hbm, gate_ref),
         (gain_hbm, gain_ref),
     ]
-    pairs += chunk_pairs(chip, (0, 2), q_hbm, k_hbm, qk)
+    pairs += chunk_pairs(chip, (0, 1, 2, 3), q_hbm, k_hbm, qk)
     copies = [pltpu.make_async_copy(a, b, sems.at[i]) for i, (a, b) in enumerate(pairs)]
     for copy in copies:
         copy.start()
@@ -183,7 +177,8 @@
     out_ref[pl.ds(HD, PARTS), :] = as_parts(total)
 
 
-def two_chips_kernel(me_ref, after_ref, also_ref, slope_ref, own_ref, other_ref, out_ref):
+def two_chips_kernel(me_ref, after_ref, slope_ref, own_ref, other_ref, *rest):
+    out_ref = rest[1]
     me = me_ref[0]
     odd = chip_of(me) & 1
     own, other = own_ref[...], other_ref[...]
@@ -194,7 +189,7 @@
     out_ref[pl.ds(HD, PARTS), :] = as_parts(total)
 
 
-def ahead_kernel(me_ref, slope_ref, other_ref, far_ref, out_ref):
+def ahead_kernel(me_ref, after_ref, slope_ref, other_ref, far_ref, *rest):
     me = me_ref[0]
     odd = chip_of(me) & 1
     near, total = opened(other_ref[...])
@@ -202,7 +197,7 @@
     total = jnp.where(odd == 1, total, 0.0)
     far, _ = opened(far_ref[...])
     slope = slope_ref[0:1, block_of(me & 1, near.shape[1])]
-    out_ref[...] = (jnp.exp2(total * slope) * far + near).astype(jnp.bfloat16)
+    rest[1][...] = (jnp.exp2(total * slope) * far + near).astype(jnp.bfloat16)
 
 
 def within_kernel(slope_ref, skips_ref, codes_ref, b_ref, x_ref, c_ref, gate_ref, own_ref, lead_ref):
@@ -267,7 +262,7 @@
         total = total + part[0:1, :]
     column = turned(lax.rsqrt(total / channels + 1e-05))
     for d in range(CHIPS):
-        cols = block_of(around(chip, d), WIDE)
+        cols = block_of(across(chip, d), WIDE)
         out = (gated_ref[:, cols] * column * gain_ref[:, cols]).astype(jnp.bfloat16)
         parts[d][...] = out
         out_ref[:, cols] = out
@@ -277,7 +272,7 @@
     chip = chip_of(me_ref[0])
     rows = rest[0].shape[0] // 2
     for d in range(CHIPS):
-        rest[CHIPS][block_of(around(chip, CHIPS - d), rows), :] = rest[d][pl.ds(rows, rows), :]
+        rest[CHIPS][block_of(across(chip, d), rows), :] = rest[d][pl.ds(rows, rows), :]
 
 
 def weights_kernel(me_ref, own_ref, other_ref, *rest):
@@ -286,7 +281,7 @@
     me = me_ref[0]
     chip, core = chip_of(me), me & 1
     for d in range(CHIPS):
-        q_ref[block_of(around(chip, CHIPS - d), rows), :] = ins[d][pl.ds(0, rows), :]
+        q_ref[block_of(across(chip, d), rows), :] = ins[d][pl.ds(0, rows), :]
     scale = LOG2E / math.sqrt(HD)
     half = rows // 2
     for head in range(2):
@@ -330,7 +325,7 @@
 def in_place(me_ref, parts, v_ref):
     chip = chip_of(me_ref[0])
     for d, part in enumerate(parts):
-        v_ref[block_of(around(chip, CHIPS - d), part.shape[0]), :] = part[...]
+        v_ref[block_of(across(chip, d), part.shape[0]), :] = part[...]
 
 
 def own_values_kernel(me_ref, weights_ref, *rest):
@@ -354,18 +349,17 @@
             o_ref[at, lanes] = (partial_ref[at, lanes] + more).astype(jnp.bfloat16)
     chip = chip_of(me_ref[0])
     for d in range(CHIPS):
-        outs[d][...] = o_ref[block_of(around(chip, d), rows), :]
+        outs[d][...] = o_ref[block_of(across(chip, d), rows), :]
 
 
 def join_kernel(me_ref, *rest):
     chip = chip_of(me_ref[0])
     for d in range(CHIPS):
-        rest[CHIPS][:, block_of(around(chip, CHIPS - d), WIDE)] = rest[d][...]
+        rest[CHIPS][:, block_of(across(chip, d), WIDE)] = rest[d][...]
 
 
 def shifted(part, d):
-    n = 2 * CHIPS
-    return lax.ppermute(part, "seq", [(i, (i + 2 * d) % n) for i in range(n)])
+    return lax.ppermute(part, "seq", [(i, i ^ (2 * d)) for i in range(2 * CHIPS)])
 
 
 def exchange(parts):
@@ -397,7 +391,7 @@
     chunk = shape((rows, WIDE), bf16)
     half_state = shape((HD + PARTS, width // 2), bf16)
 
-    state, slope, skips, codes, b, x, c, gate, gain, qk_own, qk_two = call(
+    state, slope, skips, codes, b, x, c, gate, gain, qk_own, qk_one, qk_two, qk_three = call(
         first_kernel,
         [shape((HD + PARTS, width), bf16), shape((8, width), f32), shape((8, width), f32)]
         + [
@@ -408,14 +402,14 @@
             shape((rows, width), bf16),
             shape((1, width), f32),
         ]
-        + [shape((2 * rows, WIDE), bf16)] * 2,
+        + [shape((2 * rows, WIDE), bf16)] * CHIPS,
         (me, decay_rates, skip_gain, decay_codes, b_proj, mixer_input, c_proj)
         + (gate_input, norm_gain.reshape(1, width), queries, keys),
         "shhhhhhhhhh",
         [
             pltpu.SMEM((heads,), f32),
             pltpu.SMEM((heads,), f32),
-            pltpu.SemaphoreType.DMA((12,)),
+            pltpu.SemaphoreType.DMA((16,)),
         ],
     )
     other = swapped(state)
@@ -428,21 +422,22 @@
     )
     chip_state = call(chip_kernel, half_state, (me, slope, state, other), "s")
     chip_other = lax.ppermute(chip_state, "seq", [(i, i ^ 2) for i in range(n)])
-    two_chips = call(
-        two_chips_kernel, half_state, (me, own, qk_two, slope, chip_state, chip_other), "saa"
+    two_chips, qk_one = call(
+        two_chips_kernel,
+        [half_state, shape((2 * rows, WIDE), bf16)],
+        (me, own, slope, chip_state, chip_other, qk_one),
+        "savvva",
+        through=1,
     )
     far = lax.ppermute(two_chips, "seq", [(i, i + 4) for i in range(n // 2)])
-    qk_one, qk_three = call(
-        qk_kernel,
-        [shape((2 * rows, WIDE), bf16)] * 2,
-        (me, far, queries, keys),
-        "sahh",
-        [pltpu.SemaphoreType.DMA((4,))],
+    ahead, qk_three = call(
+        ahead_kernel,
+        [shape((HD, width // 2), bf16), shape((2 * rows, WIDE), bf16)],
+        (me, qk_two, slope, chip_other, far, qk_three),
+        "savvva",
+        through=1,
     )
     qk = [qk_own, shifted(qk_one, 1), qk_two, shifted(qk_three, 3)]
-    ahead = call(
-        ahead_kernel, shape((HD, width // 2), bf16), (me, slope, chip_other, far), "s"
-    )
     gated, squares = call(
         gated_kernel,
         [shape((rows, width), f32), shape((8, rows), f32)],

time: 75.5 us -> 72 us (0.954)
  waiting for transfers between devices: 31 us -> 22.4 us
  starting transfers between devices: 28.9 us -> 35.2 us
  Pallas kernels: 14.5 us -> 13.3 us
    ppermute x9, waiting for transfers between devices: 24.1 us -> 15.4 us  [shifted(): return lax.ppermute(part, 'seq', [(i, i ^ 2 * d) for i in range(2 * CHIPS)])]
    ppermute x9, starting transfers between devices: 19.5 us -> 23.1 us  [shifted(): return lax.ppermute(part, 'seq', [(i, i ^ 2 * d) for i in range(2 * CHIPS)])]
    ppermute x1, waiting for transfers between devices: 3.22 us -> 0.01 us  [two_heads_each(): far = lax.ppermute(two_chips, 'seq', [(i, i + 4) for i in range(n // 2)])]
    ppermute x1, waiting for transfers between devices: 0.01 us -> 2.11 us  [two_heads_each(): chip_other = lax.ppermute(chip_state, 'seq', [(i, i ^ 2) for i in range(n)])]
    ppermute x1, starting transfers between devices: 1.64 us -> 3.01 us  [two_heads_each(): chip_other = lax.ppermute(chip_state, 'seq', [(i, i ^ 2) for i in range(n)])]
    ppermute x1, starting transfers between devices: 1.46 us -> 2.79 us  [two_heads_each(): far = lax.ppermute(two_chips, 'seq', [(i, i + 4) for i in range(n // 2)])]
    ppermute x7, waiting for transfers between devices: 1.42 us -> 2.64 us  [swapped(): return lax.ppermute(part, 'seq', [(i, i ^ 1) for i in range(2 * CHIPS)])]
    pallas_call x16 -> x15, Pallas kernels: 14.5 us -> 13.3 us  [call(): pl.pallas_call(body, out_shape=outs, in_specs=[kinds[space] for space in...]
  transfers between devices with their start and end apart: 21 -> 21, of which waited for: 10 -> 11; matrix products, arithmetic and copies ran while one was open for 0% -> 0% of each run, Pallas kernels for 12% -> 13%
where the time goes in v4:
time: 72 us; the launch traced here: 71.7 us
  starting transfers between devices  35.2 us (49%)
  waiting for transfers between devices  22.4 us (31%)
  Pallas kernels  13.3 us (18%)
  between operations  0.79 us (1%)
    ppermute x9, starting transfers between devices, shifted(): return lax.ppermute(part, 'seq', [(i, i ^ 2 * d) for i in range(2 * CHIPS)])  23.1 us
    ppermute x9, waiting for transfers between devices, shifted(): return lax.ppermute(part, 'seq', [(i, i ^ 2 * d) for i in range(2 * CHIPS)])  15.4 us
    pallas_call x15, Pallas kernels, call(): pl.pallas_call(body, out_shape=outs, in_specs=[kinds[space] for space in...  13.3 us
    ppermute x3, starting transfers between devices, two_heads_each(): lax.ppermute(squares, 'head', [(i, (i + k) % m) for i in range(m)])  4.49 us
    ppermute x1, starting transfers between devices, two_heads_each(): chip_other = lax.ppermute(chip_state, 'seq', [(i, i ^ 2) for i in range(n)])  3.01 us
    ppermute x1, starting transfers between devices, two_heads_each(): far = lax.ppermute(two_chips, 'seq', [(i, i + 4) for i in range(n // 2)])  2.79 us
    ppermute x7, waiting for transfers between devices, swapped(): return lax.ppermute(part, 'seq', [(i, i ^ 1) for i in range(2 * CHIPS)])  2.64 us
    ppermute x3, waiting for transfers between devices, two_heads_each(): lax.ppermute(squares, 'head', [(i, (i + k) % m) for i in range(m)])  2.22 us
  transfers between devices with their start and end apart: 21, of which 11 were waited for; matrix products, arithmetic and copies ran while one was open for 0% of the time, Pallas kernels for 13%

profile of v4, /device:TPU:0, one launch (start us, length us, event | category | flops | bytes accessed | tf_op | source)
XLA Modules:
  0.0 71.7 jit_solution(9040362134094507381)
XLA Ops:
  0.6 2.2 %shard_map.113 = (bf16[144,1024]{1,0:T(8,128)(2,1)S(1)}, f32[8,1024]{1,0:T(8,128)S(1)}, f32[8,1024]{1,0:T(8,128)S(1)}, s32[16,256]{1,0:T(8,128)S(1)}, bf16[256,1...) custom-call(s32[1]{0:T(128)} %bitcast.me_ref, ...), custom_call_target="tpu_custom_call" | custom-call | tf_op jit(solution)/shard_map/pallas_call | solution.py:34
  2.8 0.5 collective-permute-start
  3.3 1.2 %collective-permute-done.other_ref.local_ref = bf16[144,1024]{1,0:T(8,128)(2,1)S(1)} collective-permute-done((bf16[144,1024]{1,0:T(8,128)(2,1)S(1)}, bf16[144,1024]{1,0:T(8,128)(2,1)S(1)}, u32[]{:S(2)}, u32[]{:S(2)}) %collective-permute-start) | collective-permute-done | bytes 294944 | tf_op jit(solution)/shard_map/ppermute | solution.py:370
  4.5 0.1 shard_map.114.own_ref
  4.6 3.0 %collective-permute-start.2 = (bf16[144,512]{1,0:T(8,128)(2,1)S(1)}, bf16[144,512]{1,0:T(8,128)(2,1)S(1)}, u32[]{:S(2)}, u32[]{:S(2)}) collective-permute-start(bf16[144,512]{1,0:T(8,128)(2,1)S(1)} %shard_map.114.own_ref), channel_id=1, source_target_pairs={{0,8},{4,12},{8,0},{12,4},{16,24},{20,28},{24,16},{28,20},{1,9},{5... | collective-permute-start | bytes 442376 | tf_op jit(solution)/shard_map/ppermute | solution.py:424
  7.6 2.6 %collective-permute-start.1 = (bf16[512,256]{1,0:T(8,128)(2,1)S(1)}, bf16[512,256]{1,0:T(8,128)(2,1)S(1)}, u32[]{:S(2)}, u32[]{:S(2)}) collective-permute-start(bf16[512,256]{1,0:T(8,128)(2,1)S(1)} %get-tuple-element.35), channel_id=1, source_target_pairs={{0,16},{4,20},{8,24},{12,28},{16,0},{20,4},{24,8},{28,12},{1,17},{... | collective-permute-start | bytes 786440 | tf_op jit(solution)/shard_map/ppermute | solution.py:362
  10.2 2.3 %shard_map.115 = (f32[256,1024]{1,0:T(8,128)S(1)}, f32[256,1024]{1,0:T(8,128)S(1)}) custom-call(f32[8,1024]{1,0:T(8,128)S(1)} %get-tuple-element.33.slope_ref, f32[8,1024]{1,0:T(8,128)S(1)} %get-tuple-element.36.skips_ref, s32[16,256]{1,0:T(8,128)S(1)} %get-tuple-element.37.codes_ref, bf16[256,128]{1,0:T(8,128)(2,1)S(1)} %get-tuple-element.38.b_ref, ...), custom_call_target="tpu_custom_call" | custom-call | tf_op jit(solution)/shard_map/pallas_call | solution.py:34
  12.6 2.1 %collective-permute-done.2.other_ref = bf16[144,512]{1,0:T(8,128)(2,1)S(1)} collective-permute-done((bf16[144,512]{1,0:T(8,128)(2,1)S(1)}, bf16[144,512]{1,0:T(8,128)(2,1)S(1)}, u32[]{:S(2)}, u32[]{:S(2)}) %collective-permute-start.2) | collective-permute-done | bytes 147488 | tf_op jit(solution)/shard_map/ppermute | solution.py:424
  14.7 0.1 shard_map.116
  14.7 2.8 %collective-permute-start.3 = (bf16[144,512]{1,0:T(8,128)(2,1)S(1)}, bf16[144,512]{1,0:T(8,128)(2,1)S(1)}, u32[]{:S(2)}, u32[]{:S(2)}) collective-permute-start(bf16[144,512]{1,0:T(8,128)(2,1)S(1)} %get-tuple-element.44), channel_id=1, source_target_pairs={{0,16},{4,20},{8,24},{12,28},{1,17},{5,21},{9,25},{13,29},{2,18},{... | collective-permute-start | bytes 442376 | tf_op jit(solution)/shard_map/ppermute | solution.py:432
  17.5 2.5 %collective-permute-start.8 = (bf16[512,256]{1,0:T(8,128)(2,1)S(1)}, bf16[512,256]{1,0:T(8,128)(2,1)S(1)}, u32[]{:S(2)}, u32[]{:S(2)}) collective-permute-start(bf16[512,256]{1,0:T(8,128)(2,1)S(1)} %get-tuple-element.53), channel_id=1, source_target_pairs={{0,8},{4,12},{8,0},{12,4},{16,24},{20,28},{24,16},{28,20},{1,9},{5... | collective-permute-start | bytes 786440 | tf_op jit(solution)/shard_map/ppermute | solution.py:362
  20.1 2.3 %collective-permute-done.1.after_ref.rest_2_ = bf16[512,256]{1,0:T(8,128)(2,1)S(1)} collective-permute-done((bf16[512,256]{1,0:T(8,128)(2,1)S(1)}, bf16[512,256]{1,0:T(8,128)(2,1)S(1)}, u32[]{:S(2)}, u32[]{:S(2)}) %collective-permute-start.1) | collective-permute-done | bytes 262176 | tf_op jit(solution)/shard_map/ppermute | solution.py:362
  22.4 0.0 collective-permute-done.3.far_ref
  22.4 0.1 shard_map.117
  22.4 9.1 %collective-permute-start.9 = (bf16[512,256]{1,0:T(8,128)(2,1)S(1)}, bf16[512,256]{1,0:T(8,128)(2,1)S(1)}, u32[]{:S(2)}, u32[]{:S(2)}) collective-permute-start(bf16[512,256]{1,0:T(8,128)(2,1)S(1)} %get-tuple-element.54), channel_id=1, source_target_pairs={{0,24},{4,28},{8,16},{12,20},{16,8},{20,12},{24,0},{28,4},{1,25},{... | collective-permute-start | bytes 786440 | tf_op jit(solution)/shard_map/ppermute | solution.py:362
  31.5 0.0 collective-permute-start.4
  31.5 1.3 %collective-permute-done.4.other_ref = bf16[128,512]{1,0:T(8,128)(2,1)S(1)} collective-permute-done((bf16[128,512]{1,0:T(8,128)(2,1)S(1)}, bf16[128,512]{1,0:T(8,128)(2,1)S(1)}, u32[]{:S(2)}, u32[]{:S(2)}) %collective-permute-start.4) | collective-permute-done | bytes 131104 | tf_op jit(solution)/shard_map/ppermute | solution.py:370
  32.9 1.1 %shard_map.118 = (f32[256,1024]{1,0:T(8,128)S(1)}, f32[8,256]{1,0:T(8,128)S(1)}) custom-call(s32[1]{0:T(128)} %bitcast.me_ref, f32[8,1024]{1,0:T(8,128)S(1)} %get-tuple-element.33.slope_ref, bf16[144,1024]{1,0:T(8,128)(2,1)S(1)} %collective-permute-done.other_ref.local_ref, bf16[128,512]{1,0:T(8,128)(2,1)S(1)} %get-tuple-element.46.ahead_ref, ...), custom_call_target="tpu_custom_call" | custom-call | tf_op jit(solution)/shard_map/pallas_call | solution.py:34
  34.0 1.5 %collective-permute-start.5 = (f32[8,256]{1,0:T(8,128)S(1)}, f32[8,256]{1,0:T(8,128)S(1)}, u32[]{:S(2)}, u32[]{:S(2)}) collective-permute-start(f32[8,256]{1,0:T(8,128)S(1)} %get-tuple-element.49.rest_0_), channel_id=1, source_target_pairs={{0,1},{1,2},{2,3},{3,0},{4,5},{5,6},{6,7},{7,4},{8,9},{9,10},{10,1... | collective-permute-start | bytes 24584 | tf_op jit(solution)/shard_map/ppermute | solution.py:448
  35.5 1.5 %collective-permute-start.6 = (f32[8,256]{1,0:T(8,128)S(1)}, f32[8,256]{1,0:T(8,128)S(1)}, u32[]{:S(2)}, u32[]{:S(2)}) collective-permute-start(f32[8,256]{1,0:T(8,128)S(1)} %get-tuple-element.49.rest_0_), channel_id=1, source_target_pairs={{0,2},{1,3},{2,0},{3,1},{4,6},{5,7},{6,4},{7,5},{8,10},{9,11},{10,... | collective-permute-start | bytes 24584 | tf_op jit(solution)/shard_map/ppermute | solution.py:448
  37.0 1.4 %collective-permute-start.7 = (f32[8,256]{1,0:T(8,128)S(1)}, f32[8,256]{1,0:T(8,128)S(1)}, u32[]{:S(2)}, u32[]{:S(2)}) collective-permute-start(f32[8,256]{1,0:T(8,128)S(1)} %get-tuple-element.49.rest_0_), channel_id=1, source_target_pairs={{0,3},{1,0},{2,1},{3,2},{4,7},{5,4},{6,5},{7,6},{8,11},{9,8},{10,9... | collective-permute-start | bytes 24584 | tf_op jit(solution)/shard_map/ppermute | solution.py:448
  38.5 0.1 collective-permute-done.5.rest_1_
  38.6 0.6 collective-permute-done.6.rest_2_
  39.2 1.5 %collective-permute-done.7.rest_3_ = f32[8,256]{1,0:T(8,128)S(1)} collective-permute-done((f32[8,256]{1,0:T(8,128)S(1)}, f32[8,256]{1,0:T(8,128)S(1)}, u32[]{:S(2)}, u32[]{:S(2)}) %collective-permute-start.7) | collective-permute-done | bytes 8224 | tf_op jit(solution)/shard_map/ppermute | solution.py:448
  40.7 1.0 %shard_map.119 = (bf16[256,1024]{1,0:T(8,128)(2,1)}, bf16[256,256]{1,0:T(8,128)(2,1)S(1)}, bf16[256,256]{1,0:T(8,128)(2,1)S(1)}, bf16[256,256]{1,0:T(8,128)(2,1)S(1)}, bf16[256,256]{1,0:T(8,128)(2,1)S(1)}) custom-call(s32[1]{0:T(128)} %bitcast.me_ref, f32[1,1024]{1,0:T(1,128)S(1)} %get-tuple-element.32.gain_ref, ...), custom_call_target="tpu_custom_call" | custom-call | tf_op jit(solution)/shard_map/pallas_call | solution.py:34
  41.7 0.0 collective-permute-done.8.rest_1_
  41.7 0.0 collective-permute-done.9.rest_3_
  41.7 0.1 collective-permute-start.10
  41.8 0.1 collective-permute-start.13
  42.0 0.9 %collective-permute-start.12 = (bf16[256,256]{1,0:T(8,128)(2,1)S(1)}, bf16[256,256]{1,0:T(8,128)(2,1)S(1)}, u32[]{:S(2)}, u32[]{:S(2)}) collective-permute-start(bf16[256,256]{1,0:T(8,128)(2,1)S(1)} %get-tuple-element.56), channel_id=1, source_target_pairs={{0,16},{4,20},{8,24},{12,28},{16,0},{20,4},{24,8},{28,12},{1,17},{... | collective-permute-start | bytes 393224 | tf_op jit(solution)/shard_map/ppermute | solution.py:362
  42.9 3.4 %collective-permute-start.11 = (bf16[256,256]{1,0:T(8,128)(2,1)S(1)}, bf16[256,256]{1,0:T(8,128)(2,1)S(1)}, u32[]{:S(2)}, u32[]{:S(2)}) collective-permute-start(bf16[256,256]{1,0:T(8,128)(2,1)S(1)} %get-tuple-element.55), channel_id=1, source_target_pairs={{0,8},{4,12},{8,0},{12,4},{16,24},{20,28},{24,16},{28,20},{1,9},{5... | collective-permute-start | bytes 393224 | tf_op jit(solution)/shard_map/ppermute | solution.py:362
  46.3 0.0 collective-permute-start.14
  46.3 0.0 collective-permute-done.10.other_ref
  46.3 3.8 %shard_map.121.weights_ref.after_ref = bf16[2,1024,2048]{2,1,0:T(8,128)(2,1)S(1)} custom-call(s32[1]{0:T(128)} %bitcast.me_ref, bf16[1024,256]{1,0:T(8,128)(2,1)S(1)} %shard_map.120.own_ref, bf16[1024,256]{1,0:T(8,128)(2,1)S(1)} %collective-permute-done.10.other_ref, bf16[512,256]{1,0:T(8,128)(2,1)S(1)} %get-tuple-element.52.rest_0_, ...), custom_call_target="tpu_custom_call" | custom-call | tf_op jit(solution)/shard_map/pallas_call | solution.py:34
  50.1 0.0 collective-permute-done.13.rest_3_.in_ref
  50.1 0.5 collective-permute-start.17
  50.7 4.5 %collective-permute-done.12.rest_2_.in_ref = bf16[256,256]{1,0:T(8,128)(2,1)S(1)} collective-permute-done((bf16[256,256]{1,0:T(8,128)(2,1)S(1)}, bf16[256,256]{1,0:T(8,128)(2,1)S(1)}, u32[]{:S(2)}, u32[]{:S(2)}) %collective-permute-start.12) | collective-permute-done | bytes 131104 | tf_op jit(solution)/shard_map/ppermute | solution.py:362
  55.2 0.1 collective-permute-start.16
  55.3 0.0 collective-permute-done.11.rest_1_.in_ref
  55.3 0.5 collective-permute-start.15
  55.9 0.9 %shard_map.122.partial_ref = f32[1024,256]{1,0:T(8,128)S(1)} custom-call(s32[1]{0:T(128)} %bitcast.me_ref, bf16[2,1024,2048]{2,1,0:T(8,128)(2,1)S(1)} %shard_map.121.weights_ref.after_ref, bf16[256,256]{1,0:T(8,128)(2,1)S(1)} %get-tuple-element.51.after_ref.rest_0_, bf16[256,256]{1,0:T(8,128)(2,1)S(1)} %collective-permute-done.11.rest_1_.in_ref, ...), custom_call_target="tpu_custom_call" | custom-call | tf_op jit(solution)/shard_map/pallas_call | solution.py:34
  56.8 0.0 collective-permute-done.14.rest_0_
  56.8 0.0 collective-permute-done.17.rest_3_
  56.8 0.0 collective-permute-done.16.rest_2_
  56.8 0.1 collective-permute-done.15.rest_1_
  56.9 0.9 %shard_map.126 = (bf16[256,256]{1,0:T(8,128)(2,1)S(1)}, bf16[256,256]{1,0:T(8,128)(2,1)S(1)}, bf16[256,256]{1,0:T(8,128)(2,1)S(1)}, bf16[256,256]{1,0:T(8,128)(2,1)S(1)}) custom-call(s32[1]{0:T(128)} %bitcast.me_ref, f32[1024,256]{1,0:T(8,128)S(1)} %shard_map.122.partial_ref, bf16[2,1024,2048]{2,1,0:T(8,128)(2,1)S(1)} %shard_map.121.weights_ref.after_ref, ...), custom_call_target="tpu_custom_call" | custom-call | tf_op jit(solution)/shard_map/pallas_call | solution.py:34
  57.8 0.1 collective-permute-start.18
  57.9 2.1 %collective-permute-start.19 = (bf16[256,256]{1,0:T(8,128)(2,1)S(1)}, bf16[256,256]{1,0:T(8,128)(2,1)S(1)}, u32[]{:S(2)}, u32[]{:S(2)}) collective-permute-start(bf16[256,256]{1,0:T(8,128)(2,1)S(1)} %get-tuple-element.60), channel_id=1, source_target_pairs={{0,16},{4,20},{8,24},{12,28},{16,0},{20,4},{24,8},{28,12},{1,17},{... | collective-permute-start | bytes 393224 | tf_op jit(solution)/shard_map/ppermute | solution.py:362
  60.0 2.3 %collective-permute-start.20 = (bf16[256,256]{1,0:T(8,128)(2,1)S(1)}, bf16[256,256]{1,0:T(8,128)(2,1)S(1)}, u32[]{:S(2)}, u32[]{:S(2)}) collective-permute-start(bf16[256,256]{1,0:T(8,128)(2,1)S(1)} %get-tuple-element.61), channel_id=1, source_target_pairs={{0,24},{4,28},{8,16},{12,20},{16,8},{20,12},{24,0},{28,4},{1,25},{... | collective-permute-start | bytes 393224 | tf_op jit(solution)/shard_map/ppermute | solution.py:362
  62.3 3.1 %collective-permute-done.18.rest_1_ = bf16[256,256]{1,0:T(8,128)(2,1)S(1)} collective-permute-done((bf16[256,256]{1,0:T(8,128)(2,1)S(1)}, bf16[256,256]{1,0:T(8,128)(2,1)S(1)}, u32[]{:S(2)}, u32[]{:S(2)}) %collective-permute-start.18) | collective-permute-done | bytes 131104 | tf_op jit(solution)/shard_map/ppermute | solution.py:362
  65.3 5.5 %collective-permute-done.19.rest_2_ = bf16[256,256]{1,0:T(8,128)(2,1)S(1)} collective-permute-done((bf16[256,256]{1,0:T(8,128)(2,1)S(1)}, bf16[256,256]{1,0:T(8,128)(2,1)S(1)}, u32[]{:S(2)}, u32[]{:S(2)}) %collective-permute-start.19) | collective-permute-done | bytes 131104 | tf_op jit(solution)/shard_map/ppermute | solution.py:362
  70.8 0.0 collective-permute-done.20.rest_3_
  70.8 0.9 %shard_map.127 = bf16[256,1024]{1,0:T(8,128)(2,1)} custom-call(s32[1]{0:T(128)} %bitcast.me_ref, bf16[256,256]{1,0:T(8,128)(2,1)S(1)} %get-tuple-element.58.rest_0_, bf16[256,256]{1,0:T(8,128)(2,1)S(1)} %collective-permute-done.18.rest_1_, bf16[256,256]{1,0:T(8,128)(2,1)S(1)} %collective-permute-done.19.rest_2_, ...), custom_call_target="tpu_custom_call" | custom-call | tf_op jit(solution)/shard_map/pallas_call | solution.py:34
  (4 shorter events, 0.1 us)
Async XLA Ops:
  2.8 1.7 %collective-permute-start = (bf16[144,1024]{1,0:T(8,128)(2,1)S(1)}, bf16[144,1024]{1,0:T(8,128)(2,1)S(1)}, u32[]{:S(2)}, u32[]{:S(2)}) collective-permute-start(bf16[144,1024]{1,0:T(8,128)(2,1)S(1)} %get-tuple-element.34.own_ref), channel_id=1, source_target_pairs={{0,4},{4,0},{8,12},{12,8},{16,20},{20,16},{24,28},{28,24},{1,5},{5... | collective-permute-start | bytes 884744 | tf_op jit(solution)/shard_map/ppermute | solution.py:370
  4.6 10.0 %collective-permute-start.2 = (bf16[144,512]{1,0:T(8,128)(2,1)S(1)}, bf16[144,512]{1,0:T(8,128)(2,1)S(1)}, u32[]{:S(2)}, u32[]{:S(2)}) collective-permute-start(bf16[144,512]{1,0:T(8,128)(2,1)S(1)} %shard_map.114.own_ref), channel_id=1, source_target_pairs={{0,8},{4,12},{8,0},{12,4},{16,24},{20,28},{24,16},{28,20},{1,9},{5... | collective-permute-start | bytes 442376 | tf_op jit(solution)/shard_map/ppermute | solution.py:424
  7.6 14.7 %collective-permute-start.1 = (bf16[512,256]{1,0:T(8,128)(2,1)S(1)}, bf16[512,256]{1,0:T(8,128)(2,1)S(1)}, u32[]{:S(2)}, u32[]{:S(2)}) collective-permute-start(bf16[512,256]{1,0:T(8,128)(2,1)S(1)} %get-tuple-element.35), channel_id=1, source_target_pairs={{0,16},{4,20},{8,24},{12,28},{16,0},{20,4},{24,8},{28,12},{1,17},{... | collective-permute-start | bytes 786440 | tf_op jit(solution)/shard_map/ppermute | solution.py:362
  14.7 7.6 %collective-permute-start.3 = (bf16[144,512]{1,0:T(8,128)(2,1)S(1)}, bf16[144,512]{1,0:T(8,128)(2,1)S(1)}, u32[]{:S(2)}, u32[]{:S(2)}) collective-permute-start(bf16[144,512]{1,0:T(8,128)(2,1)S(1)} %get-tuple-element.44), channel_id=1, source_target_pairs={{0,16},{4,20},{8,24},{12,28},{1,17},{5,21},{9,25},{13,29},{2,18},{... | collective-permute-start | bytes 442376 | tf_op jit(solution)/shard_map/ppermute | solution.py:432
  17.5 24.2 %collective-permute-start.8 = (bf16[512,256]{1,0:T(8,128)(2,1)S(1)}, bf16[512,256]{1,0:T(8,128)(2,1)S(1)}, u32[]{:S(2)}, u32[]{:S(2)}) collective-permute-start(bf16[512,256]{1,0:T(8,128)(2,1)S(1)} %get-tuple-element.53), channel_id=1, source_target_pairs={{0,8},{4,12},{8,0},{12,4},{16,24},{20,28},{24,16},{28,20},{1,9},{5... | collective-permute-start | bytes 786440 | tf_op jit(solution)/shard_map/ppermute | solution.py:362
  22.4 19.3 %collective-permute-start.9 = (bf16[512,256]{1,0:T(8,128)(2,1)S(1)}, bf16[512,256]{1,0:T(8,128)(2,1)S(1)}, u32[]{:S(2)}, u32[]{:S(2)}) collective-permute-start(bf16[512,256]{1,0:T(8,128)(2,1)S(1)} %get-tuple-element.54), channel_id=1, source_target_pairs={{0,24},{4,28},{8,16},{12,20},{16,8},{20,12},{24,0},{28,4},{1,25},{... | collective-permute-start | bytes 786440 | tf_op jit(solution)/shard_map/ppermute | solution.py:362
  31.5 1.3 %collective-permute-start.4 = (bf16[128,512]{1,0:T(8,128)(2,1)S(1)}, bf16[128,512]{1,0:T(8,128)(2,1)S(1)}, u32[]{:S(2)}, u32[]{:S(2)}) collective-permute-start(bf16[128,512]{1,0:T(8,128)(2,1)S(1)} %get-tuple-element.46.ahead_ref), channel_id=1, source_target_pairs={{0,4},{4,0},{8,12},{12,8},{16,20},{20,16},{24,28},{28,24},{1,5},{5... | collective-permute-start | bytes 393224 | tf_op jit(solution)/shard_map/ppermute | solution.py:370
  34.0 4.6 %collective-permute-start.5 = (f32[8,256]{1,0:T(8,128)S(1)}, f32[8,256]{1,0:T(8,128)S(1)}, u32[]{:S(2)}, u32[]{:S(2)}) collective-permute-start(f32[8,256]{1,0:T(8,128)S(1)} %get-tuple-element.49.rest_0_), channel_id=1, source_target_pairs={{0,1},{1,2},{2,3},{3,0},{4,5},{5,6},{6,7},{7,4},{8,9},{9,10},{10,1... | collective-permute-start | bytes 24584 | tf_op jit(solution)/shard_map/ppermute | solution.py:448
  35.5 3.7 %collective-permute-start.6 = (f32[8,256]{1,0:T(8,128)S(1)}, f32[8,256]{1,0:T(8,128)S(1)}, u32[]{:S(2)}, u32[]{:S(2)}) collective-permute-start(f32[8,256]{1,0:T(8,128)S(1)} %get-tuple-element.49.rest_0_), channel_id=1, source_target_pairs={{0,2},{1,3},{2,0},{3,1},{4,6},{5,7},{6,4},{7,5},{8,10},{9,11},{10,... | collective-permute-start | bytes 24584 | tf_op jit(solution)/shard_map/ppermute | solution.py:448
  37.0 3.7 %collective-permute-start.7 = (f32[8,256]{1,0:T(8,128)S(1)}, f32[8,256]{1,0:T(8,128)S(1)}, u32[]{:S(2)}, u32[]{:S(2)}) collective-permute-start(f32[8,256]{1,0:T(8,128)S(1)} %get-tuple-element.49.rest_0_), channel_id=1, source_target_pairs={{0,3},{1,0},{2,1},{3,2},{4,7},{5,4},{6,5},{7,6},{8,11},{9,8},{10,9... | collective-permute-start | bytes 24584 | tf_op jit(solution)/shard_map/ppermute | solution.py:448
  41.7 4.5 %collective-permute-start.10 = (bf16[1024,256]{1,0:T(8,128)(2,1)S(1)}, bf16[1024,256]{1,0:T(8,128)(2,1)S(1)}, u32[]{:S(2)}, u32[]{:S(2)}) collective-permute-start(bf16[1024,256]{1,0:T(8,128)(2,1)S(1)} %shard_map.120.own_ref), channel_id=1, source_target_pairs={{0,4},{4,0},{8,12},{12,8},{16,20},{20,16},{24,28},{28,24},{1,5},{5... | collective-permute-start | bytes 1572872 | tf_op jit(solution)/shard_map/ppermute | solution.py:370
  41.8 8.3 %collective-permute-start.13 = (bf16[256,256]{1,0:T(8,128)(2,1)S(1)}, bf16[256,256]{1,0:T(8,128)(2,1)S(1)}, u32[]{:S(2)}, u32[]{:S(2)}) collective-permute-start(bf16[256,256]{1,0:T(8,128)(2,1)S(1)} %get-tuple-element.57), channel_id=1, source_target_pairs={{0,24},{4,28},{8,16},{12,20},{16,8},{20,12},{24,0},{28,4},{1,25},{... | collective-permute-start | bytes 393224 | tf_op jit(solution)/shard_map/ppermute | solution.py:362
  42.0 13.2 %collective-permute-start.12 = (bf16[256,256]{1,0:T(8,128)(2,1)S(1)}, bf16[256,256]{1,0:T(8,128)(2,1)S(1)}, u32[]{:S(2)}, u32[]{:S(2)}) collective-permute-start(bf16[256,256]{1,0:T(8,128)(2,1)S(1)} %get-tuple-element.56), channel_id=1, source_target_pairs={{0,16},{4,20},{8,24},{12,28},{16,0},{20,4},{24,8},{28,12},{1,17},{... | collective-permute-start | bytes 393224 | tf_op jit(solution)/shard_map/ppermute | solution.py:362
  42.9 12.4 %collective-permute-start.11 = (bf16[256,256]{1,0:T(8,128)(2,1)S(1)}, bf16[256,256]{1,0:T(8,128)(2,1)S(1)}, u32[]{:S(2)}, u32[]{:S(2)}) collective-permute-start(bf16[256,256]{1,0:T(8,128)(2,1)S(1)} %get-tuple-element.55), channel_id=1, source_target_pairs={{0,8},{4,12},{8,0},{12,4},{16,24},{20,28},{24,16},{28,20},{1,9},{5... | collective-permute-start | bytes 393224 | tf_op jit(solution)/shard_map/ppermute | solution.py:362
  46.3 10.5 %collective-permute-start.14 = (bf16[256,256]{1,0:T(8,128)(2,1)S(1)}, bf16[256,256]{1,0:T(8,128)(2,1)S(1)}, u32[]{:S(2)}, u32[]{:S(2)}) collective-permute-start(bf16[256,256]{1,0:T(8,128)(2,1)S(1)} %get-tuple-element.51.after_ref.rest_0_), channel_id=1, source_target_pairs={{0,4},{4,0},{8,12},{12,8},{16,20},{20,16},{24,28},{28,24},{1,5},{5... | collective-permute-start | bytes 393224 | tf_op jit(solution)/shard_map/ppermute | solution.py:370
  50.1 6.6 %collective-permute-start.17 = (bf16[256,256]{1,0:T(8,128)(2,1)S(1)}, bf16[256,256]{1,0:T(8,128)(2,1)S(1)}, u32[]{:S(2)}, u32[]{:S(2)}) collective-permute-start(bf16[256,256]{1,0:T(8,128)(2,1)S(1)} %shard_map.125), channel_id=1, source_target_pairs={{0,4},{4,0},{8,12},{12,8},{16,20},{20,16},{24,28},{28,24},{1,5},{5... | collective-permute-start | bytes 393224 | tf_op jit(solution)/shard_map/ppermute | solution.py:370
  55.2 1.6 %collective-permute-start.16 = (bf16[256,256]{1,0:T(8,128)(2,1)S(1)}, bf16[256,256]{1,0:T(8,128)(2,1)S(1)}, u32[]{:S(2)}, u32[]{:S(2)}) collective-permute-start(bf16[256,256]{1,0:T(8,128)(2,1)S(1)} %shard_map.124), channel_id=1, source_target_pairs={{0,4},{4,0},{8,12},{12,8},{16,20},{20,16},{24,28},{28,24},{1,5},{5... | collective-permute-start | bytes 393224 | tf_op jit(solution)/shard_map/ppermute | solution.py:370
  55.3 1.5 %collective-permute-start.15 = (bf16[256,256]{1,0:T(8,128)(2,1)S(1)}, bf16[256,256]{1,0:T(8,128)(2,1)S(1)}, u32[]{:S(2)}, u32[]{:S(2)}) collective-permute-start(bf16[256,256]{1,0:T(8,128)(2,1)S(1)} %shard_map.123), channel_id=1, source_target_pairs={{0,4},{4,0},{8,12},{12,8},{16,20},{20,16},{24,28},{28,24},{1,5},{5... | collective-permute-start | bytes 393224 | tf_op jit(solution)/shard_map/ppermute | solution.py:370
  57.8 7.5 %collective-permute-start.18 = (bf16[256,256]{1,0:T(8,128)(2,1)S(1)}, bf16[256,256]{1,0:T(8,128)(2,1)S(1)}, u32[]{:S(2)}, u32[]{:S(2)}) collective-permute-start(bf16[256,256]{1,0:T(8,128)(2,1)S(1)} %get-tuple-element.59), channel_id=1, source_target_pairs={{0,8},{4,12},{8,0},{12,4},{16,24},{20,28},{24,16},{28,20},{1,9},{5... | collective-permute-start | bytes 393224 | tf_op jit(solution)/shard_map/ppermute | solution.py:362
  57.9 13.0 %collective-permute-start.19 = (bf16[256,256]{1,0:T(8,128)(2,1)S(1)}, bf16[256,256]{1,0:T(8,128)(2,1)S(1)}, u32[]{:S(2)}, u32[]{:S(2)}) collective-permute-start(bf16[256,256]{1,0:T(8,128)(2,1)S(1)} %get-tuple-element.60), channel_id=1, source_target_pairs={{0,16},{4,20},{8,24},{12,28},{16,0},{20,4},{24,8},{28,12},{1,17},{... | collective-permute-start | bytes 393224 | tf_op jit(solution)/shard_map/ppermute | solution.py:362
  60.0 10.8 %collective-permute-start.20 = (bf16[256,256]{1,0:T(8,128)(2,1)S(1)}, bf16[256,256]{1,0:T(8,128)(2,1)S(1)}, u32[]{:S(2)}, u32[]{:S(2)}) collective-permute-start(bf16[256,256]{1,0:T(8,128)(2,1)S(1)} %get-tuple-element.61), channel_id=1, source_target_pairs={{0,24},{4,28},{8,16},{12,20},{16,8},{20,12},{24,0},{28,4},{1,25},{... | collective-permute-start | bytes 393224 | tf_op jit(solution)/shard_map/ppermute | solution.py:362

commit v5 on v4

--- a/solution.py
+++ b/solution.py
@@ -352,10 +352,10 @@
         outs[d][...] = o_ref[block_of(across(chip, d), rows), :]
 
 
-def join_kernel(me_ref, *rest):
+def join_kernel(steps, me_ref, *rest):
     chip = chip_of(me_ref[0])
-    for d in range(CHIPS):
-        rest[CHIPS][:, block_of(across(chip, d), WIDE)] = rest[d][...]
+    for d, part in zip(steps, rest[:CHIPS]):
+        rest[CHIPS][:, block_of(across(chip, d), WIDE)] = part[...]
 
 
 def shifted(part, d):
@@ -363,7 +363,8 @@
 
 
 def exchange(parts):
-    return [parts[0]] + [shifted(parts[d], d) for d in range(1, CHIPS)]
+    moved = {d: shifted(parts[d], d) for d in (3, 1, 2)}
+    return [parts[0]] + [moved[d] for d in range(1, CHIPS)]
 
 
 def swapped(part):
@@ -484,10 +485,12 @@
         "s",
         [pltpu.VMEM((CHIPS * rows, WIDE), bf16), pltpu.VMEM((CHIPS * rows, WIDE), bf16)],
     )
+    steps = (0, 3, 1, 2)
+    results = exchange(results)
     attn_out = call(
-        join_kernel,
+        functools.partial(join_kernel, steps),
         jax.ShapeDtypeStruct((rows, width), bf16),
-        (me, *exchange(results)),
+        (me, *(results[d] for d in steps)),
         "s",
     )
     return (mamba_out, attn_out)

time: 72 us -> 71.6 us (level)
  no operation moved by 1% of the time
where the time goes in v5:
time: 71.6 us; the launch traced here: 71.4 us
  starting transfers between devices  35.2 us (49%)
  waiting for transfers between devices  22.1 us (31%)
  Pallas kernels  13.3 us (19%)
  between operations  0.78 us (1%)
    ppermute x9, starting transfers between devices, shifted(): return lax.ppermute(part, 'seq', [(i, i ^ 2 * d) for i in range(2 * CHIPS)])  23.1 us
    ppermute x9, waiting for transfers between devices, shifted(): return lax.ppermute(part, 'seq', [(i, i ^ 2 * d) for i in range(2 * CHIPS)])  15.1 us
    pallas_call x15, Pallas kernels, call(): pl.pallas_call(body, out_shape=outs, in_specs=[kinds[space] for space in...  13.3 us
    ppermute x3, starting transfers between devices, two_heads_each(): lax.ppermute(squares, 'head', [(i, (i + k) % m) for i in range(m)])  4.49 us
    ppermute x1, starting transfers between devices, two_heads_each(): chip_other = lax.ppermute(chip_state, 'seq', [(i, i ^ 2) for i in range(n)])  3.01 us
    ppermute x1, starting transfers between devices, two_heads_each(): far = lax.ppermute(two_chips, 'seq', [(i, i + 4) for i in range(n // 2)])  2.79 us
    ppermute x7, waiting for transfers between devices, swapped(): return lax.ppermute(part, 'seq', [(i, i ^ 1) for i in range(2 * CHIPS)])  2.64 us
    ppermute x3, waiting for transfers between devices, two_heads_each(): lax.ppermute(squares, 'head', [(i, (i + k) % m) for i in range(m)])  2.22 us
  transfers between devices with their start and end apart: 21, of which 11 were waited for; matrix products, arithmetic and copies ran while one was open for 0% of the time, Pallas kernels for 13%

profile of v5, /device:TPU:0, one launch (start us, length us, event | category | flops | bytes accessed | tf_op | source)
XLA Modules:
  0.0 71.4 jit_solution(3955530997673409241)
XLA Ops:
  0.6 2.2 %shard_map.113 = (bf16[144,1024]{1,0:T(8,128)(2,1)S(1)}, f32[8,1024]{1,0:T(8,128)S(1)}, f32[8,1024]{1,0:T(8,128)S(1)}, s32[16,256]{1,0:T(8,128)S(1)}, bf16[256,1...) custom-call(s32[1]{0:T(128)} %bitcast.me_ref, ...), custom_call_target="tpu_custom_call" | custom-call | tf_op jit(solution)/shard_map/pallas_call | solution.py:34
  2.8 0.5 collective-permute-start
  3.3 1.2 %collective-permute-done.other_ref.local_ref = bf16[144,1024]{1,0:T(8,128)(2,1)S(1)} collective-permute-done((bf16[144,1024]{1,0:T(8,128)(2,1)S(1)}, bf16[144,1024]{1,0:T(8,128)(2,1)S(1)}, u32[]{:S(2)}, u32[]{:S(2)}) %collective-permute-start) | collective-permute-done | bytes 294944 | tf_op jit(solution)/shard_map/ppermute | solution.py:371
  4.5 0.1 shard_map.114.own_ref
  4.6 3.0 %collective-permute-start.2 = (bf16[144,512]{1,0:T(8,128)(2,1)S(1)}, bf16[144,512]{1,0:T(8,128)(2,1)S(1)}, u32[]{:S(2)}, u32[]{:S(2)}) collective-permute-start(bf16[144,512]{1,0:T(8,128)(2,1)S(1)} %shard_map.114.own_ref), channel_id=1, source_target_pairs={{0,8},{4,12},{8,0},{12,4},{16,24},{20,28},{24,16},{28,20},{1,9},{5... | collective-permute-start | bytes 442376 | tf_op jit(solution)/shard_map/ppermute | solution.py:425
  7.6 2.6 %collective-permute-start.1 = (bf16[512,256]{1,0:T(8,128)(2,1)S(1)}, bf16[512,256]{1,0:T(8,128)(2,1)S(1)}, u32[]{:S(2)}, u32[]{:S(2)}) collective-permute-start(bf16[512,256]{1,0:T(8,128)(2,1)S(1)} %get-tuple-element.35), channel_id=1, source_target_pairs={{0,16},{4,20},{8,24},{12,28},{16,0},{20,4},{24,8},{28,12},{1,17},{... | collective-permute-start | bytes 786440 | tf_op jit(solution)/shard_map/ppermute | solution.py:362
  10.2 2.3 %shard_map.115 = (f32[256,1024]{1,0:T(8,128)S(1)}, f32[256,1024]{1,0:T(8,128)S(1)}) custom-call(f32[8,1024]{1,0:T(8,128)S(1)} %get-tuple-element.33.slope_ref, f32[8,1024]{1,0:T(8,128)S(1)} %get-tuple-element.36.skips_ref, s32[16,256]{1,0:T(8,128)S(1)} %get-tuple-element.37.codes_ref, bf16[256,128]{1,0:T(8,128)(2,1)S(1)} %get-tuple-element.38.b_ref, ...), custom_call_target="tpu_custom_call" | custom-call | tf_op jit(solution)/shard_map/pallas_call | solution.py:34
  12.6 2.1 %collective-permute-done.2.other_ref = bf16[144,512]{1,0:T(8,128)(2,1)S(1)} collective-permute-done((bf16[144,512]{1,0:T(8,128)(2,1)S(1)}, bf16[144,512]{1,0:T(8,128)(2,1)S(1)}, u32[]{:S(2)}, u32[]{:S(2)}) %collective-permute-start.2) | collective-permute-done | bytes 147488 | tf_op jit(solution)/shard_map/ppermute | solution.py:425
  14.7 0.1 shard_map.116
  14.7 2.8 %collective-permute-start.3 = (bf16[144,512]{1,0:T(8,128)(2,1)S(1)}, bf16[144,512]{1,0:T(8,128)(2,1)S(1)}, u32[]{:S(2)}, u32[]{:S(2)}) collective-permute-start(bf16[144,512]{1,0:T(8,128)(2,1)S(1)} %get-tuple-element.44), channel_id=1, source_target_pairs={{0,16},{4,20},{8,24},{12,28},{1,17},{5,21},{9,25},{13,29},{2,18},{... | collective-permute-start | bytes 442376 | tf_op jit(solution)/shard_map/ppermute | solution.py:433
  17.5 2.5 %collective-permute-start.8 = (bf16[512,256]{1,0:T(8,128)(2,1)S(1)}, bf16[512,256]{1,0:T(8,128)(2,1)S(1)}, u32[]{:S(2)}, u32[]{:S(2)}) collective-permute-start(bf16[512,256]{1,0:T(8,128)(2,1)S(1)} %get-tuple-element.53), channel_id=1, source_target_pairs={{0,8},{4,12},{8,0},{12,4},{16,24},{20,28},{24,16},{28,20},{1,9},{5... | collective-permute-start | bytes 786440 | tf_op jit(solution)/shard_map/ppermute | solution.py:362
  20.1 2.3 %collective-permute-done.1.after_ref.rest_2_ = bf16[512,256]{1,0:T(8,128)(2,1)S(1)} collective-permute-done((bf16[512,256]{1,0:T(8,128)(2,1)S(1)}, bf16[512,256]{1,0:T(8,128)(2,1)S(1)}, u32[]{:S(2)}, u32[]{:S(2)}) %collective-permute-start.1) | collective-permute-done | bytes 262176 | tf_op jit(solution)/shard_map/ppermute | solution.py:362
  22.4 0.0 collective-permute-done.3.far_ref
  22.4 0.1 shard_map.117
  22.4 9.1 %collective-permute-start.9 = (bf16[512,256]{1,0:T(8,128)(2,1)S(1)}, bf16[512,256]{1,0:T(8,128)(2,1)S(1)}, u32[]{:S(2)}, u32[]{:S(2)}) collective-permute-start(bf16[512,256]{1,0:T(8,128)(2,1)S(1)} %get-tuple-element.54), channel_id=1, source_target_pairs={{0,24},{4,28},{8,16},{12,20},{16,8},{20,12},{24,0},{28,4},{1,25},{... | collective-permute-start | bytes 786440 | tf_op jit(solution)/shard_map/ppermute | solution.py:362
  31.5 0.0 collective-permute-start.4
  31.5 1.3 %collective-permute-done.4.other_ref = bf16[128,512]{1,0:T(8,128)(2,1)S(1)} collective-permute-done((bf16[128,512]{1,0:T(8,128)(2,1)S(1)}, bf16[128,512]{1,0:T(8,128)(2,1)S(1)}, u32[]{:S(2)}, u32[]{:S(2)}) %collective-permute-start.4) | collective-permute-done | bytes 131104 | tf_op jit(solution)/shard_map/ppermute | solution.py:371
  32.9 1.1 %shard_map.118 = (f32[256,1024]{1,0:T(8,128)S(1)}, f32[8,256]{1,0:T(8,128)S(1)}) custom-call(s32[1]{0:T(128)} %bitcast.me_ref, f32[8,1024]{1,0:T(8,128)S(1)} %get-tuple-element.33.slope_ref, bf16[144,1024]{1,0:T(8,128)(2,1)S(1)} %collective-permute-done.other_ref.local_ref, bf16[128,512]{1,0:T(8,128)(2,1)S(1)} %get-tuple-element.46.ahead_ref, ...), custom_call_target="tpu_custom_call" | custom-call | tf_op jit(solution)/shard_map/pallas_call | solution.py:34
  34.0 1.5 %collective-permute-start.5 = (f32[8,256]{1,0:T(8,128)S(1)}, f32[8,256]{1,0:T(8,128)S(1)}, u32[]{:S(2)}, u32[]{:S(2)}) collective-permute-start(f32[8,256]{1,0:T(8,128)S(1)} %get-tuple-element.49.rest_0_), channel_id=1, source_target_pairs={{0,1},{1,2},{2,3},{3,0},{4,5},{5,6},{6,7},{7,4},{8,9},{9,10},{10,1... | collective-permute-start | bytes 24584 | tf_op jit(solution)/shard_map/ppermute | solution.py:449
  35.5 1.5 %collective-permute-start.6 = (f32[8,256]{1,0:T(8,128)S(1)}, f32[8,256]{1,0:T(8,128)S(1)}, u32[]{:S(2)}, u32[]{:S(2)}) collective-permute-start(f32[8,256]{1,0:T(8,128)S(1)} %get-tuple-element.49.rest_0_), channel_id=1, source_target_pairs={{0,2},{1,3},{2,0},{3,1},{4,6},{5,7},{6,4},{7,5},{8,10},{9,11},{10,... | collective-permute-start | bytes 24584 | tf_op jit(solution)/shard_map/ppermute | solution.py:449
  37.0 1.4 %collective-permute-start.7 = (f32[8,256]{1,0:T(8,128)S(1)}, f32[8,256]{1,0:T(8,128)S(1)}, u32[]{:S(2)}, u32[]{:S(2)}) collective-permute-start(f32[8,256]{1,0:T(8,128)S(1)} %get-tuple-element.49.rest_0_), channel_id=1, source_target_pairs={{0,3},{1,0},{2,1},{3,2},{4,7},{5,4},{6,5},{7,6},{8,11},{9,8},{10,9... | collective-permute-start | bytes 24584 | tf_op jit(solution)/shard_map/ppermute | solution.py:449
  38.5 0.1 collective-permute-done.5.rest_1_
  38.6 0.6 collective-permute-done.6.rest_2_
  39.2 1.5 %collective-permute-done.7.rest_3_ = f32[8,256]{1,0:T(8,128)S(1)} collective-permute-done((f32[8,256]{1,0:T(8,128)S(1)}, f32[8,256]{1,0:T(8,128)S(1)}, u32[]{:S(2)}, u32[]{:S(2)}) %collective-permute-start.7) | collective-permute-done | bytes 8224 | tf_op jit(solution)/shard_map/ppermute | solution.py:449
  40.7 1.0 %shard_map.119 = (bf16[256,1024]{1,0:T(8,128)(2,1)}, bf16[256,256]{1,0:T(8,128)(2,1)S(1)}, bf16[256,256]{1,0:T(8,128)(2,1)S(1)}, bf16[256,256]{1,0:T(8,128)(2,1)S(1)}, bf16[256,256]{1,0:T(8,128)(2,1)S(1)}) custom-call(s32[1]{0:T(128)} %bitcast.me_ref, f32[1,1024]{1,0:T(1,128)S(1)} %get-tuple-element.32.gain_ref, ...), custom_call_target="tpu_custom_call" | custom-call | tf_op jit(solution)/shard_map/pallas_call | solution.py:34
  41.7 0.0 collective-permute-done.8.rest_1_
  41.7 0.0 collective-permute-done.9.rest_3_
  41.7 0.1 collective-permute-start.10
  41.8 0.1 collective-permute-start.13
  42.0 0.9 %collective-permute-start.12 = (bf16[256,256]{1,0:T(8,128)(2,1)S(1)}, bf16[256,256]{1,0:T(8,128)(2,1)S(1)}, u32[]{:S(2)}, u32[]{:S(2)}) collective-permute-start(bf16[256,256]{1,0:T(8,128)(2,1)S(1)} %get-tuple-element.56), channel_id=1, source_target_pairs={{0,16},{4,20},{8,24},{12,28},{16,0},{20,4},{24,8},{28,12},{1,17},{... | collective-permute-start | bytes 393224 | tf_op jit(solution)/shard_map/ppermute | solution.py:362
  42.9 3.4 %collective-permute-start.11 = (bf16[256,256]{1,0:T(8,128)(2,1)S(1)}, bf16[256,256]{1,0:T(8,128)(2,1)S(1)}, u32[]{:S(2)}, u32[]{:S(2)}) collective-permute-start(bf16[256,256]{1,0:T(8,128)(2,1)S(1)} %get-tuple-element.55), channel_id=1, source_target_pairs={{0,8},{4,12},{8,0},{12,4},{16,24},{20,28},{24,16},{28,20},{1,9},{5... | collective-permute-start | bytes 393224 | tf_op jit(solution)/shard_map/ppermute | solution.py:362
  46.3 0.0 collective-permute-start.14
  46.3 0.0 collective-permute-done.10.other_ref
  46.3 3.8 %shard_map.121.weights_ref.after_ref = bf16[2,1024,2048]{2,1,0:T(8,128)(2,1)S(1)} custom-call(s32[1]{0:T(128)} %bitcast.me_ref, bf16[1024,256]{1,0:T(8,128)(2,1)S(1)} %shard_map.120.own_ref, bf16[1024,256]{1,0:T(8,128)(2,1)S(1)} %collective-permute-done.10.other_ref, bf16[512,256]{1,0:T(8,128)(2,1)S(1)} %get-tuple-element.52.rest_0_, ...), custom_call_target="tpu_custom_call" | custom-call | tf_op jit(solution)/shard_map/pallas_call | solution.py:34
  50.1 0.0 collective-permute-done.13.rest_3_.in_ref
  50.1 0.5 collective-permute-start.17
  50.7 4.5 %collective-permute-done.12.rest_2_.in_ref = bf16[256,256]{1,0:T(8,128)(2,1)S(1)} collective-permute-done((bf16[256,256]{1,0:T(8,128)(2,1)S(1)}, bf16[256,256]{1,0:T(8,128)(2,1)S(1)}, u32[]{:S(2)}, u32[]{:S(2)}) %collective-permute-start.12) | collective-permute-done | bytes 131104 | tf_op jit(solution)/shard_map/ppermute | solution.py:362
  55.2 0.1 collective-permute-start.16
  55.3 0.0 collective-permute-done.11.rest_1_.in_ref
  55.3 0.5 collective-permute-start.15
  55.9 0.9 %shard_map.122.partial_ref = f32[1024,256]{1,0:T(8,128)S(1)} custom-call(s32[1]{0:T(128)} %bitcast.me_ref, bf16[2,1024,2048]{2,1,0:T(8,128)(2,1)S(1)} %shard_map.121.weights_ref.after_ref, bf16[256,256]{1,0:T(8,128)(2,1)S(1)} %get-tuple-element.51.after_ref.rest_0_, bf16[256,256]{1,0:T(8,128)(2,1)S(1)} %collective-permute-done.11.rest_1_.in_ref, ...), custom_call_target="tpu_custom_call" | custom-call | tf_op jit(solution)/shard_map/pallas_call | solution.py:34
  56.8 0.0 collective-permute-done.14.rest_0_
  56.8 0.0 collective-permute-done.17.rest_3_
  56.8 0.0 collective-permute-done.16.rest_2_
  56.8 0.1 collective-permute-done.15.rest_1_
  56.9 0.9 %shard_map.126 = (bf16[256,256]{1,0:T(8,128)(2,1)S(1)}, bf16[256,256]{1,0:T(8,128)(2,1)S(1)}, bf16[256,256]{1,0:T(8,128)(2,1)S(1)}, bf16[256,256]{1,0:T(8,128)(2,1)S(1)}) custom-call(s32[1]{0:T(128)} %bitcast.me_ref, f32[1024,256]{1,0:T(8,128)S(1)} %shard_map.122.partial_ref, bf16[2,1024,2048]{2,1,0:T(8,128)(2,1)S(1)} %shard_map.121.weights_ref.after_ref, ...), custom_call_target="tpu_custom_call" | custom-call | tf_op jit(solution)/shard_map/pallas_call | solution.py:34
  57.8 1.6 %collective-permute-start.18 = (bf16[256,256]{1,0:T(8,128)(2,1)S(1)}, bf16[256,256]{1,0:T(8,128)(2,1)S(1)}, u32[]{:S(2)}, u32[]{:S(2)}) collective-permute-start(bf16[256,256]{1,0:T(8,128)(2,1)S(1)} %get-tuple-element.59), channel_id=1, source_target_pairs={{0,24},{4,28},{8,16},{12,20},{16,8},{20,12},{24,0},{28,4},{1,25},{... | collective-permute-start | bytes 393224 | tf_op jit(solution)/shard_map/ppermute | solution.py:362
  59.4 0.0 collective-permute-start.19
  59.4 2.8 %collective-permute-start.20 = (bf16[256,256]{1,0:T(8,128)(2,1)S(1)}, bf16[256,256]{1,0:T(8,128)(2,1)S(1)}, u32[]{:S(2)}, u32[]{:S(2)}) collective-permute-start(bf16[256,256]{1,0:T(8,128)(2,1)S(1)} %get-tuple-element.61), channel_id=1, source_target_pairs={{0,16},{4,20},{8,24},{12,28},{16,0},{20,4},{24,8},{28,12},{1,17},{... | collective-permute-start | bytes 393224 | tf_op jit(solution)/shard_map/ppermute | solution.py:362
  62.3 3.9 %collective-permute-done.18.rest_1_ = bf16[256,256]{1,0:T(8,128)(2,1)S(1)} collective-permute-done((bf16[256,256]{1,0:T(8,128)(2,1)S(1)}, bf16[256,256]{1,0:T(8,128)(2,1)S(1)}, u32[]{:S(2)}, u32[]{:S(2)}) %collective-permute-start.18) | collective-permute-done | bytes 131104 | tf_op jit(solution)/shard_map/ppermute | solution.py:362
  66.1 4.4 %collective-permute-done.19.rest_2_ = bf16[256,256]{1,0:T(8,128)(2,1)S(1)} collective-permute-done((bf16[256,256]{1,0:T(8,128)(2,1)S(1)}, bf16[256,256]{1,0:T(8,128)(2,1)S(1)}, u32[]{:S(2)}, u32[]{:S(2)}) %collective-permute-start.19) | collective-permute-done | bytes 131104 | tf_op jit(solution)/shard_map/ppermute | solution.py:362
  70.5 0.0 collective-permute-done.20.rest_3_
  70.5 0.9 %shard_map.127 = bf16[256,1024]{1,0:T(8,128)(2,1)} custom-call(s32[1]{0:T(128)} %bitcast.me_ref, bf16[256,256]{1,0:T(8,128)(2,1)S(1)} %get-tuple-element.58.rest_0_, bf16[256,256]{1,0:T(8,128)(2,1)S(1)} %collective-permute-done.18.rest_1_, bf16[256,256]{1,0:T(8,128)(2,1)S(1)} %collective-permute-done.19.rest_2_, ...), custom_call_target="tpu_custom_call" | custom-call | tf_op jit(solution)/shard_map/pallas_call | solution.py:34
  (4 shorter events, 0.1 us)
Async XLA Ops:
  2.8 1.7 %collective-permute-start = (bf16[144,1024]{1,0:T(8,128)(2,1)S(1)}, bf16[144,1024]{1,0:T(8,128)(2,1)S(1)}, u32[]{:S(2)}, u32[]{:S(2)}) collective-permute-start(bf16[144,1024]{1,0:T(8,128)(2,1)S(1)} %get-tuple-element.34.own_ref), channel_id=1, source_target_pairs={{0,4},{4,0},{8,12},{12,8},{16,20},{20,16},{24,28},{28,24},{1,5},{5... | collective-permute-start | bytes 884744 | tf_op jit(solution)/shard_map/ppermute | solution.py:371
  4.6 10.0 %collective-permute-start.2 = (bf16[144,512]{1,0:T(8,128)(2,1)S(1)}, bf16[144,512]{1,0:T(8,128)(2,1)S(1)}, u32[]{:S(2)}, u32[]{:S(2)}) collective-permute-start(bf16[144,512]{1,0:T(8,128)(2,1)S(1)} %shard_map.114.own_ref), channel_id=1, source_target_pairs={{0,8},{4,12},{8,0},{12,4},{16,24},{20,28},{24,16},{28,20},{1,9},{5... | collective-permute-start | bytes 442376 | tf_op jit(solution)/shard_map/ppermute | solution.py:425
  7.6 14.7 %collective-permute-start.1 = (bf16[512,256]{1,0:T(8,128)(2,1)S(1)}, bf16[512,256]{1,0:T(8,128)(2,1)S(1)}, u32[]{:S(2)}, u32[]{:S(2)}) collective-permute-start(bf16[512,256]{1,0:T(8,128)(2,1)S(1)} %get-tuple-element.35), channel_id=1, source_target_pairs={{0,16},{4,20},{8,24},{12,28},{16,0},{20,4},{24,8},{28,12},{1,17},{... | collective-permute-start | bytes 786440 | tf_op jit(solution)/shard_map/ppermute | solution.py:362
  14.7 7.6 %collective-permute-start.3 = (bf16[144,512]{1,0:T(8,128)(2,1)S(1)}, bf16[144,512]{1,0:T(8,128)(2,1)S(1)}, u32[]{:S(2)}, u32[]{:S(2)}) collective-permute-start(bf16[144,512]{1,0:T(8,128)(2,1)S(1)} %get-tuple-element.44), channel_id=1, source_target_pairs={{0,16},{4,20},{8,24},{12,28},{1,17},{5,21},{9,25},{13,29},{2,18},{... | collective-permute-start | bytes 442376 | tf_op jit(solution)/shard_map/ppermute | solution.py:433
  17.5 24.2 %collective-permute-start.8 = (bf16[512,256]{1,0:T(8,128)(2,1)S(1)}, bf16[512,256]{1,0:T(8,128)(2,1)S(1)}, u32[]{:S(2)}, u32[]{:S(2)}) collective-permute-start(bf16[512,256]{1,0:T(8,128)(2,1)S(1)} %get-tuple-element.53), channel_id=1, source_target_pairs={{0,8},{4,12},{8,0},{12,4},{16,24},{20,28},{24,16},{28,20},{1,9},{5... | collective-permute-start | bytes 786440 | tf_op jit(solution)/shard_map/ppermute | solution.py:362
  22.4 19.3 %collective-permute-start.9 = (bf16[512,256]{1,0:T(8,128)(2,1)S(1)}, bf16[512,256]{1,0:T(8,128)(2,1)S(1)}, u32[]{:S(2)}, u32[]{:S(2)}) collective-permute-start(bf16[512,256]{1,0:T(8,128)(2,1)S(1)} %get-tuple-element.54), channel_id=1, source_target_pairs={{0,24},{4,28},{8,16},{12,20},{16,8},{20,12},{24,0},{28,4},{1,25},{... | collective-permute-start | bytes 786440 | tf_op jit(solution)/shard_map/ppermute | solution.py:362
  31.5 1.3 %collective-permute-start.4 = (bf16[128,512]{1,0:T(8,128)(2,1)S(1)}, bf16[128,512]{1,0:T(8,128)(2,1)S(1)}, u32[]{:S(2)}, u32[]{:S(2)}) collective-permute-start(bf16[128,512]{1,0:T(8,128)(2,1)S(1)} %get-tuple-element.46.ahead_ref), channel_id=1, source_target_pairs={{0,4},{4,0},{8,12},{12,8},{16,20},{20,16},{24,28},{28,24},{1,5},{5... | collective-permute-start | bytes 393224 | tf_op jit(solution)/shard_map/ppermute | solution.py:371
  34.0 4.6 %collective-permute-start.5 = (f32[8,256]{1,0:T(8,128)S(1)}, f32[8,256]{1,0:T(8,128)S(1)}, u32[]{:S(2)}, u32[]{:S(2)}) collective-permute-start(f32[8,256]{1,0:T(8,128)S(1)} %get-tuple-element.49.rest_0_), channel_id=1, source_target_pairs={{0,1},{1,2},{2,3},{3,0},{4,5},{5,6},{6,7},{7,4},{8,9},{9,10},{10,1... | collective-permute-start | bytes 24584 | tf_op jit(solution)/shard_map/ppermute | solution.py:449
  35.5 3.7 %collective-permute-start.6 = (f32[8,256]{1,0:T(8,128)S(1)}, f32[8,256]{1,0:T(8,128)S(1)}, u32[]{:S(2)}, u32[]{:S(2)}) collective-permute-start(f32[8,256]{1,0:T(8,128)S(1)} %get-tuple-element.49.rest_0_), channel_id=1, source_target_pairs={{0,2},{1,3},{2,0},{3,1},{4,6},{5,7},{6,4},{7,5},{8,10},{9,11},{10,... | collective-permute-start | bytes 24584 | tf_op jit(solution)/shard_map/ppermute | solution.py:449
  37.0 3.7 %collective-permute-start.7 = (f32[8,256]{1,0:T(8,128)S(1)}, f32[8,256]{1,0:T(8,128)S(1)}, u32[]{:S(2)}, u32[]{:S(2)}) collective-permute-start(f32[8,256]{1,0:T(8,128)S(1)} %get-tuple-element.49.rest_0_), channel_id=1, source_target_pairs={{0,3},{1,0},{2,1},{3,2},{4,7},{5,4},{6,5},{7,6},{8,11},{9,8},{10,9... | collective-permute-start | bytes 24584 | tf_op jit(solution)/shard_map/ppermute | solution.py:449
  41.7 4.5 %collective-permute-start.10 = (bf16[1024,256]{1,0:T(8,128)(2,1)S(1)}, bf16[1024,256]{1,0:T(8,128)(2,1)S(1)}, u32[]{:S(2)}, u32[]{:S(2)}) collective-permute-start(bf16[1024,256]{1,0:T(8,128)(2,1)S(1)} %shard_map.120.own_ref), channel_id=1, source_target_pairs={{0,4},{4,0},{8,12},{12,8},{16,20},{20,16},{24,28},{28,24},{1,5},{5... | collective-permute-start | bytes 1572872 | tf_op jit(solution)/shard_map/ppermute | solution.py:371
  41.8 8.3 %collective-permute-start.13 = (bf16[256,256]{1,0:T(8,128)(2,1)S(1)}, bf16[256,256]{1,0:T(8,128)(2,1)S(1)}, u32[]{:S(2)}, u32[]{:S(2)}) collective-permute-start(bf16[256,256]{1,0:T(8,128)(2,1)S(1)} %get-tuple-element.57), channel_id=1, source_target_pairs={{0,24},{4,28},{8,16},{12,20},{16,8},{20,12},{24,0},{28,4},{1,25},{... | collective-permute-start | bytes 393224 | tf_op jit(solution)/shard_map/ppermute | solution.py:362
  42.0 13.2 %collective-permute-start.12 = (bf16[256,256]{1,0:T(8,128)(2,1)S(1)}, bf16[256,256]{1,0:T(8,128)(2,1)S(1)}, u32[]{:S(2)}, u32[]{:S(2)}) collective-permute-start(bf16[256,256]{1,0:T(8,128)(2,1)S(1)} %get-tuple-element.56), channel_id=1, source_target_pairs={{0,16},{4,20},{8,24},{12,28},{16,0},{20,4},{24,8},{28,12},{1,17},{... | collective-permute-start | bytes 393224 | tf_op jit(solution)/shard_map/ppermute | solution.py:362
  42.9 12.4 %collective-permute-start.11 = (bf16[256,256]{1,0:T(8,128)(2,1)S(1)}, bf16[256,256]{1,0:T(8,128)(2,1)S(1)}, u32[]{:S(2)}, u32[]{:S(2)}) collective-permute-start(bf16[256,256]{1,0:T(8,128)(2,1)S(1)} %get-tuple-element.55), channel_id=1, source_target_pairs={{0,8},{4,12},{8,0},{12,4},{16,24},{20,28},{24,16},{28,20},{1,9},{5... | collective-permute-start | bytes 393224 | tf_op jit(solution)/shard_map/ppermute | solution.py:362
  46.3 10.5 %collective-permute-start.14 = (bf16[256,256]{1,0:T(8,128)(2,1)S(1)}, bf16[256,256]{1,0:T(8,128)(2,1)S(1)}, u32[]{:S(2)}, u32[]{:S(2)}) collective-permute-start(bf16[256,256]{1,0:T(8,128)(2,1)S(1)} %get-tuple-element.51.after_ref.rest_0_), channel_id=1, source_target_pairs={{0,4},{4,0},{8,12},{12,8},{16,20},{20,16},{24,28},{28,24},{1,5},{5... | collective-permute-start | bytes 393224 | tf_op jit(solution)/shard_map/ppermute | solution.py:371
  50.1 6.6 %collective-permute-start.17 = (bf16[256,256]{1,0:T(8,128)(2,1)S(1)}, bf16[256,256]{1,0:T(8,128)(2,1)S(1)}, u32[]{:S(2)}, u32[]{:S(2)}) collective-permute-start(bf16[256,256]{1,0:T(8,128)(2,1)S(1)} %shard_map.125), channel_id=1, source_target_pairs={{0,4},{4,0},{8,12},{12,8},{16,20},{20,16},{24,28},{28,24},{1,5},{5... | collective-permute-start | bytes 393224 | tf_op jit(solution)/shard_map/ppermute | solution.py:371
  55.2 1.6 %collective-permute-start.16 = (bf16[256,256]{1,0:T(8,128)(2,1)S(1)}, bf16[256,256]{1,0:T(8,128)(2,1)S(1)}, u32[]{:S(2)}, u32[]{:S(2)}) collective-permute-start(bf16[256,256]{1,0:T(8,128)(2,1)S(1)} %shard_map.124), channel_id=1, source_target_pairs={{0,4},{4,0},{8,12},{12,8},{16,20},{20,16},{24,28},{28,24},{1,5},{5... | collective-permute-start | bytes 393224 | tf_op jit(solution)/shard_map/ppermute | solution.py:371
  55.3 1.5 %collective-permute-start.15 = (bf16[256,256]{1,0:T(8,128)(2,1)S(1)}, bf16[256,256]{1,0:T(8,128)(2,1)S(1)}, u32[]{:S(2)}, u32[]{:S(2)}) collective-permute-start(bf16[256,256]{1,0:T(8,128)(2,1)S(1)} %shard_map.123), channel_id=1, source_target_pairs={{0,4},{4,0},{8,12},{12,8},{16,20},{20,16},{24,28},{28,24},{1,5},{5... | collective-permute-start | bytes 393224 | tf_op jit(solution)/shard_map/ppermute | solution.py:371
  57.8 8.3 %collective-permute-start.18 = (bf16[256,256]{1,0:T(8,128)(2,1)S(1)}, bf16[256,256]{1,0:T(8,128)(2,1)S(1)}, u32[]{:S(2)}, u32[]{:S(2)}) collective-permute-start(bf16[256,256]{1,0:T(8,128)(2,1)S(1)} %get-tuple-element.59), channel_id=1, source_target_pairs={{0,24},{4,28},{8,16},{12,20},{16,8},{20,12},{24,0},{28,4},{1,25},{... | collective-permute-start | bytes 393224 | tf_op jit(solution)/shard_map/ppermute | solution.py:362
  59.4 11.1 %collective-permute-start.19 = (bf16[256,256]{1,0:T(8,128)(2,1)S(1)}, bf16[256,256]{1,0:T(8,128)(2,1)S(1)}, u32[]{:S(2)}, u32[]{:S(2)}) collective-permute-start(bf16[256,256]{1,0:T(8,128)(2,1)S(1)} %get-tuple-element.60), channel_id=1, source_target_pairs={{0,8},{4,12},{8,0},{12,4},{16,24},{20,28},{24,16},{28,20},{1,9},{5... | collective-permute-start | bytes 393224 | tf_op jit(solution)/shard_map/ppermute | solution.py:362
  59.4 11.1 %collective-permute-start.20 = (bf16[256,256]{1,0:T(8,128)(2,1)S(1)}, bf16[256,256]{1,0:T(8,128)(2,1)S(1)}, u32[]{:S(2)}, u32[]{:S(2)}) collective-permute-start(bf16[256,256]{1,0:T(8,128)(2,1)S(1)} %get-tuple-element.61), channel_id=1, source_target_pairs={{0,16},{4,20},{8,24},{12,28},{16,0},{20,4},{24,8},{28,12},{1,17},{... | collective-permute-start | bytes 393224 | tf_op jit(solution)/shard_map/ppermute | solution.py:362
